TPU v7x, 256 devices: a whole 4x4x8 slice. The times are simulated.
256 devices in a mesh: gx: 16 (over y_hi, z), gy: 16 (over x, y_lo, core).
Axes of the slice: x: 4, y: 4 (y_hi: 2, y_lo: 2; y = y_hi * 2 + y_lo), z: 8, core: 2. Of those that a mesh axis runs over, the one named last changes fastest.
Arguments:
- low_res: bfloat16 [256, 256, 6, 128], P('gx', 'gy'), may hold values from -6 to 6
- kernel: bfloat16 [4, 4, 4, 64, 128], replicated, may hold values from -0.1875 to 0.1875
- bias: float32 [64], replicated, may hold values from -3 to 3
- cotangent: bfloat16 [512, 512, 6, 128], P('gx', 'gy'), may hold values from -6 to 6
Outputs:
- output: bfloat16 [512, 512, 6, 128], P('gx', 'gy')
- input_grad: bfloat16 [256, 256, 6, 128], P('gx', 'gy')
- kernel_grad: float32 [4, 4, 4, 64, 128], replicated
- bias_grad: float32 [64], replicated
All inputs are finite; a program needn't handle non-finite values.
Results may differ from a plain program's by a relative error of at most 0.0085.
Values may be sent and summed in bfloat16 or wider, within the bound.
No kernel may reach another device: no remote copies, remote signals or barrier semaphores. Data moves between devices by JAX's collectives and lax.ppermute only.
A program may use at most 64 MiB of HBM per device.

v0:
```python
import jax
import jax.numpy as jnp
from jax import lax
from jax.experimental import pallas as pl
from jax.experimental.pallas import tpu as pltpu
from jax.sharding import PartitionSpec as P

SLOPE = 0.2
F32 = jnp.float32
BF16 = jnp.bfloat16

TAP_X = ((2, 0), (3, 1))
TAP_Y = ((1, 3), (2, 0))
SHIFT_Y = ((1, 0), (1, 2))
TAP_Z = ((3, 1, None), (None, 2, 0))


def dot_nt(a, b):
    return lax.dot_general(a, b, (((1,), (1,)), ((), ())), preferred_element_type=F32)


def forward_body(low, ylo, yhi, xlo, xhi, kern, bias, cot, out, dpre, kgrad, bgrad, xf, xs, im, wt, c32, o32, dd, ddt):
    nx, nz, ny, ch = low.shape
    half = ch // 2
    rows = (nx + 1) * ny
    total = rows * nz

    for z in range(nz):
        xf[z, pl.ds(1, nx), 8:8 + ny, :] = low[:, z].astype(F32)
        xf[z, 0, 7:9 + ny, :] = xlo[z].astype(F32)
        xf[z, nx + 1, 7:9 + ny, :] = xhi[z].astype(F32)
    for x in range(nx):
        xf[:, 1 + x, 7, :] = ylo[x].astype(F32)
        xf[:, 1 + x, 8 + ny, :] = yhi[x].astype(F32)
    xs[:, 0] = jnp.zeros(xs.shape[:1] + xs.shape[2:], BF16)
    xs[:, nz + 1] = jnp.zeros(xs.shape[:1] + xs.shape[2:], BF16)

    def shift_step(z, carry):
        for s in range(3):
            xs[s, 1 + z] = xf[z, :, 7 + s:7 + s + ny, :].astype(BF16)
        return carry

    lax.fori_loop(0, nz, shift_step, 0)

    for py in range(2):
        for px in range(2):
            for c in range(2):
                row = px * ch + c * half
                for ux in range(2):
                    for vy in range(2):
                        for dz in range(3):
                            col = ((ux * 2 + vy) * 3 + dz) * ch
                            tz = TAP_Z[c][dz]
                            block = jnp.zeros((half, ch), BF16) if tz is None else kern[TAP_X[px][ux], TAP_Y[py][vy], tz]
                            wt[py, row:row + half, col:col + ch] = block

    pad = im.shape[1] - total
    im[:, total:, :] = jnp.zeros((2, pad, im.shape[2]), BF16)
    dd[:, total:, :] = jnp.zeros((2, pad, dd.shape[2]), BF16)
    bias_row = bias[...]

    def layer_step(z, acc):
        base = pl.multiple_of(z * rows, ny)
        c32[...] = cot[:, :, z].astype(F32)
        for py in range(2):
            for ux in range(2):
                for vy in range(2):
                    for dz in range(3):
                        col = ((ux * 2 + vy) * 3 + dz) * ch
                        im[py, pl.ds(base, rows), col:col + ch] = xs[SHIFT_Y[py][vy], z + dz, ux:ux + nx + 1].reshape(rows, ch)
            pre = dot_nt(im[py, pl.ds(base, rows), :], wt[py])
            dd[py, pl.ds(base, ny), 0:ch] = jnp.zeros((ny, ch), BF16)
            dd[py, pl.ds(base + nx * ny, ny), ch:2 * ch] = jnp.zeros((ny, ch), BF16)
            for q in range(2):
                part = pre[0:nx * ny, ch:2 * ch] if q == 0 else pre[ny:, 0:ch]
                part = part + bias_row
                up = part > 0
                cots = c32[:, q, pl.ds(py, ny, stride=2), :].reshape(nx * ny, ch)
                grad = (cots * jnp.where(up, 1.0, SLOPE)).astype(BF16)
                o32[:, q, pl.ds(py, ny, stride=2), :] = jnp.where(up, part, SLOPE * part).reshape(nx, ny, ch)
                if q == 0:
                    dd[py, pl.ds(base, nx * ny), ch:2 * ch] = grad
                else:
                    dd[py, pl.ds(base + ny, nx * ny), 0:ch] = grad
                dpre[py, :, q, z] = grad.reshape(nx, ny, ch)
                acc = acc + jnp.sum(grad.astype(F32).reshape(nx * ny // 8, 8, ch), axis=0)
        out[:, :, z] = o32[...].astype(BF16)
        return acc

    bgrad[...] = lax.fori_loop(0, nz, layer_step, jnp.zeros((8, ch), F32))

    for py in range(2):
        ddt[py] = dd[py].T
    for py in range(2):
        for block in range(im.shape[2] // (2 * ch)):
            terms = jnp.dot(ddt[py], im[py, :, block * 2 * ch:(block + 1) * 2 * ch], preferred_element_type=F32)
            for side in range(2):
                which = block * 2 + side
                ux, vy, dz = which // 6, which // 3 % 2, which % 3
                for px in range(2):
                    for c in range(2):
                        tz = TAP_Z[c][dz]
                        if tz is not None:
                            tap = (TAP_X[px][ux] * 4 + TAP_Y[py][vy]) * 4 + tz
                            row = px * ch + c * half
                            kgrad[tap] = terms[row:row + half, side * ch:(side + 1) * ch]


def run_forward(low, ylo, yhi, xlo, xhi, kern, bias_row, cot):
    nx, nz, ny, ch = low.shape
    rows = (nx + 1) * ny
    padded = -(-rows * nz // 128) * 128
    pairs = cot.reshape(nx, 2, nz, 2 * ny, ch)
    vmem = pl.BlockSpec(memory_space=pltpu.VMEM)
    out, dpre, kgrad, bgrad = pl.pallas_call(
        forward_body,
        out_shape=(
            jax.ShapeDtypeStruct((nx, 2, nz, 2 * ny, ch), BF16),
            jax.ShapeDtypeStruct((2, nx, 2, nz, ny, ch), BF16),
            jax.ShapeDtypeStruct((64, ch // 2, ch), F32),
            jax.ShapeDtypeStruct((8, ch), F32),
        ),
        in_specs=[vmem] * 8,
        out_specs=(vmem,) * 4,
        scratch_shapes=[
            pltpu.VMEM((nz, nx + 2, ny + 16, ch), F32),
            pltpu.VMEM((3, nz + 2, nx + 2, ny, ch), BF16),
            pltpu.VMEM((2, padded, 12 * ch), BF16),
            pltpu.VMEM((2, 2 * ch, 12 * ch), BF16),
            pltpu.VMEM((nx, 2, 2 * ny, ch), F32),
            pltpu.VMEM((nx, 2, 2 * ny, ch), F32),
            pltpu.VMEM((2, padded, 2 * ch), BF16),
            pltpu.VMEM((2, 2 * ch, padded), BF16),
        ],
        compiler_params=pltpu.CompilerParams(vmem_limit_bytes=56 << 20),
        cost_estimate=pl.CostEstimate(flops=12 * 2**30, bytes_accessed=8 << 20, transcendentals=0),
        name="forward",
    )(low, ylo, yhi, xlo, xhi, kern, bias_row, pairs)
    return out.reshape(2 * nx, nz, 2 * ny, ch), dpre.reshape(2, 2 * nx, nz, ny, ch), kgrad, bgrad


def backward_body(dpre, ylo, yhi, xlo, xhi, kern, grad, df, ds, wb):
    _, nx2, nz, ny, ch = dpre.shape
    nx = nx2 // 2
    half = ch // 2
    zero = jnp.zeros((nx + 1, 2, ny, ch), BF16)
    for var in range(4):
        ds[var, 0] = zero
        ds[var, nz + 1] = zero

    def layer_load(z, carry):
        for py in range(2):
            df[py, pl.ds(1, nx2), 8:8 + ny, :] = dpre[py, :, z].astype(F32)
            lead = 8 - py
            df[py, 0, lead:lead + ny + 1, :] = xlo[py, z].astype(F32)
            df[py, nx2 + 1, lead:lead + ny + 1, :] = xhi[py, z].astype(F32)
        df[0, pl.ds(1, nx2), 8 + ny:9 + ny, :] = yhi[z].astype(F32)
        df[1, pl.ds(1, nx2), 7:8, :] = ylo[z].astype(F32)
        for py in range(2):
            for vy in range(2):
                lead = 8 if vy == 0 else (9 if py == 0 else 7)
                ds[py * 2 + vy, 1 + z] = df[py, :, lead:lead + ny, :].astype(BF16).reshape(nx + 1, 2, ny, ch)
        return carry

    lax.fori_loop(0, nz, layer_load, 0)
    for py in range(2):
        for vy in range(2):
            for q in range(4):
                row = ((py * 2 + vy) * 4 + q) * 2 * ch
                ty = TAP_Y[py][vy]
                for place, tz in enumerate((1, 2, 3, 0)):
                    at = row + place * half
                    wb[at:at + half, :] = kern[q, ty, tz]
    lane = lax.broadcasted_iota(jnp.int32, (nx, ny, ch), 2)

    def layer_step(z, carry):
        acc = jnp.zeros((nx * ny, ch), F32)
        for var in range(4):
            pieces = []
            for q in range(4):
                same = ds[var, 1 + z, q // 2:q // 2 + nx, q % 2]
                above = ds[var, 2 + z, q // 2:q // 2 + nx, q % 2]
                below = ds[var, z, q // 2:q // 2 + nx, q % 2]
                mixed = jnp.where(lane < half, above.astype(F32), below.astype(F32)).astype(BF16)
                pieces += [same.reshape(nx * ny, ch), mixed.reshape(nx * ny, ch)]
            acc = acc + jnp.dot(jnp.concatenate(pieces, axis=1), wb[var * 8 * ch:(var + 1) * 8 * ch, :], preferred_element_type=F32)
        grad[:, z] = acc.astype(BF16).reshape(nx, ny, ch)
        return carry

    lax.fori_loop(0, nz, layer_step, 0)


def run_backward(dpre, ylo, yhi, xlo, xhi, kern):
    _, nx2, nz, ny, ch = dpre.shape
    vmem = pl.BlockSpec(memory_space=pltpu.VMEM)
    return pl.pallas_call(
        backward_body,
        out_shape=jax.ShapeDtypeStruct((nx2 // 2, nz, ny, ch), BF16),
        in_specs=[vmem] * 6,
        out_specs=vmem,
        scratch_shapes=[
            pltpu.VMEM((2, nx2 + 2, ny + 16, ch), F32),
            pltpu.VMEM((4, nz + 2, nx2 // 2 + 1, 2, ny, ch), BF16),
            pltpu.VMEM((32 * ch, ch), BF16),
        ],
        compiler_params=pltpu.CompilerParams(vmem_limit_bytes=40 << 20),
        cost_estimate=pl.CostEstimate(flops=4 * 2**30, bytes_accessed=4 << 20, transcendentals=0),
        name="backward",
    )(dpre, ylo, yhi, xlo, xhi, kern)


def from_lower(values, axis):
    count = lax.axis_size(axis)
    return lax.ppermute(values, axis, [(i, i + 1) for i in range(count - 1)])


def from_upper(values, axis):
    count = lax.axis_size(axis)
    return lax.ppermute(values, axis, [(i + 1, i) for i in range(count - 1)])


def exchanges():
    across, along = lax.axis_size("gx"), lax.axis_size("gy")
    steps = []
    bit = 1
    while bit < along:
        steps.append(("gy", bit))
        bit *= 2
    bit = 1
    while bit < across:
        steps.append(("gx", bit))
        bit *= 2
    wanted = [("gy", 1), ("gy", 4), ("gy", 2), ("gx", 1), ("gy", 8), ("gx", 8), ("gx", 2), ("gx", 4)]
    return [step for step in wanted if step in steps]


def swap(values, axis, bit):
    return lax.ppermute(values, axis, [(i, i ^ bit) for i in range(lax.axis_size(axis))])


def sum_over_devices(kgrad, brow):
    steps = exchanges()
    part = kgrad.reshape(-1, kgrad.shape[-1])
    extra = brow.reshape(1, -1)
    for at, (axis, bit) in enumerate(steps):
        half = part.shape[0] // 2
        up = (lax.axis_index(axis) & bit) != 0
        keep = jnp.where(up, part[half:], part[:half])
        give = jnp.where(up, part[:half], part[half:])
        if at < 3:
            high = extra.astype(BF16)
            low = (extra - high.astype(F32)).astype(BF16)
            tail = jnp.concatenate([jnp.broadcast_to(high, (8,) + high.shape[1:]), jnp.broadcast_to(low, (8,) + low.shape[1:])], axis=0)
            came = swap(jnp.concatenate([give.astype(BF16), tail], axis=0), axis, bit).astype(F32)
            extra = high.astype(F32) + low.astype(F32) + (came[half:half + 1] + came[half + 8:half + 9])
        else:
            tail = jnp.broadcast_to(extra, (8,) + extra.shape[1:])
            came = swap(jnp.concatenate([give, tail], axis=0), axis, bit)
            extra = extra + came[half:half + 1]
        part = keep + came[:half]
    grown = part.astype(BF16)
    for axis, bit in steps[::-1]:
        up = (lax.axis_index(axis) & bit) != 0
        came = swap(grown, axis, bit)
        grown = jnp.concatenate([jnp.where(up, came, grown), jnp.where(up, grown, came)], axis=0)
    return grown.astype(F32), extra


def per_device(low_res, kernel, bias, cotangent):
    low = jnp.transpose(low_res, (0, 2, 1, 3))
    cot = jnp.transpose(cotangent, (0, 2, 1, 3))
    nx, nz, ny, ch = low.shape
    bias_row = jnp.concatenate([bias, bias]).reshape(1, ch)
    ylo = from_lower(low[:, :, ny - 1], "gy")
    yhi = from_upper(low[:, :, 0], "gy")

    def with_corners(x):
        return jnp.concatenate([ylo[x][:, None], low[x], yhi[x][:, None]], axis=1)

    xlo = from_lower(with_corners(nx - 1), "gx")
    xhi = from_upper(with_corners(0), "gx")
    out, dpre, kgrad, bgrad = run_forward(low, ylo, yhi, xlo, xhi, kernel, bias_row, cot)
    kernel_sum, bias_sum = sum_over_devices(kgrad, jnp.sum(bgrad, axis=0))

    gyhi = from_upper(dpre[0, :, :, 0], "gy")
    gylo = from_lower(dpre[1, :, :, ny - 1], "gy")

    def grad_corners(x):
        even = jnp.concatenate([dpre[0, x], gyhi[x][:, None]], axis=1)
        odd = jnp.concatenate([gylo[x][:, None], dpre[1, x]], axis=1)
        return jnp.stack([even, odd])

    gxlo = from_lower(grad_corners(2 * nx - 1), "gx")
    gxhi = from_upper(grad_corners(0), "gx")
    tall = lambda a: jnp.transpose(a, (1, 0, 2))[:, :, None, :]
    grad = run_backward(dpre, tall(gylo), tall(gyhi), gxlo, gxhi, kernel)

    grid_rows = lax.axis_size("gx") * nx
    output = jnp.transpose(out, (0, 2, 1, 3))
    input_grad = jnp.transpose(grad, (0, 2, 1, 3))
    kernel_grad = kernel_sum.reshape(kernel.shape) / grid_rows
    bias_grad = jnp.sum(bias_sum.reshape(2, ch // 2), axis=0) / grid_rows
    return (output, input_grad, kernel_grad, bias_grad)


def solution(mesh):
    return jax.shard_map(
        per_device,
        mesh=mesh,
        in_specs=(P("gx", "gy", None, None), P(), P(), P("gx", "gy", None, None)),
        out_specs=(P("gx", "gy", None, None), P("gx", "gy", None, None), P(), P()),
        check_vma=False,
    )
```

profile of v0, /device:TPU:224, one launch (start us, length us, event | category | flops | bytes accessed | tf_op | source)
XLA Modules:
  0.0 145.7 jit_solution(15085844514297424848)
XLA Ops:
  1.8 1.7 %collective-permute-start = (bf16[16,6,128]{2,1,0:T(8,128)(2,1)S(1)}, bf16[16,6,128]{2,1,0:T(8,128)(2,1)S(1)}, u32[]{:S(2)}, u32[]{:S(2)}) collective-permute-start(bf16[16,6,128]{2,1,0:T(8,128)(2,1)S(1)} %bitcast.115), channel_id=1, source_target_pairs={{0,1},{1,2},{2,3},{3,4},{4,5},{5,6},{6,7},{7,8},{8,9},{9,10},{10,1... | collective-permute-start | bytes 73736 | tf_op jit(solution)/shard_map/ppermute | solution.py:214
  5.6 2.4 %collective-permute-done.1.yhi = bf16[16,6,128]{2,1,0:T(8,128)(2,1)S(1)} collective-permute-done((bf16[16,6,128]{2,1,0:T(8,128)(2,1)S(1)}, bf16[16,6,128]{2,1,0:T(8,128)(2,1)S(1)}, u32[]{:S(2)}, u32[]{:S(2)}) %collective-permute-start.1) | collective-permute-done | bytes 24608 | tf_op jit(solution)/shard_map/ppermute | solution.py:219
  8.0 2.9 %collective-permute-start.3 = (bf16[6,18,128]{2,1,0:T(8,128)(2,1)S(1)}, bf16[6,18,128]{2,1,0:T(8,128)(2,1)S(1)}, u32[]{:S(2)}, u32[]{:S(2)}) collective-permute-start(bf16[6,18,128]{2,1,0:T(8,128)(2,1)S(1)} %pad_maximum_fusion.12), channel_id=1, source_target_pairs={{16,0},{32,16},{48,32},{64,48},{80,64},{96,80},{112,96},{128,112},... | collective-permute-start | bytes 82952 | tf_op jit(solution)/shard_map/ppermute | solution.py:219
  11.0 6.5 %collective-permute-start.2 = (bf16[6,18,128]{2,1,0:T(8,128)(2,1)S(1)}, bf16[6,18,128]{2,1,0:T(8,128)(2,1)S(1)}, u32[]{:S(2)}, u32[]{:S(2)}) collective-permute-start(bf16[6,18,128]{2,1,0:T(8,128)(2,1)S(1)} %pad_maximum_fusion.11), channel_id=1, source_target_pairs={{0,16},{16,32},{32,48},{48,64},{64,80},{80,96},{96,112},{112,128},... | collective-permute-start | bytes 82952 | tf_op jit(solution)/shard_map/ppermute | solution.py:214
  19.8 12.0 %forward.1 = (bf16[16,2,6,32,128]{4,3,2,1,0:T(8,128)(2,1)}, bf16[2,16,2,6,16,128]{5,4,3,2,1,0:T(8,128)(2,1)}, f32[64,64,128]{2,1,0:T(8,128)}, f32[8,128]{1,0:T(8,128)}) custom-call(bf16[16,6,16,128]{3,2,1,0:T(8,128)(2,1)} %bitcast.111, bf16[16,6,128]{2,1,0:T(8,128)(2,1)} %copy-done.3, bf16[16,6,128]{2,1,0:T(8,128)(2,1)} %copy-done.4, ...), custom_call_target="tpu_custom_call" | custom-call | flops 12884901888 | bytes 8388608 | tf_op jit(solution)/shard_map/forward/pallas_call | solution.py:115
  32.6 1.6 %select_convert_fusion = bf16[32,64,128]{2,1,0:T(8,128)(2,1)S(1)} fusion(f32[64,64,128]{2,1,0:T(8,128)} %get-tuple-element.10, pred[]{:T(512)S(6)} %ne.32), kind=kLoop, calls=%fused_computation.2 | loop fusion | flops 262144 | bytes 1572865 | tf_op jit(solution)/shard_map/convert_element_type | solution.py:254
  34.3 1.9 %collective-permute-start.8 = (bf16[2064,128]{1,0:T(8,128)(2,1)S(1)}, bf16[2064,128]{1,0:T(8,128)(2,1)S(1)}, u32[]{:S(2)}, u32[]{:S(2)}) collective-permute-start(bf16[2064,128]{1,0:T(8,128)(2,1)S(1)} %pad_maximum_fusion), channel_id=1, source_target_pairs={{0,1},{1,0},{2,3},{3,2},{4,5},{5,4},{6,7},{7,6},{8,9},{9,8},{10,11... | collective-permute-start | bytes 1585160 | tf_op jit(solution)/shard_map/ppermute | solution.py:238
  38.1 2.0 %collective-permute-start.9 = (bf16[1040,128]{1,0:T(8,128)(2,1)S(1)}, bf16[1040,128]{1,0:T(8,128)(2,1)S(1)}, u32[]{:S(2)}, u32[]{:S(2)}) collective-permute-start(bf16[1040,128]{1,0:T(8,128)(2,1)S(1)} %pad_maximum_fusion.2), channel_id=1, source_target_pairs={{0,4},{1,5},{2,6},{3,7},{4,0},{5,1},{6,2},{7,3},{8,12},{9,13},{10,... | collective-permute-start | bytes 798728 | tf_op jit(solution)/shard_map/ppermute | solution.py:238
  40.1 6.8 %collective-permute-done.9 = bf16[1040,128]{1,0:T(8,128)(2,1)S(1)} collective-permute-done((bf16[1040,128]{1,0:T(8,128)(2,1)S(1)}, bf16[1040,128]{1,0:T(8,128)(2,1)S(1)}, u32[]{:S(2)}, u32[]{:S(2)}) %collective-permute-start.9) | collective-permute-done | bytes 266272 | tf_op jit(solution)/shard_map/ppermute | solution.py:238
  47.1 2.4 %collective-permute-start.10 = (bf16[528,128]{1,0:T(8,128)(2,1)S(1)}, bf16[528,128]{1,0:T(8,128)(2,1)S(1)}, u32[]{:S(2)}, u32[]{:S(2)}) collective-permute-start(bf16[528,128]{1,0:T(8,128)(2,1)S(1)} %pad_maximum_fusion.4), channel_id=1, source_target_pairs={{0,2},{1,3},{2,0},{3,1},{4,6},{5,7},{6,4},{7,5},{8,10},{9,11},{10,... | collective-permute-start | bytes 405512 | tf_op jit(solution)/shard_map/ppermute | solution.py:238
  49.4 3.3 %collective-permute-done.10 = bf16[528,128]{1,0:T(8,128)(2,1)S(1)} collective-permute-done((bf16[528,128]{1,0:T(8,128)(2,1)S(1)}, bf16[528,128]{1,0:T(8,128)(2,1)S(1)}, u32[]{:S(2)}, u32[]{:S(2)}) %collective-permute-start.10) | collective-permute-done | bytes 135200 | tf_op jit(solution)/shard_map/ppermute | solution.py:238
  52.9 5.0 %collective-permute-done.11 = f32[264,128]{1,0:T(8,128)S(1)} collective-permute-done((f32[264,128]{1,0:T(8,128)S(1)}, f32[264,128]{1,0:T(8,128)S(1)}, u32[]{:S(2)}, u32[]{:S(2)}) %collective-permute-start.11) | collective-permute-done | bytes 135200 | tf_op jit(solution)/shard_map/ppermute | solution.py:238
  58.0 2.8 %collective-permute-start.12 = (f32[136,128]{1,0:T(8,128)S(1)}, f32[136,128]{1,0:T(8,128)S(1)}, u32[]{:S(2)}, u32[]{:S(2)}) collective-permute-start(f32[136,128]{1,0:T(8,128)S(1)} %pad_maximum_fusion.9), channel_id=1, source_target_pairs={{0,8},{1,9},{2,10},{3,11},{4,12},{5,13},{6,14},{7,15},{8,0},{9,1},... | collective-permute-start | bytes 208904 | tf_op jit(solution)/shard_map/ppermute | solution.py:238
  60.8 3.1 %collective-permute-done.12 = f32[136,128]{1,0:T(8,128)S(1)} collective-permute-done((f32[136,128]{1,0:T(8,128)S(1)}, f32[136,128]{1,0:T(8,128)S(1)}, u32[]{:S(2)}, u32[]{:S(2)}) %collective-permute-start.12) | collective-permute-done | bytes 69664 | tf_op jit(solution)/shard_map/ppermute | solution.py:238
  64.4 5.1 %collective-permute-done.13 = f32[72,128]{1,0:T(8,128)S(1)} collective-permute-done((f32[72,128]{1,0:T(8,128)S(1)}, f32[72,128]{1,0:T(8,128)S(1)}, u32[]{:S(2)}, u32[]{:S(2)}) %collective-permute-start.13) | collective-permute-done | bytes 36896 | tf_op jit(solution)/shard_map/ppermute | solution.py:238
  69.7 4.7 %collective-permute-done.14 = f32[40,128]{1,0:T(8,128)S(1)} collective-permute-done((f32[40,128]{1,0:T(8,128)S(1)}, f32[40,128]{1,0:T(8,128)S(1)}, u32[]{:S(2)}, u32[]{:S(2)}) %collective-permute-start.14) | collective-permute-done | bytes 20512 | tf_op jit(solution)/shard_map/ppermute | solution.py:238
  74.4 2.0 %collective-permute-start.15 = (f32[24,128]{1,0:T(8,128)S(1)}, f32[24,128]{1,0:T(8,128)S(1)}, u32[]{:S(2)}, u32[]{:S(2)}) collective-permute-start(f32[24,128]{1,0:T(8,128)S(1)} %pad_maximum_fusion.17), channel_id=1, source_target_pairs={{0,64},{16,80},{32,96},{48,112},{64,0},{80,16},{96,32},{112,48},{1... | collective-permute-start | bytes 36872 | tf_op jit(solution)/shard_map/ppermute | solution.py:238
  76.4 5.7 %collective-permute-done.15 = f32[24,128]{1,0:T(8,128)S(1)} collective-permute-done((f32[24,128]{1,0:T(8,128)S(1)}, f32[24,128]{1,0:T(8,128)S(1)}, u32[]{:S(2)}, u32[]{:S(2)}) %collective-permute-start.15) | collective-permute-done | bytes 12320 | tf_op jit(solution)/shard_map/ppermute | solution.py:238
  82.1 1.9 %collective-permute-start.16 = (bf16[16,128]{1,0:T(8,128)(2,1)S(1)}, bf16[16,128]{1,0:T(8,128)(2,1)S(1)}, u32[]{:S(2)}, u32[]{:S(2)}) collective-permute-start(bf16[16,128]{1,0:T(8,128)(2,1)S(1)} %fusion), channel_id=1, source_target_pairs={{0,64},{16,80},{32,96},{48,112},{64,0},{80,16},{96,32},{112,48},{1... | collective-permute-start | bytes 12296 | tf_op jit(solution)/shard_map/ppermute | solution.py:238
  84.0 5.6 %collective-permute-done.16 = bf16[16,128]{1,0:T(8,128)(2,1)S(1)} collective-permute-done((bf16[16,128]{1,0:T(8,128)(2,1)S(1)}, bf16[16,128]{1,0:T(8,128)(2,1)S(1)}, u32[]{:S(2)}, u32[]{:S(2)}) %collective-permute-start.16) | collective-permute-done | bytes 4128 | tf_op jit(solution)/shard_map/ppermute | solution.py:238
  89.7 4.5 %collective-permute-done.17 = bf16[32,128]{1,0:T(8,128)(2,1)S(1)} collective-permute-done((bf16[32,128]{1,0:T(8,128)(2,1)S(1)}, bf16[32,128]{1,0:T(8,128)(2,1)S(1)}, u32[]{:S(2)}, u32[]{:S(2)}) %collective-permute-start.17) | collective-permute-done | bytes 8224 | tf_op jit(solution)/shard_map/ppermute | solution.py:238
  94.8 4.8 %collective-permute-done.18 = bf16[64,128]{1,0:T(8,128)(2,1)S(1)} collective-permute-done((bf16[64,128]{1,0:T(8,128)(2,1)S(1)}, bf16[64,128]{1,0:T(8,128)(2,1)S(1)}, u32[]{:S(2)}, u32[]{:S(2)}) %collective-permute-start.18) | collective-permute-done | bytes 16416 | tf_op jit(solution)/shard_map/ppermute | solution.py:238
  99.6 2.8 %collective-permute-start.19 = (bf16[128,128]{1,0:T(8,128)(2,1)S(1)}, bf16[128,128]{1,0:T(8,128)(2,1)S(1)}, u32[]{:S(2)}, u32[]{:S(2)}) collective-permute-start(bf16[128,128]{1,0:T(8,128)(2,1)S(1)} %pad_maximum_fusion.14), channel_id=1, source_target_pairs={{0,8},{1,9},{2,10},{3,11},{4,12},{5,13},{6,14},{7,15},{8,0},{9,1},... | collective-permute-start | bytes 98312 | tf_op jit(solution)/shard_map/ppermute | solution.py:238
  105.5 4.2 %collective-permute-done.20 = bf16[256,128]{1,0:T(8,128)(2,1)S(1)} collective-permute-done((bf16[256,128]{1,0:T(8,128)(2,1)S(1)}, bf16[256,128]{1,0:T(8,128)(2,1)S(1)}, u32[]{:S(2)}, u32[]{:S(2)}) %collective-permute-start.20) | collective-permute-done | bytes 65568 | tf_op jit(solution)/shard_map/ppermute | solution.py:238
  109.7 4.8 %collective-permute-start.21 = (bf16[512,128]{1,0:T(8,128)(2,1)S(1)}, bf16[512,128]{1,0:T(8,128)(2,1)S(1)}, u32[]{:S(2)}, u32[]{:S(2)}) collective-permute-start(bf16[512,128]{1,0:T(8,128)(2,1)S(1)} %pad_maximum_fusion.6), channel_id=1, source_target_pairs={{0,2},{1,3},{2,0},{3,1},{4,6},{5,7},{6,4},{7,5},{8,10},{9,11},{10,... | collective-permute-start | bytes 393224 | tf_op jit(solution)/shard_map/ppermute | solution.py:238
  114.6 2.9 %collective-permute-done.21 = bf16[512,128]{1,0:T(8,128)(2,1)S(1)} collective-permute-done((bf16[512,128]{1,0:T(8,128)(2,1)S(1)}, bf16[512,128]{1,0:T(8,128)(2,1)S(1)}, u32[]{:S(2)}, u32[]{:S(2)}) %collective-permute-start.21) | collective-permute-done | bytes 131104 | tf_op jit(solution)/shard_map/ppermute | solution.py:238
  117.6 1.9 %collective-permute-start.22 = (bf16[1024,128]{1,0:T(8,128)(2,1)S(1)}, bf16[1024,128]{1,0:T(8,128)(2,1)S(1)}, u32[]{:S(2)}, u32[]{:S(2)}) collective-permute-start(bf16[1024,128]{1,0:T(8,128)(2,1)S(1)} %pad_maximum_fusion.3), channel_id=1, source_target_pairs={{0,4},{1,5},{2,6},{3,7},{4,0},{5,1},{6,2},{7,3},{8,12},{9,13},{10,... | collective-permute-start | bytes 786440 | tf_op jit(solution)/shard_map/ppermute | solution.py:238
  119.5 7.9 %collective-permute-start.6 = (bf16[2,6,17,128]{3,2,1,0:T(8,128)(2,1)S(1)}, bf16[2,6,17,128]{3,2,1,0:T(8,128)(2,1)S(1)}, u32[]{:S(2)}, u32[]{:S(2)}) collective-permute-start(bf16[2,6,17,128]{3,2,1,0:T(8,128)(2,1)S(1)} %pad_maximum_fusion.7), channel_id=1, source_target_pairs={{0,16},{16,32},{32,48},{48,64},{64,80},{80,96},{96,112},{112,128},... | collective-permute-start | bytes 156680 | tf_op jit(solution)/shard_map/ppermute | solution.py:214
  127.5 1.9 %collective-permute-start.7 = (bf16[2,6,17,128]{3,2,1,0:T(8,128)(2,1)S(1)}, bf16[2,6,17,128]{3,2,1,0:T(8,128)(2,1)S(1)}, u32[]{:S(2)}, u32[]{:S(2)}) collective-permute-start(bf16[2,6,17,128]{3,2,1,0:T(8,128)(2,1)S(1)} %pad_maximum_fusion.8), channel_id=1, source_target_pairs={{16,0},{32,16},{48,32},{64,48},{80,64},{96,80},{112,96},{128,112},... | collective-permute-start | bytes 156680 | tf_op jit(solution)/shard_map/ppermute | solution.py:219
  129.9 7.5 %collective-permute-done.7.xhi = bf16[2,6,17,128]{3,2,1,0:T(8,128)(2,1)S(1)} collective-permute-done((bf16[2,6,17,128]{3,2,1,0:T(8,128)(2,1)S(1)}, bf16[2,6,17,128]{3,2,1,0:T(8,128)(2,1)S(1)}, u32[]{:S(2)}, u32[]{:S(2)}) %collective-permute-start.7) | collective-permute-done | bytes 52256 | tf_op jit(solution)/shard_map/ppermute | solution.py:219
  137.4 6.0 %backward.1 = bf16[16,6,16,128]{3,2,1,0:T(8,128)(2,1)} custom-call(bf16[2,32,6,16,128]{4,3,2,1,0:T(8,128)(2,1)S(1)} %bitcast.104, bf16[6,32,1,128]{3,2,1,0:T(2,128)(2,1)S(1)} %copy.67.ylo, bf16[6,32,1,128]{3,2,1,0:T(2,128)(2,1)S(1)} %copy.68.yhi, bf16[2,6,17,128]{3,2,1,0:T(8,128)(2,1)S(1)} %collective-permute-done.6.xlo, ...), custom_call_target="tpu_custom_call" | custom-call | flops 4294967296 | bytes 4194304 | tf_op jit(solution)/shard_map/backward/pallas_call | solution.py:196
  144.2 1.5 %convert_multiply_fusion = f32[4096,128]{1,0:T(8,128)} fusion(bf16[2048,128]{1,0:T(8,128)(2,1)S(1)} %get-tuple-element.23, bf16[2048,128]{1,0:T(8,128)(2,1)S(1)} %get-tuple-element.22), kind=kLoop, calls=%fused_computation | loop fusion | flops 2621440 | bytes 3145728 | tf_op jit(solution)/shard_map/div | solution.py:301
  (127 shorter events, 14.4 us)
Async XLA Ops:
  1.8 3.8 %collective-permute-start = (bf16[16,6,128]{2,1,0:T(8,128)(2,1)S(1)}, bf16[16,6,128]{2,1,0:T(8,128)(2,1)S(1)}, u32[]{:S(2)}, u32[]{:S(2)}) collective-permute-start(bf16[16,6,128]{2,1,0:T(8,128)(2,1)S(1)} %bitcast.115), channel_id=1, source_target_pairs={{0,1},{1,2},{2,3},{3,4},{4,5},{5,6},{6,7},{7,8},{8,9},{9,10},{10,1... | collective-permute-start | bytes 73736 | tf_op jit(solution)/shard_map/ppermute | solution.py:214
  3.5 4.5 %collective-permute-start.1 = (bf16[16,6,128]{2,1,0:T(8,128)(2,1)S(1)}, bf16[16,6,128]{2,1,0:T(8,128)(2,1)S(1)}, u32[]{:S(2)}, u32[]{:S(2)}) collective-permute-start(bf16[16,6,128]{2,1,0:T(8,128)(2,1)S(1)} %bitcast.114), channel_id=1, source_target_pairs={{1,0},{2,1},{3,2},{4,3},{5,4},{6,5},{7,6},{8,7},{9,8},{10,9},{11,1... | collective-permute-start | bytes 73736 | tf_op jit(solution)/shard_map/ppermute | solution.py:219
  5.6 13.6 %copy-start.3 = (bf16[16,6,128]{2,1,0:T(8,128)(2,1)}, bf16[16,6,128]{2,1,0:T(8,128)(2,1)S(1)}, u32[]{:S(2)}) copy-start(bf16[16,6,128]{2,1,0:T(8,128)(2,1)S(1)} %collective-permute-done.ylo) | copy-start | bytes 73732
  8.0 11.2 %copy-start.4 = (bf16[16,6,128]{2,1,0:T(8,128)(2,1)}, bf16[16,6,128]{2,1,0:T(8,128)(2,1)S(1)}, u32[]{:S(2)}) copy-start(bf16[16,6,128]{2,1,0:T(8,128)(2,1)S(1)} %collective-permute-done.1.yhi) | copy-start | bytes 73732
  8.0 10.8 %collective-permute-start.3 = (bf16[6,18,128]{2,1,0:T(8,128)(2,1)S(1)}, bf16[6,18,128]{2,1,0:T(8,128)(2,1)S(1)}, u32[]{:S(2)}, u32[]{:S(2)}) collective-permute-start(bf16[6,18,128]{2,1,0:T(8,128)(2,1)S(1)} %pad_maximum_fusion.12), channel_id=1, source_target_pairs={{16,0},{32,16},{48,32},{64,48},{80,64},{96,80},{112,96},{128,112},... | collective-permute-start | bytes 82952 | tf_op jit(solution)/shard_map/ppermute | solution.py:219
  11.0 8.2 %collective-permute-start.2 = (bf16[6,18,128]{2,1,0:T(8,128)(2,1)S(1)}, bf16[6,18,128]{2,1,0:T(8,128)(2,1)S(1)}, u32[]{:S(2)}, u32[]{:S(2)}) collective-permute-start(bf16[6,18,128]{2,1,0:T(8,128)(2,1)S(1)} %pad_maximum_fusion.11), channel_id=1, source_target_pairs={{0,16},{16,32},{32,48},{48,64},{64,80},{80,96},{96,112},{112,128},... | collective-permute-start | bytes 82952 | tf_op jit(solution)/shard_map/ppermute | solution.py:214
  18.9 0.6 copy-start.5
  19.2 0.6 copy-start.6
  31.8 4.4 %copy-start.2 = (f32[64,64,128]{2,1,0:T(8,128)S(1)}, f32[64,64,128]{2,1,0:T(8,128)}, u32[]{:S(2)}) copy-start(f32[64,64,128]{2,1,0:T(8,128)} %get-tuple-element.10) | copy-start | bytes 6291460
  34.3 3.4 %collective-permute-start.8 = (bf16[2064,128]{1,0:T(8,128)(2,1)S(1)}, bf16[2064,128]{1,0:T(8,128)(2,1)S(1)}, u32[]{:S(2)}, u32[]{:S(2)}) collective-permute-start(bf16[2064,128]{1,0:T(8,128)(2,1)S(1)} %pad_maximum_fusion), channel_id=1, source_target_pairs={{0,1},{1,0},{2,3},{3,2},{4,5},{5,4},{6,7},{7,6},{8,9},{9,8},{10,11... | collective-permute-start | bytes 1585160 | tf_op jit(solution)/shard_map/ppermute | solution.py:238
  38.1 8.8 %collective-permute-start.9 = (bf16[1040,128]{1,0:T(8,128)(2,1)S(1)}, bf16[1040,128]{1,0:T(8,128)(2,1)S(1)}, u32[]{:S(2)}, u32[]{:S(2)}) collective-permute-start(bf16[1040,128]{1,0:T(8,128)(2,1)S(1)} %pad_maximum_fusion.2), channel_id=1, source_target_pairs={{0,4},{1,5},{2,6},{3,7},{4,0},{5,1},{6,2},{7,3},{8,12},{9,13},{10,... | collective-permute-start | bytes 798728 | tf_op jit(solution)/shard_map/ppermute | solution.py:238
  47.1 5.6 %collective-permute-start.10 = (bf16[528,128]{1,0:T(8,128)(2,1)S(1)}, bf16[528,128]{1,0:T(8,128)(2,1)S(1)}, u32[]{:S(2)}, u32[]{:S(2)}) collective-permute-start(bf16[528,128]{1,0:T(8,128)(2,1)S(1)} %pad_maximum_fusion.4), channel_id=1, source_target_pairs={{0,2},{1,3},{2,0},{3,1},{4,6},{5,7},{6,4},{7,5},{8,10},{9,11},{10,... | collective-permute-start | bytes 405512 | tf_op jit(solution)/shard_map/ppermute | solution.py:238
  52.7 42.0 %copy-start = (bf16[2,16,2,6,16,128]{5,4,3,2,1,0:T(8,128)(2,1)S(1)}, bf16[2,16,2,6,16,128]{5,4,3,2,1,0:T(8,128)(2,1)}, u32[]{:S(2)}) copy-start(bf16[2,16,2,6,16,128]{5,4,3,2,1,0:T(8,128)(2,1)} %get-tuple-element.9) | copy-start | bytes 4718596
  52.8 5.1 %collective-permute-start.11 = (f32[264,128]{1,0:T(8,128)S(1)}, f32[264,128]{1,0:T(8,128)S(1)}, u32[]{:S(2)}, u32[]{:S(2)}) collective-permute-start(f32[264,128]{1,0:T(8,128)S(1)} %pad_maximum_fusion.5), channel_id=1, source_target_pairs={{0,16},{16,0},{32,48},{48,32},{64,80},{80,64},{96,112},{112,96},{1... | collective-permute-start | bytes 405512 | tf_op jit(solution)/shard_map/ppermute | solution.py:238
  58.0 5.9 %collective-permute-start.12 = (f32[136,128]{1,0:T(8,128)S(1)}, f32[136,128]{1,0:T(8,128)S(1)}, u32[]{:S(2)}, u32[]{:S(2)}) collective-permute-start(f32[136,128]{1,0:T(8,128)S(1)} %pad_maximum_fusion.9), channel_id=1, source_target_pairs={{0,8},{1,9},{2,10},{3,11},{4,12},{5,13},{6,14},{7,15},{8,0},{9,1},... | collective-permute-start | bytes 208904 | tf_op jit(solution)/shard_map/ppermute | solution.py:238
  64.0 5.5 %collective-permute-start.13 = (f32[72,128]{1,0:T(8,128)S(1)}, f32[72,128]{1,0:T(8,128)S(1)}, u32[]{:S(2)}, u32[]{:S(2)}) collective-permute-start(f32[72,128]{1,0:T(8,128)S(1)} %pad_maximum_fusion.13), channel_id=1, source_target_pairs={{0,128},{16,144},{32,160},{48,176},{64,192},{80,208},{96,224},{112... | collective-permute-start | bytes 110600 | tf_op jit(solution)/shard_map/ppermute | solution.py:238
  69.6 4.8 %collective-permute-start.14 = (f32[40,128]{1,0:T(8,128)S(1)}, f32[40,128]{1,0:T(8,128)S(1)}, u32[]{:S(2)}, u32[]{:S(2)}) collective-permute-start(f32[40,128]{1,0:T(8,128)S(1)} %pad_maximum_fusion.15), channel_id=1, source_target_pairs={{0,32},{16,48},{32,0},{48,16},{64,96},{80,112},{96,64},{112,80},{1... | collective-permute-start | bytes 61448 | tf_op jit(solution)/shard_map/ppermute | solution.py:238
  74.4 7.7 %collective-permute-start.15 = (f32[24,128]{1,0:T(8,128)S(1)}, f32[24,128]{1,0:T(8,128)S(1)}, u32[]{:S(2)}, u32[]{:S(2)}) collective-permute-start(f32[24,128]{1,0:T(8,128)S(1)} %pad_maximum_fusion.17), channel_id=1, source_target_pairs={{0,64},{16,80},{32,96},{48,112},{64,0},{80,16},{96,32},{112,48},{1... | collective-permute-start | bytes 36872 | tf_op jit(solution)/shard_map/ppermute | solution.py:238
  82.1 7.5 %collective-permute-start.16 = (bf16[16,128]{1,0:T(8,128)(2,1)S(1)}, bf16[16,128]{1,0:T(8,128)(2,1)S(1)}, u32[]{:S(2)}, u32[]{:S(2)}) collective-permute-start(bf16[16,128]{1,0:T(8,128)(2,1)S(1)} %fusion), channel_id=1, source_target_pairs={{0,64},{16,80},{32,96},{48,112},{64,0},{80,16},{96,32},{112,48},{1... | collective-permute-start | bytes 12296 | tf_op jit(solution)/shard_map/ppermute | solution.py:238
  89.6 4.6 %collective-permute-start.17 = (bf16[32,128]{1,0:T(8,128)(2,1)S(1)}, bf16[32,128]{1,0:T(8,128)(2,1)S(1)}, u32[]{:S(2)}, u32[]{:S(2)}) collective-permute-start(bf16[32,128]{1,0:T(8,128)(2,1)S(1)} %pad_maximum_fusion.18), channel_id=1, source_target_pairs={{0,32},{16,48},{32,0},{48,16},{64,96},{80,112},{96,64},{112,80},{1... | collective-permute-start | bytes 24584 | tf_op jit(solution)/shard_map/ppermute | solution.py:238
  94.3 5.3 %collective-permute-start.18 = (bf16[64,128]{1,0:T(8,128)(2,1)S(1)}, bf16[64,128]{1,0:T(8,128)(2,1)S(1)}, u32[]{:S(2)}, u32[]{:S(2)}) collective-permute-start(bf16[64,128]{1,0:T(8,128)(2,1)S(1)} %pad_maximum_fusion.16), channel_id=1, source_target_pairs={{0,128},{16,144},{32,160},{48,176},{64,192},{80,208},{96,224},{112... | collective-permute-start | bytes 49160 | tf_op jit(solution)/shard_map/ppermute | solution.py:238
  99.6 5.5 %collective-permute-start.19 = (bf16[128,128]{1,0:T(8,128)(2,1)S(1)}, bf16[128,128]{1,0:T(8,128)(2,1)S(1)}, u32[]{:S(2)}, u32[]{:S(2)}) collective-permute-start(bf16[128,128]{1,0:T(8,128)(2,1)S(1)} %pad_maximum_fusion.14), channel_id=1, source_target_pairs={{0,8},{1,9},{2,10},{3,11},{4,12},{5,13},{6,14},{7,15},{8,0},{9,1},... | collective-permute-start | bytes 98312 | tf_op jit(solution)/shard_map/ppermute | solution.py:238
  102.5 3.0 %collective-permute-start.4 = (bf16[32,6,128]{2,0,1:T(8,128)(2,1)S(1)}, bf16[32,6,128]{2,0,1:T(8,128)(2,1)S(1)}, u32[]{:S(2)}, u32[]{:S(2)}) collective-permute-start(bf16[32,6,128]{2,0,1:T(8,128)(2,1)S(1)} %bitcast.113), channel_id=1, source_target_pairs={{0,1},{1,2},{2,3},{3,4},{4,5},{5,6},{6,7},{7,8},{8,9},{9,10},{10,1... | collective-permute-start | bytes 147464 | tf_op jit(solution)/shard_map/ppermute | solution.py:214
  103.8 10.7 %collective-permute-start.5 = (bf16[32,6,128]{2,0,1:T(8,128)(2,1)S(1)}, bf16[32,6,128]{2,0,1:T(8,128)(2,1)S(1)}, u32[]{:S(2)}, u32[]{:S(2)}) collective-permute-start(bf16[32,6,128]{2,0,1:T(8,128)(2,1)S(1)} %bitcast.112), channel_id=1, source_target_pairs={{1,0},{2,1},{3,2},{4,3},{5,4},{6,5},{7,6},{8,7},{9,8},{10,9},{11,1... | collective-permute-start | bytes 147464 | tf_op jit(solution)/shard_map/ppermute | solution.py:219
  105.2 4.5 %collective-permute-start.20 = (bf16[256,128]{1,0:T(8,128)(2,1)S(1)}, bf16[256,128]{1,0:T(8,128)(2,1)S(1)}, u32[]{:S(2)}, u32[]{:S(2)}) collective-permute-start(bf16[256,128]{1,0:T(8,128)(2,1)S(1)} %pad_maximum_fusion.10), channel_id=1, source_target_pairs={{0,16},{16,0},{32,48},{48,32},{64,80},{80,64},{96,112},{112,96},{1... | collective-permute-start | bytes 196616 | tf_op jit(solution)/shard_map/ppermute | solution.py:238
  109.7 7.7 %collective-permute-start.21 = (bf16[512,128]{1,0:T(8,128)(2,1)S(1)}, bf16[512,128]{1,0:T(8,128)(2,1)S(1)}, u32[]{:S(2)}, u32[]{:S(2)}) collective-permute-start(bf16[512,128]{1,0:T(8,128)(2,1)S(1)} %pad_maximum_fusion.6), channel_id=1, source_target_pairs={{0,2},{1,3},{2,0},{3,1},{4,6},{5,7},{6,4},{7,5},{8,10},{9,11},{10,... | collective-permute-start | bytes 393224 | tf_op jit(solution)/shard_map/ppermute | solution.py:238
  117.5 19.8 %copy-start.1 = (bf16[4,4,4,64,128]{4,3,2,1,0:T(8,128)(2,1)S(1)}, bf16[4,4,4,64,128]{4,3,2,1,0:T(8,128)(2,1)}, u32[]{:S(2)}) copy-start(bf16[4,4,4,64,128]{4,3,2,1,0:T(8,128)(2,1)} %kern.3) | copy-start | bytes 3145732
  117.6 12.0 %collective-permute-start.22 = (bf16[1024,128]{1,0:T(8,128)(2,1)S(1)}, bf16[1024,128]{1,0:T(8,128)(2,1)S(1)}, u32[]{:S(2)}, u32[]{:S(2)}) collective-permute-start(bf16[1024,128]{1,0:T(8,128)(2,1)S(1)} %pad_maximum_fusion.3), channel_id=1, source_target_pairs={{0,4},{1,5},{2,6},{3,7},{4,0},{5,1},{6,2},{7,3},{8,12},{9,13},{10,... | collective-permute-start | bytes 786440 | tf_op jit(solution)/shard_map/ppermute | solution.py:238
  119.5 10.4 %collective-permute-start.6 = (bf16[2,6,17,128]{3,2,1,0:T(8,128)(2,1)S(1)}, bf16[2,6,17,128]{3,2,1,0:T(8,128)(2,1)S(1)}, u32[]{:S(2)}, u32[]{:S(2)}) collective-permute-start(bf16[2,6,17,128]{3,2,1,0:T(8,128)(2,1)S(1)} %pad_maximum_fusion.7), channel_id=1, source_target_pairs={{0,16},{16,32},{32,48},{48,64},{64,80},{80,96},{96,112},{112,128},... | collective-permute-start | bytes 156680 | tf_op jit(solution)/shard_map/ppermute | solution.py:214
  127.5 9.9 %collective-permute-start.7 = (bf16[2,6,17,128]{3,2,1,0:T(8,128)(2,1)S(1)}, bf16[2,6,17,128]{3,2,1,0:T(8,128)(2,1)S(1)}, u32[]{:S(2)}, u32[]{:S(2)}) collective-permute-start(bf16[2,6,17,128]{3,2,1,0:T(8,128)(2,1)S(1)} %pad_maximum_fusion.8), channel_id=1, source_target_pairs={{16,0},{32,16},{48,32},{64,48},{80,64},{96,80},{112,96},{128,112},... | collective-permute-start | bytes 156680 | tf_op jit(solution)/shard_map/ppermute | solution.py:219
  129.8 14.2 %collective-permute-start.23 = (bf16[2048,128]{1,0:T(8,128)(2,1)S(1)}, bf16[2048,128]{1,0:T(8,128)(2,1)S(1)}, u32[]{:S(2)}, u32[]{:S(2)}) collective-permute-start(bf16[2048,128]{1,0:T(8,128)(2,1)S(1)} %pad_maximum_fusion.1), channel_id=1, source_target_pairs={{0,1},{1,0},{2,3},{3,2},{4,5},{5,4},{6,7},{7,6},{8,9},{9,8},{10,11... | collective-permute-start | bytes 1572872 | tf_op jit(solution)/shard_map/ppermute | solution.py:238
where the time goes:
time: 146 us
  waiting for transfers between devices  67.2 us (46%)
  starting transfers between devices  48.9 us (33%)
  Pallas kernels  18 us (12%)
  other arithmetic  7.31 us (5%)
  local copies, waits for them, and re-layouts  3.02 us (2%)
    ppermute x16, waiting for transfers between devices, swap(): lax.ppermute(values, axis, [(i, i ^ bit) for i in range(lax.axis_size(axi...  57 us
    ppermute x16, starting transfers between devices, swap(): lax.ppermute(values, axis, [(i, i ^ bit) for i in range(lax.axis_size(axi...  24 us
    ppermute x4, starting transfers between devices, from_lower(): return lax.ppermute(values, axis, [(i, i + 1) for i in range(count - 1)])  17.5 us
    pallas_call x1, Pallas kernels, run_forward(): pl.pallas_call(forward_body, out_shape=(jax.ShapeDtypeStruct((nx, 2, nz,...  12 us
    ppermute x4, waiting for transfers between devices, from_upper(): return lax.ppermute(values, axis, [(i + 1, i) for i in range(count - 1)])  9.84 us
    ppermute x4, starting transfers between devices, from_upper(): return lax.ppermute(values, axis, [(i + 1, i) for i in range(count - 1)])  7.42 us
    pallas_call x1, Pallas kernels, run_backward(): pl.pallas_call(backward_body, out_shape=jax.ShapeDtypeStruct((nx2 // 2, n...  5.97 us
  transfers between devices with their start and end apart: 24, of which 17 were waited for; matrix products, arithmetic and copies ran while one was open for 2% of the time, Pallas kernels for 4%

commit v1 on v0

v1 whole, which is shorter than its diff:
```python
import jax
import jax.numpy as jnp
from jax import lax
from jax.experimental import pallas as pl
from jax.experimental.pallas import tpu as pltpu
from jax.sharding import PartitionSpec as P


SLOPE = 0.2
F32 = jnp.float32
BF16 = jnp.bfloat16

TAP_X = ((2, 0), (3, 1))
TAP_Y = ((1, 3), (2, 0))
SHIFT_Y = ((1, 0), (1, 2))
TAP_Z = ((3, 1, None), (None, 2, 0))


def dot_nt(a, b):
    return lax.dot_general(a, b, (((1,), (1,)), ((), ())), preferred_element_type=F32)


def forward_body(upper, low, ylo, yhi, xlo, xhi, kern, bias, cot, out, dpre, keep, give, bgrad, wt, xf, xs, im, c32, o32, ch32, dd, ddt, kgrad):
    nx, nz, ny, ch = low.shape
    half = ch // 2
    rows = (nx + 1) * ny
    total = rows * nz

    for z in range(nz):
        xf[z, pl.ds(1, nx), 8:8 + ny, :] = low[:, z].astype(F32)
        xf[z, 0, 7:9 + ny, :] = xlo[z, 2 * ny:3 * ny + 2].astype(F32)
        xf[z, nx + 1, 7:9 + ny, :] = xhi[z, 2 * ny:3 * ny + 2].astype(F32)
    for x in range(nx):
        xf[:, 1 + x, 7, :] = ylo[x].astype(F32)
        xf[:, 1 + x, 8 + ny, :] = yhi[x].astype(F32)
    xs[:, 0] = jnp.zeros(xs.shape[:1] + xs.shape[2:], BF16)
    xs[:, nz + 1] = jnp.zeros(xs.shape[:1] + xs.shape[2:], BF16)

    def shift_step(z, carry):
        for s in range(3):
            xs[s, 1 + z] = xf[z, :, 7 + s:7 + s + ny, :].astype(BF16)
        return carry

    lax.fori_loop(0, nz, shift_step, 0)

    for py in range(2):
        for px in range(2):
            for c in range(2):
                row = px * ch + c * half
                for ux in range(2):
                    for vy in range(2):
                        for dz in range(3):
                            col = ((ux * 2 + vy) * 3 + dz) * ch
                            tz = TAP_Z[c][dz]
                            block = jnp.zeros((half, ch), BF16) if tz is None else kern[TAP_X[px][ux], TAP_Y[py][vy], tz]
                            wt[py, row:row + half, col:col + ch] = block

    pad = im.shape[1] - total
    im[:, total:, :] = jnp.zeros((2, pad, im.shape[2]), BF16)
    dd[:, total:, :] = jnp.zeros((2, pad, dd.shape[2]), BF16)
    bias_row = bias[...]

    def layer_step(z, acc):
        base = pl.multiple_of(z * rows, ny)
        c32[...] = cot[:, :, z].astype(F32)
        ch32[0] = xlo[z, 0:2 * ny].astype(F32)
        ch32[1] = xhi[z, 0:2 * ny].astype(F32)
        for py in range(2):
            for ux in range(2):
                for vy in range(2):
                    for dz in range(3):
                        col = ((ux * 2 + vy) * 3 + dz) * ch
                        im[py, pl.ds(base, rows), col:col + ch] = xs[SHIFT_Y[py][vy], z + dz, ux:ux + nx + 1].reshape(rows, ch)
            pre = dot_nt(im[py, pl.ds(base, rows), :], wt[py])
            dd[py, pl.ds(base, ny), 0:ch] = jnp.zeros((ny, ch), BF16)
            dd[py, pl.ds(base + nx * ny, ny), ch:2 * ch] = jnp.zeros((ny, ch), BF16)
            for q in range(2):
                part = pre[0:nx * ny, ch:2 * ch] if q == 0 else pre[ny:, 0:ch]
                part = part + bias_row
                up = part > 0
                cots = c32[:, q, pl.ds(py, ny, stride=2), :].reshape(nx * ny, ch)
                grad = (cots * jnp.where(up, 1.0, SLOPE)).astype(BF16)
                o32[:, q, pl.ds(py, ny, stride=2), :] = jnp.where(up, part, SLOPE * part).reshape(nx, ny, ch)
                if q == 0:
                    dd[py, pl.ds(base, nx * ny), ch:2 * ch] = grad
                else:
                    dd[py, pl.ds(base + ny, nx * ny), 0:ch] = grad
                dpre[py, q:q + nx, 1 - q, z] = grad.reshape(nx, ny, ch)
                acc = acc + jnp.sum(grad.astype(F32).reshape(nx * ny // 8, 8, ch), axis=0)
            for side in range(2):
                part = (pre[0:ny, 0:ch] if side == 0 else pre[nx * ny:, ch:2 * ch]) + bias_row
                cots = ch32[side, pl.ds(py, ny, stride=2), :]
                dpre[py, side * nx, side, z] = (cots * jnp.where(part > 0, 1.0, SLOPE)).astype(BF16)
        out[:, :, z] = o32[...].astype(BF16)
        return acc

    sums = jnp.sum(lax.fori_loop(0, nz, layer_step, jnp.zeros((8, ch), F32)), axis=0, keepdims=True)
    high = sums.astype(BF16)
    rest = (sums - high.astype(F32)).astype(BF16)
    bgrad[...] = jnp.broadcast_to(high.astype(F32) + rest.astype(F32), bgrad.shape)

    for py in range(2):
        ddt[py] = dd[py].T
    for py in range(2):
        for block in range(im.shape[2] // (2 * ch)):
            terms = jnp.dot(ddt[py], im[py, :, block * 2 * ch:(block + 1) * 2 * ch], preferred_element_type=F32)
            for side in range(2):
                which = block * 2 + side
                ux, vy, dz = which // 6, which // 3 % 2, which % 3
                for px in range(2):
                    for c in range(2):
                        tz = TAP_Z[c][dz]
                        if tz is not None:
                            tx = TAP_X[px][ux]
                            at = (((tx % 2) * 4 + TAP_Y[py][vy]) * 4 + tz) * half
                            row = px * ch + c * half
                            kgrad[tx // 2, at:at + half] = terms[row:row + half, side * ch:(side + 1) * ch]
    mine = upper[0]
    taps = keep.shape[0]
    keep[...] = kgrad[mine]
    give[0:taps] = kgrad[1 - mine].astype(BF16)
    for k, extra in enumerate((high, rest)):
        give[taps + 8 * k:taps + 8 * k + 8] = jnp.broadcast_to(extra, (8, ch))


def run_forward(upper, low, ylo, yhi, xlo, xhi, kern, bias_row, cot):
    nx, nz, ny, ch = low.shape
    rows = (nx + 1) * ny
    padded = -(-rows * nz // 128) * 128
    pairs = cot.reshape(nx, 2, nz, 2 * ny, ch)
    vmem = pl.BlockSpec(memory_space=pltpu.VMEM)
    taps = 32 * ch // 2
    out, dpre, keep, give, bgrad, wt = pl.pallas_call(
        forward_body,
        out_shape=(
            jax.ShapeDtypeStruct((nx, 2, nz, 2 * ny, ch), BF16),
            jax.ShapeDtypeStruct((2, nx + 1, 2, nz, ny, ch), BF16),
            jax.ShapeDtypeStruct((taps, ch), F32),
            jax.ShapeDtypeStruct((taps + 16, ch), BF16),
            jax.ShapeDtypeStruct((8, ch), F32),
            jax.ShapeDtypeStruct((2, 2 * ch, 12 * ch), BF16),
        ),
        in_specs=[pl.BlockSpec(memory_space=pltpu.SMEM)] + [vmem] * 8,
        out_specs=(vmem,) * 6,
        scratch_shapes=[
            pltpu.VMEM((nz, nx + 2, ny + 16, ch), F32),
            pltpu.VMEM((3, nz + 2, nx + 2, ny, ch), BF16),
            pltpu.VMEM((2, padded, 12 * ch), BF16),
            pltpu.VMEM((nx, 2, 2 * ny, ch), F32),
            pltpu.VMEM((nx, 2, 2 * ny, ch), F32),
            pltpu.VMEM((2, 2 * ny, ch), F32),
            pltpu.VMEM((2, padded, 2 * ch), BF16),
            pltpu.VMEM((2, 2 * ch, padded), BF16),
            pltpu.VMEM((2, taps, ch), F32),
        ],
        compiler_params=pltpu.CompilerParams(vmem_limit_bytes=56 << 20),
        cost_estimate=pl.CostEstimate(flops=12 * 2**30, bytes_accessed=8 << 20, transcendentals=0),
        name="forward",
    )(upper, low, ylo, yhi, xlo, xhi, kern, bias_row, pairs)
    return out.reshape(2 * nx, nz, 2 * ny, ch), dpre, keep, give, bgrad, wt


def backward_body(dpre, cols, ccols, kern, bias, wt, grad, df, ds, wb, gh):
    _, duals, _, nz, ny, ch = dpre.shape
    nx = duals - 1
    half = ch // 2
    lanes = gh.shape[3]
    bias_row = bias[...]
    for py in range(2):
        pieces = []
        for ux in range(2):
            for vy in range(2):
                which = ((3, 2), (0, 1))[py][vy]
                for dz in range(3):
                    pieces.append(cols[which, dz:dz + nz, ux:ux + lanes, :].reshape(nz * lanes, ch).astype(BF16))
        pre = dot_nt(jnp.concatenate(pieces, axis=1), wt[py])
        for px in range(2):
            part = pre[:, px * ch:(px + 1) * ch] + bias_row
            cots = ccols[py, px].reshape(nz * lanes, ch)
            gh[py, px] = (cots * jnp.where(part > 0, 1.0, SLOPE)).astype(BF16).astype(F32).reshape(nz, lanes, ch)
    zero = jnp.zeros((nx + 1, 2, ny, ch), BF16)
    for var in range(4):
        ds[var, 0] = zero
        ds[var, nz + 1] = zero

    def layer_load(z, carry):
        for py in range(2):
            df[py, :, :, 8:8 + ny, :] = dpre[py, :, :, z].astype(F32)
            for px in range(2):
                df[py, :, px, 7 if py else 8 + ny, :] = gh[py, px, z, 0:nx + 1]
        for py in range(2):
            for vy in range(2):
                lead = 8 if vy == 0 else (9 if py == 0 else 7)
                ds[py * 2 + vy, 1 + z] = df[py, :, :, lead:lead + ny, :].astype(BF16)
        return carry

    lax.fori_loop(0, nz, layer_load, 0)
    for py in range(2):
        for vy in range(2):
            for q in range(4):
                row = ((py * 2 + vy) * 4 + q) * 2 * ch
                ty = TAP_Y[py][vy]
                for place, tz in enumerate((1, 2, 3, 0)):
                    at = row + place * half
                    wb[at:at + half, :] = kern[q, ty, tz]
    lane = lax.broadcasted_iota(jnp.int32, (nx, ny, ch), 2)

    def layer_step(z, carry):
        acc = jnp.zeros((nx * ny, ch), F32)
        for var in range(4):
            pieces = []
            for q in range(4):
                same = ds[var, 1 + z, q // 2:q // 2 + nx, q % 2]
                above = ds[var, 2 + z, q // 2:q // 2 + nx, q % 2]
                below = ds[var, z, q // 2:q // 2 + nx, q % 2]
                mixed = jnp.where(lane < half, above.astype(F32), below.astype(F32)).astype(BF16)
                pieces += [same.reshape(nx * ny, ch), mixed.reshape(nx * ny, ch)]
            acc = acc + jnp.dot(jnp.concatenate(pieces, axis=1), wb[var * 8 * ch:(var + 1) * 8 * ch, :], preferred_element_type=F32)
        grad[:, z] = acc.astype(BF16).reshape(nx, ny, ch)
        return carry

    lax.fori_loop(0, nz, layer_step, 0)


def run_backward(dpre, cols, ccols, kern, bias_row, wt):
    _, duals, _, nz, ny, ch = dpre.shape
    nx = duals - 1
    vmem = pl.BlockSpec(memory_space=pltpu.VMEM)
    return pl.pallas_call(
        backward_body,
        out_shape=jax.ShapeDtypeStruct((nx, nz, ny, ch), BF16),
        in_specs=[vmem] * 6,
        out_specs=vmem,
        scratch_shapes=[
            pltpu.VMEM((2, nx + 1, 2, ny + 16, ch), F32),
            pltpu.VMEM((4, nz + 2, nx + 1, 2, ny, ch), BF16),
            pltpu.VMEM((32 * ch, ch), BF16),
            pltpu.VMEM((2, 2, nz, nx + 8, ch), F32),
        ],
        compiler_params=pltpu.CompilerParams(vmem_limit_bytes=40 << 20),
        cost_estimate=pl.CostEstimate(flops=4 * 2**30, bytes_accessed=4 << 20, transcendentals=0),
        name="backward",
    )(dpre, cols, ccols, kern, bias_row, wt)


def from_both(first, last, axis):
    count = lax.axis_size(axis)
    odd = lax.axis_index(axis) % 2 == 1
    inner = lax.ppermute(jnp.where(odd, first, last), axis, [(i, i ^ 1) for i in range(count)])
    outer = lax.ppermute(jnp.where(odd, last, first), axis, [(i, i + 1 if i % 2 else i - 1) for i in range(1, count - 1)])
    return jnp.where(odd, inner, outer), jnp.where(odd, outer, inner)


HALVE = (("gy", 1), ("gy", 4), ("gy", 2), ("gy", 8))
GROUPS = (("gx", (1, 8, 9)), ("gx", (2, 4, 6)))


def swap(values, axis, bits):
    return lax.ppermute(values, axis, [(i, i ^ bits) for i in range(lax.axis_size(axis))])


def rounded(values):
    return lax.reduce_precision(values, 8, 7)


def with_extra(values, extra):
    high = rounded(extra)
    tail = [jnp.broadcast_to(part.astype(BF16), (8,) + part.shape[1:]) for part in (high, rounded(extra - high))]
    return jnp.concatenate([values.astype(BF16)] + tail, axis=0), high + rounded(extra - high)


def take_extra(message):
    rows = message.shape[0] - 16
    wide = message.astype(F32)
    return wide[:rows], wide[rows:rows + 1] + wide[rows + 8:rows + 9]


def sum_over_devices(keep, message, brow):
    steps = [(axis, bit) for axis, bit in HALVE if bit < lax.axis_size(axis)]
    groups = [(axis, [bits for bits in some if bits < lax.axis_size(axis)]) for axis, some in GROUPS]
    extra = brow[0:1]
    for at, (axis, bit) in enumerate(steps):
        if at:
            half = part.shape[0] // 2
            up = (lax.axis_index(axis) & bit) != 0
            keep = jnp.where(up, part[half:], part[:half])
            message, extra = with_extra(jnp.where(up, part[:half], part[half:]), extra)
        came, came_extra = take_extra(swap(message, axis, bit))
        part = keep + came
        extra = extra + came_extra
    for axis, some in groups:
        own = rounded(part)
        message, own_extra = with_extra(own, extra)
        arrived = [take_extra(swap(message, axis, bits)) for bits in some]
        if len(arrived) == 3:
            part = (own + arrived[0][0]) + (arrived[1][0] + arrived[2][0])
            extra = (own_extra + arrived[0][1]) + (arrived[1][1] + arrived[2][1])
        else:
            for more, more_extra in arrived:
                part, extra = own + more, own_extra + more_extra
    grown = part.astype(BF16)
    for axis, bit in steps[::-1]:
        up = (lax.axis_index(axis) & bit) != 0
        came = swap(grown, axis, bit)
        grown = jnp.concatenate([jnp.where(up, came, grown), jnp.where(up, grown, came)], axis=0)
    return grown.astype(F32), extra


def per_device(low_res, kernel, bias, cotangent):
    low = jnp.transpose(low_res, (0, 2, 1, 3))
    cot = jnp.transpose(cotangent, (0, 2, 1, 3))
    nx, nz, ny, ch = low.shape
    bias_row = jnp.concatenate([bias, bias]).reshape(1, ch)

    first = jnp.concatenate([low[:, :, 0], cot[:, :, 0]], axis=0)
    last = jnp.concatenate([low[:, :, ny - 1], cot[:, :, 2 * ny - 1]], axis=0)
    ylo, yhi = from_both(first, last, "gy")

    def row(cell, output):
        pieces = [cot[output], ylo[cell][:, None], low[cell], yhi[cell][:, None], ylo[nx + output][:, None], yhi[nx + output][:, None]]
        return jnp.concatenate(pieces, axis=1)

    xlo, xhi = from_both(row(0, 0), row(nx - 1, 2 * nx - 1), "gx")
    axis, bit = HALVE[0]
    upper = (lax.axis_index(axis) // bit % 2).astype(jnp.int32).reshape(1)
    out, dpre, keep, give, bgrad, wt = run_forward(upper, low, ylo, yhi, xlo, xhi, kernel, bias_row, cot)

    def column(at, middle):
        first, last = xlo[:, at][:, None], xhi[:, at][:, None]
        return jnp.concatenate([first, jnp.transpose(middle, (1, 0, 2)), last], axis=1)

    cols = jnp.stack([column(2 * ny, ylo[:nx]), column(2 * ny + 1, low[:, :, 0]), column(3 * ny, low[:, :, ny - 1]), column(3 * ny + 1, yhi[:nx])])
    cols = jnp.pad(cols.astype(F32), ((0, 0), (1, 1), (0, 14), (0, 0)))
    ccols = jnp.stack([column(3 * ny + 3, yhi[nx:]), column(3 * ny + 2, ylo[nx:])]).astype(F32)
    ccols = jnp.transpose(ccols.reshape(2, nz, nx + 1, 2, ch), (0, 3, 1, 2, 4))
    ccols = jnp.pad(ccols, ((0, 0), (0, 0), (0, 0), (0, 7), (0, 0)))
    grad = run_backward(dpre, cols, ccols, kernel, bias_row, wt)
    kernel_sum, bias_sum = sum_over_devices(keep, give, bgrad)

    grid_rows = lax.axis_size("gx") * nx
    output = jnp.transpose(out, (0, 2, 1, 3))
    input_grad = jnp.transpose(grad, (0, 2, 1, 3))
    kernel_grad = kernel_sum.reshape(kernel.shape) / grid_rows
    bias_grad = jnp.sum(bias_sum.reshape(2, ch // 2), axis=0) / grid_rows
    return (output, input_grad, kernel_grad, bias_grad)


def solution(mesh):
    return jax.shard_map(
        per_device,
        mesh=mesh,
        in_specs=(P("gx", "gy", None, None), P(), P(), P("gx", "gy", None, None)),
        out_specs=(P("gx", "gy", None, None), P("gx", "gy", None, None), P(), P()),
        check_vma=False,
    )
```

time: 146 us -> 109 us (0.75)
  the two profiles are of different devices: /device:TPU:224 before, /device:TPU:1 now
where the time goes in v1:
time: 109 us
  starting transfers between devices  43.3 us (40%)
  waiting for transfers between devices  31.7 us (29%)
  Pallas kernels  18.9 us (17%)
  local copies, waits for them, and re-layouts  7.89 us (7%)
  other arithmetic  5.57 us (5%)
  between operations  1.18 us (1%)
    ppermute x14, starting transfers between devices, swap(): lax.ppermute(values, axis, [(i, i ^ bits) for i in range(lax.axis_size(ax...  33.4 us
    ppermute x14, waiting for transfers between devices, swap(): lax.ppermute(values, axis, [(i, i ^ bits) for i in range(lax.axis_size(ax...  30.9 us
    pallas_call x1, Pallas kernels, run_forward(): pl.pallas_call(forward_body, out_shape=(jax.ShapeDtypeStruct((nx, 2, nz,...  12.4 us
    pallas_call x1, Pallas kernels, run_backward(): pl.pallas_call(backward_body, out_shape=jax.ShapeDtypeStruct((nx, nz, ny,...  6.52 us
    ppermute x2, starting transfers between devices, from_both(): lax.ppermute(jnp.where(odd, last, first), axis, [(i, i + 1 if i % 2 else...  5.25 us
    ppermute x2, starting transfers between devices, from_both(): lax.ppermute(jnp.where(odd, first, last), axis, [(i, i ^ 1) for i in rang...  4.7 us
    slice x2, local copies, waits for them, and re-layouts, per_device(): first = jnp.concatenate([low[:, :, 0], cot[:, :, 0]], axis=0)  2.39 us
  transfers between devices with their start and end apart: 18, of which 12 were waited for; matrix products, arithmetic and copies ran while one was open for 6% of the time, Pallas kernels for 6%

profile of v1, /device:TPU:1, one launch (start us, length us, event | category | flops | bytes accessed | tf_op | source)
XLA Modules:
  0.0 108.6 jit_solution(12336220866971044062)
XLA Ops:
  0.7 1.3 %fusion.33 = (bf16[32,6,1,128]{3,2,1,0:T(2,128)(2,1)S(1)}, bf16[32,6,1,128]{3,2,1,0:T(2,128)(2,1)S(1)}) fusion(bf16[32,6,32,128]{3,2,1,0:T(8,128)(2,1)} %bitcast.89), kind=kLoop, calls=%fused_computation.126 | loop fusion | bytes 196608 | tf_op jit(solution)/shard_map/slice | solution.py:315
  1.9 1.1 %fusion.34 = (bf16[16,6,1,128]{3,2,1,0:T(2,128)(2,1)S(1)}, bf16[16,6,1,128]{3,2,1,0:T(2,128)(2,1)S(1)}) fusion(bf16[16,6,16,128]{3,2,1,0:T(8,128)(2,1)} %bitcast.92), kind=kLoop, calls=%fused_computation.127 | loop fusion | bytes 98304 | tf_op jit(solution)/shard_map/slice | solution.py:315
  3.1 4.6 %collective-permute-start.1 = (bf16[48,6,128]{2,0,1:T(8,128)(2,1)S(1)}, bf16[48,6,128]{2,0,1:T(8,128)(2,1)S(1)}, u32[]{:S(2)}, u32[]{:S(2)}) collective-permute-start(bf16[48,6,128]{2,0,1:T(8,128)(2,1)S(1)} %get-tuple-element.50), channel_id=1, source_target_pairs={{1,2},{2,1},{3,4},{4,3},{5,6},{6,5},{7,8},{8,7},{9,10},{10,9},{11,... | collective-permute-start | bytes 221192 | tf_op jit(solution)/shard_map/ppermute | solution.py:250
  7.8 0.8 slice_bitcast_fusion.2
  8.7 0.8 slice_bitcast_fusion.6
  11.0 4.6 %collective-permute-start.2 = (bf16[6,52,128]{2,1,0:T(8,128)(2,1)S(1)}, bf16[6,52,128]{2,1,0:T(8,128)(2,1)S(1)}, u32[]{:S(2)}, u32[]{:S(2)}) collective-permute-start(bf16[6,52,128]{2,1,0:T(8,128)(2,1)S(1)} %get-tuple-element.47), channel_id=1, source_target_pairs={{0,16},{16,0},{32,48},{48,32},{64,80},{80,64},{96,112},{112,96},{1... | collective-permute-start | bytes 239624 | tf_op jit(solution)/shard_map/ppermute | solution.py:249
  18.1 0.7 broadcast_select_fusion.6
  18.8 12.4 %forward.1 = (bf16[16,2,6,32,128]{4,3,2,1,0:T(8,128)(2,1)}, bf16[2,17,2,6,16,128]{5,4,3,2,1,0:T(8,128)(2,1)}, f32[2048,128]{1,0:T(8,128)}, bf16[2064,128]{1,0:T(...) custom-call(s32[1]{0:T(128)} %bitcast.upper, bf16[16,6,16,128]{3,2,1,0:T(8,128)(2,1)} %bitcast.94, ...), custom_call_target="tpu_custom_call" | custom-call | flops 12884901888 | bytes 8388608 | tf_op jit(solution)/shard_map/forward/pallas_call | solution.py:133
  31.2 1.1 %collective-permute-start.4 = (bf16[2064,128]{1,0:T(8,128)(2,1)}, bf16[2064,128]{1,0:T(8,128)(2,1)S(1)}, u32[]{:S(2)}, u32[]{:S(2)}) collective-permute-start(bf16[2064,128]{1,0:T(8,128)(2,1)} %get-tuple-element.14), channel_id=1, source_target_pairs={{0,1},{1,0},{2,3},{3,2},{4,5},{5,4},{6,7},{7,6},{8,9},{9,8},{10,11... | collective-permute-start | bytes 1585160 | tf_op jit(solution)/shard_map/ppermute | solution.py:259
  32.3 1.7 %collective-permute-done.4 = bf16[2064,128]{1,0:T(8,128)(2,1)S(1)} collective-permute-done((bf16[2064,128]{1,0:T(8,128)(2,1)}, bf16[2064,128]{1,0:T(8,128)(2,1)S(1)}, u32[]{:S(2)}, u32[]{:S(2)}) %collective-permute-start.4) | collective-permute-done | bytes 528416 | tf_op jit(solution)/shard_map/ppermute | solution.py:259
  35.1 2.3 %collective-permute-start.5 = (bf16[1040,128]{1,0:T(8,128)(2,1)S(1)}, bf16[1040,128]{1,0:T(8,128)(2,1)S(1)}, u32[]{:S(2)}, u32[]{:S(2)}) collective-permute-start(bf16[1040,128]{1,0:T(8,128)(2,1)S(1)} %pad_maximum_fusion.1), channel_id=1, source_target_pairs={{0,4},{1,5},{2,6},{3,7},{4,0},{5,1},{6,2},{7,3},{8,12},{9,13},{10,... | collective-permute-start | bytes 798728 | tf_op jit(solution)/shard_map/ppermute | solution.py:259
  37.4 0.9 fusion.36
  38.3 5.5 %collective-permute-done.5 = bf16[1040,128]{1,0:T(8,128)(2,1)S(1)} collective-permute-done((bf16[1040,128]{1,0:T(8,128)(2,1)S(1)}, bf16[1040,128]{1,0:T(8,128)(2,1)S(1)}, u32[]{:S(2)}, u32[]{:S(2)}) %collective-permute-start.5) | collective-permute-done | bytes 266272 | tf_op jit(solution)/shard_map/ppermute | solution.py:259
  44.0 1.1 %collective-permute-start.6 = (bf16[528,128]{1,0:T(8,128)(2,1)S(1)}, bf16[528,128]{1,0:T(8,128)(2,1)S(1)}, u32[]{:S(2)}, u32[]{:S(2)}) collective-permute-start(bf16[528,128]{1,0:T(8,128)(2,1)S(1)} %pad_maximum_fusion.3), channel_id=1, source_target_pairs={{0,2},{1,3},{2,0},{3,1},{4,6},{5,7},{6,4},{7,5},{8,10},{9,11},{10,... | collective-permute-start | bytes 405512 | tf_op jit(solution)/shard_map/ppermute | solution.py:259
  45.1 0.9 fusion.35
  46.0 2.3 %collective-permute-done.6 = bf16[528,128]{1,0:T(8,128)(2,1)S(1)} collective-permute-done((bf16[528,128]{1,0:T(8,128)(2,1)S(1)}, bf16[528,128]{1,0:T(8,128)(2,1)S(1)}, u32[]{:S(2)}, u32[]{:S(2)}) %collective-permute-start.6) | collective-permute-done | bytes 135200 | tf_op jit(solution)/shard_map/ppermute | solution.py:259
  48.4 2.5 %collective-permute-start.7 = (bf16[272,128]{1,0:T(8,128)(2,1)S(1)}, bf16[272,128]{1,0:T(8,128)(2,1)S(1)}, u32[]{:S(2)}, u32[]{:S(2)}) collective-permute-start(bf16[272,128]{1,0:T(8,128)(2,1)S(1)} %pad_maximum_fusion.7), channel_id=1, source_target_pairs={{0,8},{1,9},{2,10},{3,11},{4,12},{5,13},{6,14},{7,15},{8,0},{9,1},... | collective-permute-start | bytes 208904 | tf_op jit(solution)/shard_map/ppermute | solution.py:259
  50.9 2.3 %collective-permute-done.7 = bf16[272,128]{1,0:T(8,128)(2,1)S(1)} collective-permute-done((bf16[272,128]{1,0:T(8,128)(2,1)S(1)}, bf16[272,128]{1,0:T(8,128)(2,1)S(1)}, u32[]{:S(2)}, u32[]{:S(2)}) %collective-permute-start.7) | collective-permute-done | bytes 69664 | tf_op jit(solution)/shard_map/ppermute | solution.py:259
  53.3 6.4 %collective-permute-start.10 = (bf16[272,128]{1,0:T(8,128)(2,1)S(1)}, bf16[272,128]{1,0:T(8,128)(2,1)S(1)}, u32[]{:S(2)}, u32[]{:S(2)}) collective-permute-start(bf16[272,128]{1,0:T(8,128)(2,1)S(1)} %pad_maximum_fusion.8), channel_id=1, source_target_pairs={{0,144},{16,128},{32,176},{48,160},{64,208},{80,192},{96,240},{112... | collective-permute-start | bytes 208904 | tf_op jit(solution)/shard_map/ppermute | solution.py:259
  60.2 1.1 collective-permute-start.8
  61.5 3.7 %collective-permute-done.9 = bf16[272,128]{1,0:T(8,128)(2,1)S(1)} collective-permute-done((bf16[272,128]{1,0:T(8,128)(2,1)S(1)}, bf16[272,128]{1,0:T(8,128)(2,1)S(1)}, u32[]{:S(2)}, u32[]{:S(2)}) %collective-permute-start.9) | collective-permute-done | bytes 69664 | tf_op jit(solution)/shard_map/ppermute | solution.py:259
  65.3 3.4 %collective-permute-start.13 = (bf16[272,128]{1,0:T(8,128)(2,1)S(1)}, bf16[272,128]{1,0:T(8,128)(2,1)S(1)}, u32[]{:S(2)}, u32[]{:S(2)}) collective-permute-start(bf16[272,128]{1,0:T(8,128)(2,1)S(1)} %pad_maximum_fusion.9), channel_id=1, source_target_pairs={{0,96},{16,112},{32,64},{48,80},{64,32},{80,48},{96,0},{112,16},{1... | collective-permute-start | bytes 208904 | tf_op jit(solution)/shard_map/ppermute | solution.py:259
  68.7 2.2 %collective-permute-start.12 = (bf16[272,128]{1,0:T(8,128)(2,1)S(1)}, bf16[272,128]{1,0:T(8,128)(2,1)S(1)}, u32[]{:S(2)}, u32[]{:S(2)}) collective-permute-start(bf16[272,128]{1,0:T(8,128)(2,1)S(1)} %pad_maximum_fusion.9), channel_id=1, source_target_pairs={{0,64},{16,80},{32,96},{48,112},{64,0},{80,16},{96,32},{112,48},{1... | collective-permute-start | bytes 208904 | tf_op jit(solution)/shard_map/ppermute | solution.py:259
  71.1 5.4 %collective-permute-done.12 = bf16[272,128]{1,0:T(8,128)(2,1)S(1)} collective-permute-done((bf16[272,128]{1,0:T(8,128)(2,1)S(1)}, bf16[272,128]{1,0:T(8,128)(2,1)S(1)}, u32[]{:S(2)}, u32[]{:S(2)}) %collective-permute-start.12) | collective-permute-done | bytes 69664 | tf_op jit(solution)/shard_map/ppermute | solution.py:259
  76.6 2.3 %collective-permute-start.14 = (bf16[256,128]{1,0:T(8,128)(2,1)S(1)}, bf16[256,128]{1,0:T(8,128)(2,1)S(1)}, u32[]{:S(2)}, u32[]{:S(2)}) collective-permute-start(bf16[256,128]{1,0:T(8,128)(2,1)S(1)} %fusion.9), channel_id=1, source_target_pairs={{0,8},{1,9},{2,10},{3,11},{4,12},{5,13},{6,14},{7,15},{8,0},{9,1},... | collective-permute-start | bytes 196616 | tf_op jit(solution)/shard_map/ppermute | solution.py:259
  78.9 2.5 %collective-permute-done.14 = bf16[256,128]{1,0:T(8,128)(2,1)S(1)} collective-permute-done((bf16[256,128]{1,0:T(8,128)(2,1)S(1)}, bf16[256,128]{1,0:T(8,128)(2,1)S(1)}, u32[]{:S(2)}, u32[]{:S(2)}) %collective-permute-start.14) | collective-permute-done | bytes 65568 | tf_op jit(solution)/shard_map/ppermute | solution.py:259
  82.3 3.1 %collective-permute-done.15 = bf16[512,128]{1,0:T(8,128)(2,1)S(1)} collective-permute-done((bf16[512,128]{1,0:T(8,128)(2,1)S(1)}, bf16[512,128]{1,0:T(8,128)(2,1)S(1)}, u32[]{:S(2)}, u32[]{:S(2)}) %collective-permute-start.15) | collective-permute-done | bytes 131104 | tf_op jit(solution)/shard_map/ppermute | solution.py:259
  85.5 0.9 collective-permute-start.16
  86.5 4.3 %collective-permute-done.16 = bf16[1024,128]{1,0:T(8,128)(2,1)S(1)} collective-permute-done((bf16[1024,128]{1,0:T(8,128)(2,1)S(1)}, bf16[1024,128]{1,0:T(8,128)(2,1)S(1)}, u32[]{:S(2)}, u32[]{:S(2)}) %collective-permute-start.16) | collective-permute-done | bytes 262176 | tf_op jit(solution)/shard_map/ppermute | solution.py:259
  90.9 8.8 %collective-permute-start.17 = (bf16[2048,128]{1,0:T(8,128)(2,1)S(1)}, bf16[2048,128]{1,0:T(8,128)(2,1)S(1)}, u32[]{:S(2)}, u32[]{:S(2)}) collective-permute-start(bf16[2048,128]{1,0:T(8,128)(2,1)S(1)} %pad_maximum_fusion), channel_id=1, source_target_pairs={{0,1},{1,0},{2,3},{3,2},{4,5},{5,4},{6,7},{7,6},{8,9},{9,8},{10,11... | collective-permute-start | bytes 1572872 | tf_op jit(solution)/shard_map/ppermute | solution.py:259
  99.8 6.5 %backward.1 = bf16[16,6,16,128]{3,2,1,0:T(8,128)(2,1)} custom-call(bf16[2,17,2,6,16,128]{5,4,3,2,1,0:T(8,128)(2,1)S(1)} %copy-done.2, f32[4,8,32,128]{3,2,1,0:T(8,128)S(1)} %fusion.2.cols, f32[2,2,6,24,128]{4,3,2,1,0:T(8,128)S(1)} %pad_convert_fusion.ccols, bf16[4,4,4,64,128]{4,3,2,1,0:T(8,128)(2,1)S(1)} %copy-done, f32[1,128]{1,0:T(1,128)S(1)} %copy-done.1, ...), custom_call_target="tpu_custom_call" | custom-call | flops 4294967296 | bytes 4194304 | tf_op jit(solution)/shard_map/backward/pallas_call | solution.py:229
  107.1 1.5 %convert_multiply_fusion = f32[4096,128]{1,0:T(8,128)} fusion(bf16[2048,128]{1,0:T(8,128)(2,1)S(1)} %get-tuple-element.35, bf16[2048,128]{1,0:T(8,128)(2,1)S(1)} %get-tuple-element.34), kind=kLoop, calls=%fused_computation | loop fusion | flops 2621440 | bytes 3145728 | tf_op jit(solution)/shard_map/div | solution.py:343
  (110 shorter events, 8.5 us)
Async XLA Ops:
  0.6 15.0 %copy-start.5 = (f32[64]{0:T(128)S(1)}, f32[64]{0:T(128)}, u32[]{:S(2)}) copy-start(f32[64]{0:T(128)} %param.6) | copy-start | bytes 772
  3.1 6.6 %collective-permute-start.1 = (bf16[48,6,128]{2,0,1:T(8,128)(2,1)S(1)}, bf16[48,6,128]{2,0,1:T(8,128)(2,1)S(1)}, u32[]{:S(2)}, u32[]{:S(2)}) collective-permute-start(bf16[48,6,128]{2,0,1:T(8,128)(2,1)S(1)} %get-tuple-element.50), channel_id=1, source_target_pairs={{1,2},{2,1},{3,4},{4,3},{5,6},{6,5},{7,8},{8,7},{9,10},{10,9},{11,... | collective-permute-start | bytes 221192 | tf_op jit(solution)/shard_map/ppermute | solution.py:250
  7.7 2.0 %collective-permute-start = (bf16[48,6,128]{2,0,1:T(8,128)(2,1)S(1)}, bf16[48,6,128]{2,0,1:T(8,128)(2,1)S(1)}, u32[]{:S(2)}, u32[]{:S(2)}) collective-permute-start(bf16[48,6,128]{2,0,1:T(8,128)(2,1)S(1)} %get-tuple-element.51), channel_id=1, source_target_pairs={{0,1},{1,0},{2,3},{3,2},{4,5},{5,4},{6,7},{7,6},{8,9},{9,8},{10,11... | collective-permute-start | bytes 221192 | tf_op jit(solution)/shard_map/ppermute | solution.py:249
  10.3 7.2 %collective-permute-start.3 = (bf16[6,52,128]{2,1,0:T(8,128)(2,1)S(1)}, bf16[6,52,128]{2,1,0:T(8,128)(2,1)S(1)}, u32[]{:S(2)}, u32[]{:S(2)}) collective-permute-start(bf16[6,52,128]{2,1,0:T(8,128)(2,1)S(1)} %get-tuple-element.46), channel_id=1, source_target_pairs={{16,32},{32,16},{48,64},{64,48},{80,96},{96,80},{112,128},{128,112... | collective-permute-start | bytes 239624 | tf_op jit(solution)/shard_map/ppermute | solution.py:250
  11.0 7.1 %collective-permute-start.2 = (bf16[6,52,128]{2,1,0:T(8,128)(2,1)S(1)}, bf16[6,52,128]{2,1,0:T(8,128)(2,1)S(1)}, u32[]{:S(2)}, u32[]{:S(2)}) collective-permute-start(bf16[6,52,128]{2,1,0:T(8,128)(2,1)S(1)} %get-tuple-element.47), channel_id=1, source_target_pairs={{0,16},{16,0},{32,48},{48,32},{64,80},{80,64},{96,112},{112,96},{1... | collective-permute-start | bytes 239624 | tf_op jit(solution)/shard_map/ppermute | solution.py:249
  31.2 3.7 %copy-start.4 = (f32[2048,128]{1,0:T(8,128)S(1)}, f32[2048,128]{1,0:T(8,128)}, u32[]{:S(2)}) copy-start(f32[2048,128]{1,0:T(8,128)} %get-tuple-element.13) | copy-start | bytes 3145732
  31.2 2.9 %collective-permute-start.4 = (bf16[2064,128]{1,0:T(8,128)(2,1)}, bf16[2064,128]{1,0:T(8,128)(2,1)S(1)}, u32[]{:S(2)}, u32[]{:S(2)}) collective-permute-start(bf16[2064,128]{1,0:T(8,128)(2,1)} %get-tuple-element.14), channel_id=1, source_target_pairs={{0,1},{1,0},{2,3},{3,2},{4,5},{5,4},{6,7},{7,6},{8,9},{9,8},{10,11... | collective-permute-start | bytes 1585160 | tf_op jit(solution)/shard_map/ppermute | solution.py:259
  35.1 8.7 %collective-permute-start.5 = (bf16[1040,128]{1,0:T(8,128)(2,1)S(1)}, bf16[1040,128]{1,0:T(8,128)(2,1)S(1)}, u32[]{:S(2)}, u32[]{:S(2)}) collective-permute-start(bf16[1040,128]{1,0:T(8,128)(2,1)S(1)} %pad_maximum_fusion.1), channel_id=1, source_target_pairs={{0,4},{1,5},{2,6},{3,7},{4,0},{5,1},{6,2},{7,3},{8,12},{9,13},{10,... | collective-permute-start | bytes 798728 | tf_op jit(solution)/shard_map/ppermute | solution.py:259
  44.0 4.3 %collective-permute-start.6 = (bf16[528,128]{1,0:T(8,128)(2,1)S(1)}, bf16[528,128]{1,0:T(8,128)(2,1)S(1)}, u32[]{:S(2)}, u32[]{:S(2)}) collective-permute-start(bf16[528,128]{1,0:T(8,128)(2,1)S(1)} %pad_maximum_fusion.3), channel_id=1, source_target_pairs={{0,2},{1,3},{2,0},{3,1},{4,6},{5,7},{6,4},{7,5},{8,10},{9,11},{10,... | collective-permute-start | bytes 405512 | tf_op jit(solution)/shard_map/ppermute | solution.py:259
  48.4 4.8 %collective-permute-start.7 = (bf16[272,128]{1,0:T(8,128)(2,1)S(1)}, bf16[272,128]{1,0:T(8,128)(2,1)S(1)}, u32[]{:S(2)}, u32[]{:S(2)}) collective-permute-start(bf16[272,128]{1,0:T(8,128)(2,1)S(1)} %pad_maximum_fusion.7), channel_id=1, source_target_pairs={{0,8},{1,9},{2,10},{3,11},{4,12},{5,13},{6,14},{7,15},{8,0},{9,1},... | collective-permute-start | bytes 208904 | tf_op jit(solution)/shard_map/ppermute | solution.py:259
  53.3 8.1 %collective-permute-start.10 = (bf16[272,128]{1,0:T(8,128)(2,1)S(1)}, bf16[272,128]{1,0:T(8,128)(2,1)S(1)}, u32[]{:S(2)}, u32[]{:S(2)}) collective-permute-start(bf16[272,128]{1,0:T(8,128)(2,1)S(1)} %pad_maximum_fusion.8), channel_id=1, source_target_pairs={{0,144},{16,128},{32,176},{48,160},{64,208},{80,192},{96,240},{112... | collective-permute-start | bytes 208904 | tf_op jit(solution)/shard_map/ppermute | solution.py:259
  59.7 5.4 %collective-permute-start.9 = (bf16[272,128]{1,0:T(8,128)(2,1)S(1)}, bf16[272,128]{1,0:T(8,128)(2,1)S(1)}, u32[]{:S(2)}, u32[]{:S(2)}) collective-permute-start(bf16[272,128]{1,0:T(8,128)(2,1)S(1)} %pad_maximum_fusion.8), channel_id=1, source_target_pairs={{0,128},{16,144},{32,160},{48,176},{64,192},{80,208},{96,224},{112... | collective-permute-start | bytes 208904 | tf_op jit(solution)/shard_map/ppermute | solution.py:259
  60.2 4.9 %collective-permute-start.8 = (bf16[272,128]{1,0:T(8,128)(2,1)S(1)}, bf16[272,128]{1,0:T(8,128)(2,1)S(1)}, u32[]{:S(2)}, u32[]{:S(2)}) collective-permute-start(bf16[272,128]{1,0:T(8,128)(2,1)S(1)} %pad_maximum_fusion.8), channel_id=1, source_target_pairs={{0,16},{16,0},{32,48},{48,32},{64,80},{80,64},{96,112},{112,96},{1... | collective-permute-start | bytes 208904 | tf_op jit(solution)/shard_map/ppermute | solution.py:259
  65.3 5.8 %collective-permute-start.13 = (bf16[272,128]{1,0:T(8,128)(2,1)S(1)}, bf16[272,128]{1,0:T(8,128)(2,1)S(1)}, u32[]{:S(2)}, u32[]{:S(2)}) collective-permute-start(bf16[272,128]{1,0:T(8,128)(2,1)S(1)} %pad_maximum_fusion.9), channel_id=1, source_target_pairs={{0,96},{16,112},{32,64},{48,80},{64,32},{80,48},{96,0},{112,16},{1... | collective-permute-start | bytes 208904 | tf_op jit(solution)/shard_map/ppermute | solution.py:259
  68.7 7.8 %collective-permute-start.12 = (bf16[272,128]{1,0:T(8,128)(2,1)S(1)}, bf16[272,128]{1,0:T(8,128)(2,1)S(1)}, u32[]{:S(2)}, u32[]{:S(2)}) collective-permute-start(bf16[272,128]{1,0:T(8,128)(2,1)S(1)} %pad_maximum_fusion.9), channel_id=1, source_target_pairs={{0,64},{16,80},{32,96},{48,112},{64,0},{80,16},{96,32},{112,48},{1... | collective-permute-start | bytes 208904 | tf_op jit(solution)/shard_map/ppermute | solution.py:259
  70.9 5.6 %collective-permute-start.11 = (bf16[272,128]{1,0:T(8,128)(2,1)S(1)}, bf16[272,128]{1,0:T(8,128)(2,1)S(1)}, u32[]{:S(2)}, u32[]{:S(2)}) collective-permute-start(bf16[272,128]{1,0:T(8,128)(2,1)S(1)} %pad_maximum_fusion.9), channel_id=1, source_target_pairs={{0,32},{16,48},{32,0},{48,16},{64,96},{80,112},{96,64},{112,80},{1... | collective-permute-start | bytes 208904 | tf_op jit(solution)/shard_map/ppermute | solution.py:259
  76.6 4.8 %collective-permute-start.14 = (bf16[256,128]{1,0:T(8,128)(2,1)S(1)}, bf16[256,128]{1,0:T(8,128)(2,1)S(1)}, u32[]{:S(2)}, u32[]{:S(2)}) collective-permute-start(bf16[256,128]{1,0:T(8,128)(2,1)S(1)} %fusion.9), channel_id=1, source_target_pairs={{0,8},{1,9},{2,10},{3,11},{4,12},{5,13},{6,14},{7,15},{8,0},{9,1},... | collective-permute-start | bytes 196616 | tf_op jit(solution)/shard_map/ppermute | solution.py:259
  81.4 3.9 %collective-permute-start.15 = (bf16[512,128]{1,0:T(8,128)(2,1)S(1)}, bf16[512,128]{1,0:T(8,128)(2,1)S(1)}, u32[]{:S(2)}, u32[]{:S(2)}) collective-permute-start(bf16[512,128]{1,0:T(8,128)(2,1)S(1)} %pad_maximum_fusion.4), channel_id=1, source_target_pairs={{0,2},{1,3},{2,0},{3,1},{4,6},{5,7},{6,4},{7,5},{8,10},{9,11},{10,... | collective-permute-start | bytes 393224 | tf_op jit(solution)/shard_map/ppermute | solution.py:259
  85.3 14.4 %copy-start.3 = (bf16[2,256,1536]{2,1,0:T(8,128)(2,1)S(1)}, bf16[2,256,1536]{2,1,0:T(8,128)(2,1)}, u32[]{:S(2)}) copy-start(bf16[2,256,1536]{2,1,0:T(8,128)(2,1)} %get-tuple-element.12.wt) | copy-start | bytes 4718596
  85.4 14.3 %copy-start = (bf16[4,4,4,64,128]{4,3,2,1,0:T(8,128)(2,1)S(1)}, bf16[4,4,4,64,128]{4,3,2,1,0:T(8,128)(2,1)}, u32[]{:S(2)}) copy-start(bf16[4,4,4,64,128]{4,3,2,1,0:T(8,128)(2,1)} %kern.3) | copy-start | bytes 3145732
  85.4 14.3 %copy-start.1 = (f32[1,128]{1,0:T(1,128)S(1)}, f32[1,128]{1,0:T(1,128)}, u32[]{:S(2)}) copy-start(f32[1,128]{1,0:T(1,128)} %maximum_bitcast_fusion.5.bias) | copy-start | bytes 1540
  85.4 14.3 %copy-start.2 = (bf16[2,17,2,6,16,128]{5,4,3,2,1,0:T(8,128)(2,1)S(1)}, bf16[2,17,2,6,16,128]{5,4,3,2,1,0:T(8,128)(2,1)}, u32[]{:S(2)}) copy-start(bf16[2,17,2,6,16,128]{5,4,3,2,1,0:T(8,128)(2,1)} %get-tuple-element.11.dpre) | copy-start | bytes 5013508
  85.5 5.3 %collective-permute-start.16 = (bf16[1024,128]{1,0:T(8,128)(2,1)S(1)}, bf16[1024,128]{1,0:T(8,128)(2,1)S(1)}, u32[]{:S(2)}, u32[]{:S(2)}) collective-permute-start(bf16[1024,128]{1,0:T(8,128)(2,1)S(1)} %pad_maximum_fusion.2), channel_id=1, source_target_pairs={{0,4},{1,5},{2,6},{3,7},{4,0},{5,1},{6,2},{7,3},{8,12},{9,13},{10,... | collective-permute-start | bytes 786440 | tf_op jit(solution)/shard_map/ppermute | solution.py:259
  90.9 16.0 %collective-permute-start.17 = (bf16[2048,128]{1,0:T(8,128)(2,1)S(1)}, bf16[2048,128]{1,0:T(8,128)(2,1)S(1)}, u32[]{:S(2)}, u32[]{:S(2)}) collective-permute-start(bf16[2048,128]{1,0:T(8,128)(2,1)S(1)} %pad_maximum_fusion), channel_id=1, source_target_pairs={{0,1},{1,0},{2,3},{3,2},{4,5},{5,4},{6,7},{7,6},{8,9},{9,8},{10,11... | collective-permute-start | bytes 1572872 | tf_op jit(solution)/shard_map/ppermute | solution.py:259

commit v2 on v1

--- a/solution.py
+++ b/solution.py
@@ -20,7 +20,11 @@
     return lax.dot_general(a, b, (((1,), (1,)), ((), ())), preferred_element_type=F32)
 
 
-def forward_body(upper, low, ylo, yhi, xlo, xhi, kern, bias, cot, out, dpre, keep, give, bgrad, wt, xf, xs, im, c32, o32, ch32, dd, ddt, kgrad):
+def forward_body(upper, low, ylo, yhi, xlo, xhi, kern_in, bias, cot_in, out_to, dpre_to, keep, give, bgrad, wt_to, xf, xs, im, c32, o32, ch32, dd, ddt, kgrad, kern, cot, out, dpre, wt, sems):
+    get_kern = pltpu.make_async_copy(kern_in, kern, sems.at[0])
+    get_kern.start()
+    get_cot = pltpu.make_async_copy(cot_in, cot, sems.at[1])
+    get_cot.start()
     nx, nz, ny, ch = low.shape
     half = ch // 2
     rows = (nx + 1) * ny
@@ -43,6 +47,7 @@
 
     lax.fori_loop(0, nz, shift_step, 0)
 
+    get_kern.wait()
     for py in range(2):
         for px in range(2):
             for c in range(2):
@@ -55,10 +60,14 @@
                             block = jnp.zeros((half, ch), BF16) if tz is None else kern[TAP_X[px][ux], TAP_Y[py][vy], tz]
                             wt[py, row:row + half, col:col + ch] = block
 
+    put_wt = pltpu.make_async_copy(wt, wt_to, sems.at[2])
+    put_wt.start()
+
     pad = im.shape[1] - total
     im[:, total:, :] = jnp.zeros((2, pad, im.shape[2]), BF16)
     dd[:, total:, :] = jnp.zeros((2, pad, dd.shape[2]), BF16)
-    bias_row = bias[...]
+    bias_row = jnp.concatenate([bias[...], bias[...]], axis=1)
+    get_cot.wait()
 
     def layer_step(z, acc):
         base = pl.multiple_of(z * rows, ny)
@@ -95,6 +104,10 @@
         return acc
 
     sums = jnp.sum(lax.fori_loop(0, nz, layer_step, jnp.zeros((8, ch), F32)), axis=0, keepdims=True)
+    put_out = pltpu.make_async_copy(out, out_to, sems.at[3])
+    put_out.start()
+    put_dpre = pltpu.make_async_copy(dpre, dpre_to, sems.at[4])
+    put_dpre.start()
     high = sums.astype(BF16)
     rest = (sums - high.astype(F32)).astype(BF16)
     bgrad[...] = jnp.broadcast_to(high.astype(F32) + rest.astype(F32), bgrad.shape)
@@ -121,6 +134,9 @@
     give[0:taps] = kgrad[1 - mine].astype(BF16)
     for k, extra in enumerate((high, rest)):
         give[taps + 8 * k:taps + 8 * k + 8] = jnp.broadcast_to(extra, (8, ch))
+    put_wt.wait()
+    put_out.wait()
+    put_dpre.wait()
 
 
 def run_forward(upper, low, ylo, yhi, xlo, xhi, kern, bias_row, cot):
@@ -128,7 +144,7 @@
     rows = (nx + 1) * ny
     padded = -(-rows * nz // 128) * 128
     pairs = cot.reshape(nx, 2, nz, 2 * ny, ch)
-    vmem = pl.BlockSpec(memory_space=pltpu.VMEM)
+    vmem, stay = pl.BlockSpec(memory_space=pltpu.VMEM), pl.BlockSpec(memory_space=pl.ANY)
     taps = 32 * ch // 2
     out, dpre, keep, give, bgrad, wt = pl.pallas_call(
         forward_body,
@@ -140,8 +156,8 @@
             jax.ShapeDtypeStruct((8, ch), F32),
             jax.ShapeDtypeStruct((2, 2 * ch, 12 * ch), BF16),
         ),
-        in_specs=[pl.BlockSpec(memory_space=pltpu.SMEM)] + [vmem] * 8,
-        out_specs=(vmem,) * 6,
+        in_specs=[pl.BlockSpec(memory_space=pltpu.SMEM)] + [vmem] * 5 + [stay, vmem, stay],
+        out_specs=(stay, stay, vmem, vmem, vmem, stay),
         scratch_shapes=[
             pltpu.VMEM((nz, nx + 2, ny + 16, ch), F32),
             pltpu.VMEM((3, nz + 2, nx + 2, ny, ch), BF16),
@@ -152,6 +168,12 @@
             pltpu.VMEM((2, padded, 2 * ch), BF16),
             pltpu.VMEM((2, 2 * ch, padded), BF16),
             pltpu.VMEM((2, taps, ch), F32),
+            pltpu.VMEM(kern.shape, BF16),
+            pltpu.VMEM(pairs.shape, BF16),
+            pltpu.VMEM(pairs.shape, BF16),
+            pltpu.VMEM((2, nx + 1, 2, nz, ny, ch), BF16),
+            pltpu.VMEM((2, 2 * ch, 12 * ch), BF16),
+            pltpu.SemaphoreType.DMA((5,)),
         ],
         compiler_params=pltpu.CompilerParams(vmem_limit_bytes=56 << 20),
         cost_estimate=pl.CostEstimate(flops=12 * 2**30, bytes_accessed=8 << 20, transcendentals=0),
@@ -165,7 +187,7 @@
     nx = duals - 1
     half = ch // 2
     lanes = gh.shape[3]
-    bias_row = bias[...]
+    bias_row = jnp.concatenate([bias[...], bias[...]], axis=1)
     for py in range(2):
         pieces = []
         for ux in range(2):
@@ -252,7 +274,7 @@
 
 
 HALVE = (("gy", 1), ("gy", 4), ("gy", 2), ("gy", 8))
-GROUPS = (("gx", (1, 8, 9)), ("gx", (2, 4, 6)))
+GROUPS = (("gx", (1, 8, 9)), ("gx", (2, 5, 7)))
 
 
 def swap(values, axis, bits):
@@ -310,7 +332,7 @@
     low = jnp.transpose(low_res, (0, 2, 1, 3))
     cot = jnp.transpose(cotangent, (0, 2, 1, 3))
     nx, nz, ny, ch = low.shape
-    bias_row = jnp.concatenate([bias, bias]).reshape(1, ch)
+    bias_row = bias.reshape(1, -1)
 
     first = jnp.concatenate([low[:, :, 0], cot[:, :, 0]], axis=0)
     last = jnp.concatenate([low[:, :, ny - 1], cot[:, :, 2 * ny - 1]], axis=0)

time: 109 us -> 107 us (0.982)
  starting transfers between devices: 43.3 us -> 42.1 us
    ppermute x14, starting transfers between devices: 33.4 us -> 32.2 us  [swap(): lax.ppermute(values, axis, [(i, i ^ bits) for i in range(lax.axis_size(ax...]
  transfers between devices with their start and end apart: 18 -> 18, of which waited for: 12 -> 13; matrix products, arithmetic and copies ran while one was open for 6% -> 5% of each run, Pallas kernels for 6% -> 6%
where the time goes in v2:
time: 107 us
  starting transfers between devices  42.1 us (39%)
  waiting for transfers between devices  31.9 us (30%)
  Pallas kernels  18.8 us (18%)
  local copies, waits for them, and re-layouts  7.91 us (7%)
  other arithmetic  4.95 us (5%)
  between operations  1.19 us (1%)
    ppermute x14, starting transfers between devices, swap(): lax.ppermute(values, axis, [(i, i ^ bits) for i in range(lax.axis_size(ax...  32.2 us
    ppermute x14, waiting for transfers between devices, swap(): lax.ppermute(values, axis, [(i, i ^ bits) for i in range(lax.axis_size(ax...  30.4 us
    pallas_call x1, Pallas kernels, run_forward(): pl.pallas_call(forward_body, out_shape=(jax.ShapeDtypeStruct((nx, 2, nz,...  12.3 us
    pallas_call x1, Pallas kernels, run_backward(): pl.pallas_call(backward_body, out_shape=jax.ShapeDtypeStruct((nx, nz, ny,...  6.51 us
    ppermute x2, starting transfers between devices, from_both(): lax.ppermute(jnp.where(odd, last, first), axis, [(i, i + 1 if i % 2 else...  5.25 us
    ppermute x2, starting transfers between devices, from_both(): lax.ppermute(jnp.where(odd, first, last), axis, [(i, i ^ 1) for i in rang...  4.7 us
    slice x2, local copies, waits for them, and re-layouts, per_device(): first = jnp.concatenate([low[:, :, 0], cot[:, :, 0]], axis=0)  2.39 us
  transfers between devices with their start and end apart: 18, of which 13 were waited for; matrix products, arithmetic and copies ran while one was open for 5% of the time, Pallas kernels for 6%

profile of v2, /device:TPU:1, one launch (start us, length us, event | category | flops | bytes accessed | tf_op | source)
XLA Modules:
  0.0 106.9 jit_solution(5861615812011271615)
XLA Ops:
  0.6 1.3 %fusion.33 = (bf16[32,6,1,128]{3,2,1,0:T(2,128)(2,1)S(1)}, bf16[32,6,1,128]{3,2,1,0:T(2,128)(2,1)S(1)}) fusion(bf16[32,6,32,128]{3,2,1,0:T(8,128)(2,1)} %bitcast.90), kind=kLoop, calls=%fused_computation.125 | loop fusion | bytes 196608 | tf_op jit(solution)/shard_map/slice | solution.py:337
  1.9 1.1 %fusion.34 = (bf16[16,6,1,128]{3,2,1,0:T(2,128)(2,1)S(1)}, bf16[16,6,1,128]{3,2,1,0:T(2,128)(2,1)S(1)}) fusion(bf16[16,6,16,128]{3,2,1,0:T(8,128)(2,1)} %bitcast.93), kind=kLoop, calls=%fused_computation.126 | loop fusion | bytes 98304 | tf_op jit(solution)/shard_map/slice | solution.py:337
  3.1 4.6 %collective-permute-start.1 = (bf16[48,6,128]{2,0,1:T(8,128)(2,1)S(1)}, bf16[48,6,128]{2,0,1:T(8,128)(2,1)S(1)}, u32[]{:S(2)}, u32[]{:S(2)}) collective-permute-start(bf16[48,6,128]{2,0,1:T(8,128)(2,1)S(1)} %get-tuple-element.50), channel_id=1, source_target_pairs={{1,2},{2,1},{3,4},{4,3},{5,6},{6,5},{7,8},{8,7},{9,10},{10,9},{11,... | collective-permute-start | bytes 221192 | tf_op jit(solution)/shard_map/ppermute | solution.py:272
  7.8 0.8 slice_bitcast_fusion.2
  8.7 0.8 slice_bitcast_fusion.6
  11.0 4.6 %collective-permute-start.2 = (bf16[6,52,128]{2,1,0:T(8,128)(2,1)S(1)}, bf16[6,52,128]{2,1,0:T(8,128)(2,1)S(1)}, u32[]{:S(2)}, u32[]{:S(2)}) collective-permute-start(bf16[6,52,128]{2,1,0:T(8,128)(2,1)S(1)} %get-tuple-element.47), channel_id=1, source_target_pairs={{0,16},{16,0},{32,48},{48,32},{64,80},{80,64},{96,112},{112,96},{1... | collective-permute-start | bytes 239624 | tf_op jit(solution)/shard_map/ppermute | solution.py:271
  16.9 1.1 %collective-permute-done.2 = bf16[6,52,128]{2,1,0:T(8,128)(2,1)S(1)} collective-permute-done((bf16[6,52,128]{2,1,0:T(8,128)(2,1)S(1)}, bf16[6,52,128]{2,1,0:T(8,128)(2,1)S(1)}, u32[]{:S(2)}, u32[]{:S(2)}) %collective-permute-start.2) | collective-permute-done | bytes 79904 | tf_op jit(solution)/shard_map/ppermute | solution.py:271
  18.8 12.3 %forward.1 = (bf16[16,2,6,32,128]{4,3,2,1,0:T(8,128)(2,1)}, bf16[2,17,2,6,16,128]{5,4,3,2,1,0:T(8,128)(2,1)}, f32[2048,128]{1,0:T(8,128)}, bf16[2064,128]{1,0:T(...) custom-call(s32[1]{0:T(128)} %bitcast.upper, bf16[16,6,16,128]{3,2,1,0:T(8,128)(2,1)} %bitcast.95, ...), custom_call_target="tpu_custom_call" | custom-call | flops 12884901888 | bytes 8388608 | tf_op jit(solution)/shard_map/forward/pallas_call | solution.py:149
  31.1 1.1 %collective-permute-start.4 = (bf16[2064,128]{1,0:T(8,128)(2,1)}, bf16[2064,128]{1,0:T(8,128)(2,1)S(1)}, u32[]{:S(2)}, u32[]{:S(2)}) collective-permute-start(bf16[2064,128]{1,0:T(8,128)(2,1)} %get-tuple-element.14), channel_id=1, source_target_pairs={{0,1},{1,0},{2,3},{3,2},{4,5},{5,4},{6,7},{7,6},{8,9},{9,8},{10,11... | collective-permute-start | bytes 1585160 | tf_op jit(solution)/shard_map/ppermute | solution.py:281
  32.2 1.7 %collective-permute-done.4 = bf16[2064,128]{1,0:T(8,128)(2,1)S(1)} collective-permute-done((bf16[2064,128]{1,0:T(8,128)(2,1)}, bf16[2064,128]{1,0:T(8,128)(2,1)S(1)}, u32[]{:S(2)}, u32[]{:S(2)}) %collective-permute-start.4) | collective-permute-done | bytes 528416 | tf_op jit(solution)/shard_map/ppermute | solution.py:281
  35.0 2.3 %collective-permute-start.5 = (bf16[1040,128]{1,0:T(8,128)(2,1)S(1)}, bf16[1040,128]{1,0:T(8,128)(2,1)S(1)}, u32[]{:S(2)}, u32[]{:S(2)}) collective-permute-start(bf16[1040,128]{1,0:T(8,128)(2,1)S(1)} %pad_maximum_fusion.1), channel_id=1, source_target_pairs={{0,4},{1,5},{2,6},{3,7},{4,0},{5,1},{6,2},{7,3},{8,12},{9,13},{10,... | collective-permute-start | bytes 798728 | tf_op jit(solution)/shard_map/ppermute | solution.py:281
  37.3 0.9 fusion.36
  38.2 5.5 %collective-permute-done.5 = bf16[1040,128]{1,0:T(8,128)(2,1)S(1)} collective-permute-done((bf16[1040,128]{1,0:T(8,128)(2,1)S(1)}, bf16[1040,128]{1,0:T(8,128)(2,1)S(1)}, u32[]{:S(2)}, u32[]{:S(2)}) %collective-permute-start.5) | collective-permute-done | bytes 266272 | tf_op jit(solution)/shard_map/ppermute | solution.py:281
  43.9 1.1 %collective-permute-start.6 = (bf16[528,128]{1,0:T(8,128)(2,1)S(1)}, bf16[528,128]{1,0:T(8,128)(2,1)S(1)}, u32[]{:S(2)}, u32[]{:S(2)}) collective-permute-start(bf16[528,128]{1,0:T(8,128)(2,1)S(1)} %pad_maximum_fusion.3), channel_id=1, source_target_pairs={{0,2},{1,3},{2,0},{3,1},{4,6},{5,7},{6,4},{7,5},{8,10},{9,11},{10,... | collective-permute-start | bytes 405512 | tf_op jit(solution)/shard_map/ppermute | solution.py:281
  45.0 0.9 fusion.35
  45.9 2.3 %collective-permute-done.6 = bf16[528,128]{1,0:T(8,128)(2,1)S(1)} collective-permute-done((bf16[528,128]{1,0:T(8,128)(2,1)S(1)}, bf16[528,128]{1,0:T(8,128)(2,1)S(1)}, u32[]{:S(2)}, u32[]{:S(2)}) %collective-permute-start.6) | collective-permute-done | bytes 135200 | tf_op jit(solution)/shard_map/ppermute | solution.py:281
  48.4 2.5 %collective-permute-start.7 = (bf16[272,128]{1,0:T(8,128)(2,1)S(1)}, bf16[272,128]{1,0:T(8,128)(2,1)S(1)}, u32[]{:S(2)}, u32[]{:S(2)}) collective-permute-start(bf16[272,128]{1,0:T(8,128)(2,1)S(1)} %pad_maximum_fusion.7), channel_id=1, source_target_pairs={{0,8},{1,9},{2,10},{3,11},{4,12},{5,13},{6,14},{7,15},{8,0},{9,1},... | collective-permute-start | bytes 208904 | tf_op jit(solution)/shard_map/ppermute | solution.py:281
  50.9 2.3 %collective-permute-done.7 = bf16[272,128]{1,0:T(8,128)(2,1)S(1)} collective-permute-done((bf16[272,128]{1,0:T(8,128)(2,1)S(1)}, bf16[272,128]{1,0:T(8,128)(2,1)S(1)}, u32[]{:S(2)}, u32[]{:S(2)}) %collective-permute-start.7) | collective-permute-done | bytes 69664 | tf_op jit(solution)/shard_map/ppermute | solution.py:281
  53.2 6.4 %collective-permute-start.10 = (bf16[272,128]{1,0:T(8,128)(2,1)S(1)}, bf16[272,128]{1,0:T(8,128)(2,1)S(1)}, u32[]{:S(2)}, u32[]{:S(2)}) collective-permute-start(bf16[272,128]{1,0:T(8,128)(2,1)S(1)} %pad_maximum_fusion.8), channel_id=1, source_target_pairs={{0,144},{16,128},{32,176},{48,160},{64,208},{80,192},{96,240},{112... | collective-permute-start | bytes 208904 | tf_op jit(solution)/shard_map/ppermute | solution.py:281
  60.1 1.1 %collective-permute-start.8 = (bf16[272,128]{1,0:T(8,128)(2,1)S(1)}, bf16[272,128]{1,0:T(8,128)(2,1)S(1)}, u32[]{:S(2)}, u32[]{:S(2)}) collective-permute-start(bf16[272,128]{1,0:T(8,128)(2,1)S(1)} %pad_maximum_fusion.8), channel_id=1, source_target_pairs={{0,16},{16,0},{32,48},{48,32},{64,80},{80,64},{96,112},{112,96},{1... | collective-permute-start | bytes 208904 | tf_op jit(solution)/shard_map/ppermute | solution.py:281
  61.4 3.7 %collective-permute-done.9 = bf16[272,128]{1,0:T(8,128)(2,1)S(1)} collective-permute-done((bf16[272,128]{1,0:T(8,128)(2,1)S(1)}, bf16[272,128]{1,0:T(8,128)(2,1)S(1)}, u32[]{:S(2)}, u32[]{:S(2)}) %collective-permute-start.9) | collective-permute-done | bytes 69664 | tf_op jit(solution)/shard_map/ppermute | solution.py:281
  65.2 2.0 %collective-permute-start.13 = (bf16[272,128]{1,0:T(8,128)(2,1)S(1)}, bf16[272,128]{1,0:T(8,128)(2,1)S(1)}, u32[]{:S(2)}, u32[]{:S(2)}) collective-permute-start(bf16[272,128]{1,0:T(8,128)(2,1)S(1)} %pad_maximum_fusion.9), channel_id=1, source_target_pairs={{0,112},{16,96},{32,80},{48,64},{64,48},{80,32},{96,16},{112,0},{1... | collective-permute-start | bytes 208904 | tf_op jit(solution)/shard_map/ppermute | solution.py:281
  67.2 3.6 %collective-permute-start.12 = (bf16[272,128]{1,0:T(8,128)(2,1)S(1)}, bf16[272,128]{1,0:T(8,128)(2,1)S(1)}, u32[]{:S(2)}, u32[]{:S(2)}) collective-permute-start(bf16[272,128]{1,0:T(8,128)(2,1)S(1)} %pad_maximum_fusion.9), channel_id=1, source_target_pairs={{0,80},{16,64},{32,112},{48,96},{64,16},{80,0},{96,48},{112,32},{1... | collective-permute-start | bytes 208904 | tf_op jit(solution)/shard_map/ppermute | solution.py:281
  70.9 2.5 %collective-permute-done.12 = bf16[272,128]{1,0:T(8,128)(2,1)S(1)} collective-permute-done((bf16[272,128]{1,0:T(8,128)(2,1)S(1)}, bf16[272,128]{1,0:T(8,128)(2,1)S(1)}, u32[]{:S(2)}, u32[]{:S(2)}) %collective-permute-start.12) | collective-permute-done | bytes 69664 | tf_op jit(solution)/shard_map/ppermute | solution.py:281
  73.4 1.5 %collective-permute-done.11 = bf16[272,128]{1,0:T(8,128)(2,1)S(1)} collective-permute-done((bf16[272,128]{1,0:T(8,128)(2,1)S(1)}, bf16[272,128]{1,0:T(8,128)(2,1)S(1)}, u32[]{:S(2)}, u32[]{:S(2)}) %collective-permute-start.11) | collective-permute-done | bytes 69664 | tf_op jit(solution)/shard_map/ppermute | solution.py:281
  74.9 2.1 %collective-permute-start.14 = (bf16[256,128]{1,0:T(8,128)(2,1)S(1)}, bf16[256,128]{1,0:T(8,128)(2,1)S(1)}, u32[]{:S(2)}, u32[]{:S(2)}) collective-permute-start(bf16[256,128]{1,0:T(8,128)(2,1)S(1)} %fusion.9), channel_id=1, source_target_pairs={{0,8},{1,9},{2,10},{3,11},{4,12},{5,13},{6,14},{7,15},{8,0},{9,1},... | collective-permute-start | bytes 196616 | tf_op jit(solution)/shard_map/ppermute | solution.py:281
  77.0 2.6 %collective-permute-done.14 = bf16[256,128]{1,0:T(8,128)(2,1)S(1)} collective-permute-done((bf16[256,128]{1,0:T(8,128)(2,1)S(1)}, bf16[256,128]{1,0:T(8,128)(2,1)S(1)}, u32[]{:S(2)}, u32[]{:S(2)}) %collective-permute-start.14) | collective-permute-done | bytes 65568 | tf_op jit(solution)/shard_map/ppermute | solution.py:281
  80.0 3.6 %collective-permute-done.15 = bf16[512,128]{1,0:T(8,128)(2,1)S(1)} collective-permute-done((bf16[512,128]{1,0:T(8,128)(2,1)S(1)}, bf16[512,128]{1,0:T(8,128)(2,1)S(1)}, u32[]{:S(2)}, u32[]{:S(2)}) %collective-permute-start.15) | collective-permute-done | bytes 131104 | tf_op jit(solution)/shard_map/ppermute | solution.py:281
  84.4 4.6 %collective-permute-done.16 = bf16[1024,128]{1,0:T(8,128)(2,1)S(1)} collective-permute-done((bf16[1024,128]{1,0:T(8,128)(2,1)S(1)}, bf16[1024,128]{1,0:T(8,128)(2,1)S(1)}, u32[]{:S(2)}, u32[]{:S(2)}) %collective-permute-start.16) | collective-permute-done | bytes 262176 | tf_op jit(solution)/shard_map/ppermute | solution.py:281
  89.2 8.9 %collective-permute-start.17 = (bf16[2048,128]{1,0:T(8,128)(2,1)S(1)}, bf16[2048,128]{1,0:T(8,128)(2,1)S(1)}, u32[]{:S(2)}, u32[]{:S(2)}) collective-permute-start(bf16[2048,128]{1,0:T(8,128)(2,1)S(1)} %pad_maximum_fusion), channel_id=1, source_target_pairs={{0,1},{1,0},{2,3},{3,2},{4,5},{5,4},{6,7},{7,6},{8,9},{9,8},{10,11... | collective-permute-start | bytes 1572872 | tf_op jit(solution)/shard_map/ppermute | solution.py:281
  98.0 6.5 %backward.1 = bf16[16,6,16,128]{3,2,1,0:T(8,128)(2,1)} custom-call(bf16[2,17,2,6,16,128]{5,4,3,2,1,0:T(8,128)(2,1)S(1)} %copy-done.2, f32[4,8,32,128]{3,2,1,0:T(8,128)S(1)} %fusion.2.cols, f32[2,2,6,24,128]{4,3,2,1,0:T(8,128)S(1)} %pad_convert_fusion.ccols, bf16[4,4,4,64,128]{4,3,2,1,0:T(8,128)(2,1)S(1)} %copy-done, f32[1,64]{1,0:T(1,128)S(1)} %bitcast.88, ...), custom_call_target="tpu_custom_call" | custom-call | flops 4294967296 | bytes 4194304 | tf_op jit(solution)/shard_map/backward/pallas_call | solution.py:251
  105.4 1.5 %convert_multiply_fusion = f32[4096,128]{1,0:T(8,128)} fusion(bf16[2048,128]{1,0:T(8,128)(2,1)S(1)} %get-tuple-element.35, bf16[2048,128]{1,0:T(8,128)(2,1)S(1)} %get-tuple-element.34), kind=kLoop, calls=%fused_computation | loop fusion | flops 2621440 | bytes 3145728 | tf_op jit(solution)/shard_map/div | solution.py:365
  (107 shorter events, 8.0 us)
Async XLA Ops:
  3.1 6.6 %collective-permute-start.1 = (bf16[48,6,128]{2,0,1:T(8,128)(2,1)S(1)}, bf16[48,6,128]{2,0,1:T(8,128)(2,1)S(1)}, u32[]{:S(2)}, u32[]{:S(2)}) collective-permute-start(bf16[48,6,128]{2,0,1:T(8,128)(2,1)S(1)} %get-tuple-element.50), channel_id=1, source_target_pairs={{1,2},{2,1},{3,4},{4,3},{5,6},{6,5},{7,8},{8,7},{9,10},{10,9},{11,... | collective-permute-start | bytes 221192 | tf_op jit(solution)/shard_map/ppermute | solution.py:272
  7.7 2.0 %collective-permute-start = (bf16[48,6,128]{2,0,1:T(8,128)(2,1)S(1)}, bf16[48,6,128]{2,0,1:T(8,128)(2,1)S(1)}, u32[]{:S(2)}, u32[]{:S(2)}) collective-permute-start(bf16[48,6,128]{2,0,1:T(8,128)(2,1)S(1)} %get-tuple-element.51), channel_id=1, source_target_pairs={{0,1},{1,0},{2,3},{3,2},{4,5},{5,4},{6,7},{7,6},{8,9},{9,8},{10,11... | collective-permute-start | bytes 221192 | tf_op jit(solution)/shard_map/ppermute | solution.py:271
  10.3 6.6 %collective-permute-start.3 = (bf16[6,52,128]{2,1,0:T(8,128)(2,1)S(1)}, bf16[6,52,128]{2,1,0:T(8,128)(2,1)S(1)}, u32[]{:S(2)}, u32[]{:S(2)}) collective-permute-start(bf16[6,52,128]{2,1,0:T(8,128)(2,1)S(1)} %get-tuple-element.46), channel_id=1, source_target_pairs={{16,32},{32,16},{48,64},{64,48},{80,96},{96,80},{112,128},{128,112... | collective-permute-start | bytes 239624 | tf_op jit(solution)/shard_map/ppermute | solution.py:272
  11.0 7.1 %collective-permute-start.2 = (bf16[6,52,128]{2,1,0:T(8,128)(2,1)S(1)}, bf16[6,52,128]{2,1,0:T(8,128)(2,1)S(1)}, u32[]{:S(2)}, u32[]{:S(2)}) collective-permute-start(bf16[6,52,128]{2,1,0:T(8,128)(2,1)S(1)} %get-tuple-element.47), channel_id=1, source_target_pairs={{0,16},{16,0},{32,48},{48,32},{64,80},{80,64},{96,112},{112,96},{1... | collective-permute-start | bytes 239624 | tf_op jit(solution)/shard_map/ppermute | solution.py:271
  31.1 3.6 %copy-start.4 = (f32[2048,128]{1,0:T(8,128)S(1)}, f32[2048,128]{1,0:T(8,128)}, u32[]{:S(2)}) copy-start(f32[2048,128]{1,0:T(8,128)} %get-tuple-element.13) | copy-start | bytes 3145732
  31.1 2.9 %collective-permute-start.4 = (bf16[2064,128]{1,0:T(8,128)(2,1)}, bf16[2064,128]{1,0:T(8,128)(2,1)S(1)}, u32[]{:S(2)}, u32[]{:S(2)}) collective-permute-start(bf16[2064,128]{1,0:T(8,128)(2,1)} %get-tuple-element.14), channel_id=1, source_target_pairs={{0,1},{1,0},{2,3},{3,2},{4,5},{5,4},{6,7},{7,6},{8,9},{9,8},{10,11... | collective-permute-start | bytes 1585160 | tf_op jit(solution)/shard_map/ppermute | solution.py:281
  35.0 8.7 %collective-permute-start.5 = (bf16[1040,128]{1,0:T(8,128)(2,1)S(1)}, bf16[1040,128]{1,0:T(8,128)(2,1)S(1)}, u32[]{:S(2)}, u32[]{:S(2)}) collective-permute-start(bf16[1040,128]{1,0:T(8,128)(2,1)S(1)} %pad_maximum_fusion.1), channel_id=1, source_target_pairs={{0,4},{1,5},{2,6},{3,7},{4,0},{5,1},{6,2},{7,3},{8,12},{9,13},{10,... | collective-permute-start | bytes 798728 | tf_op jit(solution)/shard_map/ppermute | solution.py:281
  43.9 4.3 %collective-permute-start.6 = (bf16[528,128]{1,0:T(8,128)(2,1)S(1)}, bf16[528,128]{1,0:T(8,128)(2,1)S(1)}, u32[]{:S(2)}, u32[]{:S(2)}) collective-permute-start(bf16[528,128]{1,0:T(8,128)(2,1)S(1)} %pad_maximum_fusion.3), channel_id=1, source_target_pairs={{0,2},{1,3},{2,0},{3,1},{4,6},{5,7},{6,4},{7,5},{8,10},{9,11},{10,... | collective-permute-start | bytes 405512 | tf_op jit(solution)/shard_map/ppermute | solution.py:281
  48.4 4.8 %collective-permute-start.7 = (bf16[272,128]{1,0:T(8,128)(2,1)S(1)}, bf16[272,128]{1,0:T(8,128)(2,1)S(1)}, u32[]{:S(2)}, u32[]{:S(2)}) collective-permute-start(bf16[272,128]{1,0:T(8,128)(2,1)S(1)} %pad_maximum_fusion.7), channel_id=1, source_target_pairs={{0,8},{1,9},{2,10},{3,11},{4,12},{5,13},{6,14},{7,15},{8,0},{9,1},... | collective-permute-start | bytes 208904 | tf_op jit(solution)/shard_map/ppermute | solution.py:281
  53.2 8.1 %collective-permute-start.10 = (bf16[272,128]{1,0:T(8,128)(2,1)S(1)}, bf16[272,128]{1,0:T(8,128)(2,1)S(1)}, u32[]{:S(2)}, u32[]{:S(2)}) collective-permute-start(bf16[272,128]{1,0:T(8,128)(2,1)S(1)} %pad_maximum_fusion.8), channel_id=1, source_target_pairs={{0,144},{16,128},{32,176},{48,160},{64,208},{80,192},{96,240},{112... | collective-permute-start | bytes 208904 | tf_op jit(solution)/shard_map/ppermute | solution.py:281
  59.7 5.4 %collective-permute-start.9 = (bf16[272,128]{1,0:T(8,128)(2,1)S(1)}, bf16[272,128]{1,0:T(8,128)(2,1)S(1)}, u32[]{:S(2)}, u32[]{:S(2)}) collective-permute-start(bf16[272,128]{1,0:T(8,128)(2,1)S(1)} %pad_maximum_fusion.8), channel_id=1, source_target_pairs={{0,128},{16,144},{32,160},{48,176},{64,192},{80,208},{96,224},{112... | collective-permute-start | bytes 208904 | tf_op jit(solution)/shard_map/ppermute | solution.py:281
  60.1 4.9 %collective-permute-start.8 = (bf16[272,128]{1,0:T(8,128)(2,1)S(1)}, bf16[272,128]{1,0:T(8,128)(2,1)S(1)}, u32[]{:S(2)}, u32[]{:S(2)}) collective-permute-start(bf16[272,128]{1,0:T(8,128)(2,1)S(1)} %pad_maximum_fusion.8), channel_id=1, source_target_pairs={{0,16},{16,0},{32,48},{48,32},{64,80},{80,64},{96,112},{112,96},{1... | collective-permute-start | bytes 208904 | tf_op jit(solution)/shard_map/ppermute | solution.py:281
  65.2 5.6 %collective-permute-start.13 = (bf16[272,128]{1,0:T(8,128)(2,1)S(1)}, bf16[272,128]{1,0:T(8,128)(2,1)S(1)}, u32[]{:S(2)}, u32[]{:S(2)}) collective-permute-start(bf16[272,128]{1,0:T(8,128)(2,1)S(1)} %pad_maximum_fusion.9), channel_id=1, source_target_pairs={{0,112},{16,96},{32,80},{48,64},{64,48},{80,32},{96,16},{112,0},{1... | collective-permute-start | bytes 208904 | tf_op jit(solution)/shard_map/ppermute | solution.py:281
  67.2 6.2 %collective-permute-start.12 = (bf16[272,128]{1,0:T(8,128)(2,1)S(1)}, bf16[272,128]{1,0:T(8,128)(2,1)S(1)}, u32[]{:S(2)}, u32[]{:S(2)}) collective-permute-start(bf16[272,128]{1,0:T(8,128)(2,1)S(1)} %pad_maximum_fusion.9), channel_id=1, source_target_pairs={{0,80},{16,64},{32,112},{48,96},{64,16},{80,0},{96,48},{112,32},{1... | collective-permute-start | bytes 208904 | tf_op jit(solution)/shard_map/ppermute | solution.py:281
  70.8 4.1 %collective-permute-start.11 = (bf16[272,128]{1,0:T(8,128)(2,1)S(1)}, bf16[272,128]{1,0:T(8,128)(2,1)S(1)}, u32[]{:S(2)}, u32[]{:S(2)}) collective-permute-start(bf16[272,128]{1,0:T(8,128)(2,1)S(1)} %pad_maximum_fusion.9), channel_id=1, source_target_pairs={{0,32},{16,48},{32,0},{48,16},{64,96},{80,112},{96,64},{112,80},{1... | collective-permute-start | bytes 208904 | tf_op jit(solution)/shard_map/ppermute | solution.py:281
  74.9 4.7 %collective-permute-start.14 = (bf16[256,128]{1,0:T(8,128)(2,1)S(1)}, bf16[256,128]{1,0:T(8,128)(2,1)S(1)}, u32[]{:S(2)}, u32[]{:S(2)}) collective-permute-start(bf16[256,128]{1,0:T(8,128)(2,1)S(1)} %fusion.9), channel_id=1, source_target_pairs={{0,8},{1,9},{2,10},{3,11},{4,12},{5,13},{6,14},{7,15},{8,0},{9,1},... | collective-permute-start | bytes 196616 | tf_op jit(solution)/shard_map/ppermute | solution.py:281
  79.7 3.9 %collective-permute-start.15 = (bf16[512,128]{1,0:T(8,128)(2,1)S(1)}, bf16[512,128]{1,0:T(8,128)(2,1)S(1)}, u32[]{:S(2)}, u32[]{:S(2)}) collective-permute-start(bf16[512,128]{1,0:T(8,128)(2,1)S(1)} %pad_maximum_fusion.4), channel_id=1, source_target_pairs={{0,2},{1,3},{2,0},{3,1},{4,6},{5,7},{6,4},{7,5},{8,10},{9,11},{10,... | collective-permute-start | bytes 393224 | tf_op jit(solution)/shard_map/ppermute | solution.py:281
  83.6 14.5 %copy-start.3 = (bf16[2,256,1536]{2,1,0:T(8,128)(2,1)S(1)}, bf16[2,256,1536]{2,1,0:T(8,128)(2,1)}, u32[]{:S(2)}) copy-start(bf16[2,256,1536]{2,1,0:T(8,128)(2,1)} %get-tuple-element.12.wt) | copy-start | bytes 4718596
  83.7 14.4 %copy-start = (bf16[4,4,4,64,128]{4,3,2,1,0:T(8,128)(2,1)S(1)}, bf16[4,4,4,64,128]{4,3,2,1,0:T(8,128)(2,1)}, u32[]{:S(2)}) copy-start(bf16[4,4,4,64,128]{4,3,2,1,0:T(8,128)(2,1)} %kern.1) | copy-start | bytes 3145732
  83.7 14.4 %copy-start.1 = (f32[64]{0:T(128)S(1)}, f32[64]{0:T(128)}, u32[]{:S(2)}) copy-start(f32[64]{0:T(128)} %param.6) | copy-start | bytes 772
  83.7 14.4 %copy-start.2 = (bf16[2,17,2,6,16,128]{5,4,3,2,1,0:T(8,128)(2,1)S(1)}, bf16[2,17,2,6,16,128]{5,4,3,2,1,0:T(8,128)(2,1)}, u32[]{:S(2)}) copy-start(bf16[2,17,2,6,16,128]{5,4,3,2,1,0:T(8,128)(2,1)} %get-tuple-element.11.dpre) | copy-start | bytes 5013508
  83.7 5.3 %collective-permute-start.16 = (bf16[1024,128]{1,0:T(8,128)(2,1)S(1)}, bf16[1024,128]{1,0:T(8,128)(2,1)S(1)}, u32[]{:S(2)}, u32[]{:S(2)}) collective-permute-start(bf16[1024,128]{1,0:T(8,128)(2,1)S(1)} %pad_maximum_fusion.2), channel_id=1, source_target_pairs={{0,4},{1,5},{2,6},{3,7},{4,0},{5,1},{6,2},{7,3},{8,12},{9,13},{10,... | collective-permute-start | bytes 786440 | tf_op jit(solution)/shard_map/ppermute | solution.py:281
  89.2 16.1 %collective-permute-start.17 = (bf16[2048,128]{1,0:T(8,128)(2,1)S(1)}, bf16[2048,128]{1,0:T(8,128)(2,1)S(1)}, u32[]{:S(2)}, u32[]{:S(2)}) collective-permute-start(bf16[2048,128]{1,0:T(8,128)(2,1)S(1)} %pad_maximum_fusion), channel_id=1, source_target_pairs={{0,1},{1,0},{2,3},{3,2},{4,5},{5,4},{6,7},{7,6},{8,9},{9,8},{10,11... | collective-permute-start | bytes 1572872 | tf_op jit(solution)/shard_map/ppermute | solution.py:281

commit v3 on v2

--- a/solution.py
+++ b/solution.py
@@ -20,34 +20,8 @@
     return lax.dot_general(a, b, (((1,), (1,)), ((), ())), preferred_element_type=F32)
 
 
-def forward_body(upper, low, ylo, yhi, xlo, xhi, kern_in, bias, cot_in, out_to, dpre_to, keep, give, bgrad, wt_to, xf, xs, im, c32, o32, ch32, dd, ddt, kgrad, kern, cot, out, dpre, wt, sems):
-    get_kern = pltpu.make_async_copy(kern_in, kern, sems.at[0])
-    get_kern.start()
-    get_cot = pltpu.make_async_copy(cot_in, cot, sems.at[1])
-    get_cot.start()
-    nx, nz, ny, ch = low.shape
-    half = ch // 2
-    rows = (nx + 1) * ny
-    total = rows * nz
-
-    for z in range(nz):
-        xf[z, pl.ds(1, nx), 8:8 + ny, :] = low[:, z].astype(F32)
-        xf[z, 0, 7:9 + ny, :] = xlo[z, 2 * ny:3 * ny + 2].astype(F32)
-        xf[z, nx + 1, 7:9 + ny, :] = xhi[z, 2 * ny:3 * ny + 2].astype(F32)
-    for x in range(nx):
-        xf[:, 1 + x, 7, :] = ylo[x].astype(F32)
-        xf[:, 1 + x, 8 + ny, :] = yhi[x].astype(F32)
-    xs[:, 0] = jnp.zeros(xs.shape[:1] + xs.shape[2:], BF16)
-    xs[:, nz + 1] = jnp.zeros(xs.shape[:1] + xs.shape[2:], BF16)
-
-    def shift_step(z, carry):
-        for s in range(3):
-            xs[s, 1 + z] = xf[z, :, 7 + s:7 + s + ny, :].astype(BF16)
-        return carry
-
-    lax.fori_loop(0, nz, shift_step, 0)
-
-    get_kern.wait()
+def build_weights(kern, wt):
+    half, ch = kern.shape[3:]
     for py in range(2):
         for px in range(2):
             for c in range(2):
@@ -60,8 +34,36 @@
                             block = jnp.zeros((half, ch), BF16) if tz is None else kern[TAP_X[px][ux], TAP_Y[py][vy], tz]
                             wt[py, row:row + half, col:col + ch] = block
 
-    put_wt = pltpu.make_async_copy(wt, wt_to, sems.at[2])
-    put_wt.start()
+
+def forward_body(upper, low, ylo, yhi, xlo, xhi, kern_in, bias, cot_in, out_to, dpre_to, keep, give, bgrad, xf, xs, im, c32, o32, ch32, dd, ddt, kgrad, kern, cot, out, dpre, wt, sems):
+    get_kern = pltpu.make_async_copy(kern_in, kern, sems.at[0])
+    get_kern.start()
+    get_cot = pltpu.make_async_copy(cot_in, cot, sems.at[1])
+    get_cot.start()
+    nx, nz, ny, ch = low.shape
+    half = ch // 2
+    rows = (nx + 1) * ny
+    total = rows * nz
+
+    for z in range(nz):
+        xf[z, pl.ds(1, nx), 8:8 + ny, :] = low[:, z].astype(F32)
+        xf[z, 0, 7:9 + ny, :] = xlo[z, 2 * ny:3 * ny + 2].astype(F32)
+        xf[z, nx + 1, 7:9 + ny, :] = xhi[z, 2 * ny:3 * ny + 2].astype(F32)
+    for x in range(nx):
+        xf[:, 1 + x, 7, :] = ylo[x].astype(F32)
+        xf[:, 1 + x, 8 + ny, :] = yhi[x].astype(F32)
+    xs[:, 0] = jnp.zeros(xs.shape[:1] + xs.shape[2:], BF16)
+    xs[:, nz + 1] = jnp.zeros(xs.shape[:1] + xs.shape[2:], BF16)
+
+    def shift_step(z, carry):
+        for s in range(3):
+            xs[s, 1 + z] = xf[z, :, 7 + s:7 + s + ny, :].astype(BF16)
+        return carry
+
+    lax.fori_loop(0, nz, shift_step, 0)
+
+    get_kern.wait()
+    build_weights(kern, wt)
 
     pad = im.shape[1] - total
     im[:, total:, :] = jnp.zeros((2, pad, im.shape[2]), BF16)
@@ -134,7 +136,6 @@
     give[0:taps] = kgrad[1 - mine].astype(BF16)
     for k, extra in enumerate((high, rest)):
         give[taps + 8 * k:taps + 8 * k + 8] = jnp.broadcast_to(extra, (8, ch))
-    put_wt.wait()
     put_out.wait()
     put_dpre.wait()
 
@@ -146,7 +147,7 @@
     pairs = cot.reshape(nx, 2, nz, 2 * ny, ch)
     vmem, stay = pl.BlockSpec(memory_space=pltpu.VMEM), pl.BlockSpec(memory_space=pl.ANY)
     taps = 32 * ch // 2
-    out, dpre, keep, give, bgrad, wt = pl.pallas_call(
+    out, dpre, keep, give, bgrad = pl.pallas_call(
         forward_body,
         out_shape=(
             jax.ShapeDtypeStruct((nx, 2, nz, 2 * ny, ch), BF16),
@@ -154,10 +155,9 @@
             jax.ShapeDtypeStruct((taps, ch), F32),
             jax.ShapeDtypeStruct((taps + 16, ch), BF16),
             jax.ShapeDtypeStruct((8, ch), F32),
-            jax.ShapeDtypeStruct((2, 2 * ch, 12 * ch), BF16),
         ),
         in_specs=[pl.BlockSpec(memory_space=pltpu.SMEM)] + [vmem] * 5 + [stay, vmem, stay],
-        out_specs=(stay, stay, vmem, vmem, vmem, stay),
+        out_specs=(stay, stay, vmem, vmem, vmem),
         scratch_shapes=[
             pltpu.VMEM((nz, nx + 2, ny + 16, ch), F32),
             pltpu.VMEM((3, nz + 2, nx + 2, ny, ch), BF16),
@@ -179,10 +179,11 @@
         cost_estimate=pl.CostEstimate(flops=12 * 2**30, bytes_accessed=8 << 20, transcendentals=0),
         name="forward",
     )(upper, low, ylo, yhi, xlo, xhi, kern, bias_row, pairs)
-    return out.reshape(2 * nx, nz, 2 * ny, ch), dpre, keep, give, bgrad, wt
-
-
-def backward_body(dpre, cols, ccols, kern, bias, wt, grad, df, ds, wb, gh):
+    return out.reshape(2 * nx, nz, 2 * ny, ch), dpre, keep, give, bgrad
+
+
+def backward_body(dpre, cols, ccols, kern, bias, grad, df, ds, wb, gh, wt):
+    build_weights(kern, wt)
     _, duals, _, nz, ny, ch = dpre.shape
     nx = duals - 1
     half = ch // 2
@@ -244,32 +245,34 @@
     lax.fori_loop(0, nz, layer_step, 0)
 
 
-def run_backward(dpre, cols, ccols, kern, bias_row, wt):
+def run_backward(dpre, cols, ccols, kern, bias_row):
     _, duals, _, nz, ny, ch = dpre.shape
     nx = duals - 1
     vmem = pl.BlockSpec(memory_space=pltpu.VMEM)
     return pl.pallas_call(
         backward_body,
         out_shape=jax.ShapeDtypeStruct((nx, nz, ny, ch), BF16),
-        in_specs=[vmem] * 6,
+        in_specs=[vmem] * 5,
         out_specs=vmem,
         scratch_shapes=[
             pltpu.VMEM((2, nx + 1, 2, ny + 16, ch), F32),
             pltpu.VMEM((4, nz + 2, nx + 1, 2, ny, ch), BF16),
             pltpu.VMEM((32 * ch, ch), BF16),
             pltpu.VMEM((2, 2, nz, nx + 8, ch), F32),
+            pltpu.VMEM((2, 2 * ch, 12 * ch), BF16),
         ],
         compiler_params=pltpu.CompilerParams(vmem_limit_bytes=40 << 20),
         cost_estimate=pl.CostEstimate(flops=4 * 2**30, bytes_accessed=4 << 20, transcendentals=0),
         name="backward",
-    )(dpre, cols, ccols, kern, bias_row, wt)
+    )(dpre, cols, ccols, kern, bias_row)
 
 
 def from_both(first, last, axis):
     count = lax.axis_size(axis)
     odd = lax.axis_index(axis) % 2 == 1
     inner = lax.ppermute(jnp.where(odd, first, last), axis, [(i, i ^ 1) for i in range(count)])
-    outer = lax.ppermute(jnp.where(odd, last, first), axis, [(i, i + 1 if i % 2 else i - 1) for i in range(1, count - 1)])
+    other = jnp.where(odd, last, first)
+    outer = lax.ppermute(other, axis, [(i, i + 1 if i % 2 else i - 1) for i in range(1, count - 1)])
     return jnp.where(odd, inner, outer), jnp.where(odd, outer, inner)
 
 
@@ -345,7 +348,7 @@
     xlo, xhi = from_both(row(0, 0), row(nx - 1, 2 * nx - 1), "gx")
     axis, bit = HALVE[0]
     upper = (lax.axis_index(axis) // bit % 2).astype(jnp.int32).reshape(1)
-    out, dpre, keep, give, bgrad, wt = run_forward(upper, low, ylo, yhi, xlo, xhi, kernel, bias_row, cot)
+    out, dpre, keep, give, bgrad = run_forward(upper, low, ylo, yhi, xlo, xhi, kernel, bias_row, cot)
 
     def column(at, middle):
         first, last = xlo[:, at][:, None], xhi[:, at][:, None]
@@ -356,7 +359,7 @@
     ccols = jnp.stack([column(3 * ny + 3, yhi[nx:]), column(3 * ny + 2, ylo[nx:])]).astype(F32)
     ccols = jnp.transpose(ccols.reshape(2, nz, nx + 1, 2, ch), (0, 3, 1, 2, 4))
     ccols = jnp.pad(ccols, ((0, 0), (0, 0), (0, 0), (0, 7), (0, 0)))
-    grad = run_backward(dpre, cols, ccols, kernel, bias_row, wt)
+    grad = run_backward(dpre, cols, ccols, kernel, bias_row)
     kernel_sum, bias_sum = sum_over_devices(keep, give, bgrad)
 
     grid_rows = lax.axis_size("gx") * nx

time: 107 us -> 108 us (level)
  no operation moved by 1% of the time
where the time goes in v3:
time: 108 us; the launch traced here: 107 us
  starting transfers between devices  42.1 us (39%)
  waiting for transfers between devices  31.8 us (29%)
  Pallas kernels  19.1 us (18%)
  local copies, waits for them, and re-layouts  7.98 us (7%)
  other arithmetic  4.92 us (5%)
  between operations  1.18 us (1%)
    ppermute x14, starting transfers between devices, swap(): lax.ppermute(values, axis, [(i, i ^ bits) for i in range(lax.axis_size(ax...  32.2 us
    ppermute x14, waiting for transfers between devices, swap(): lax.ppermute(values, axis, [(i, i ^ bits) for i in range(lax.axis_size(ax...  30.3 us
    pallas_call x1, Pallas kernels, run_forward(): pl.pallas_call(forward_body, out_shape=(jax.ShapeDtypeStruct((nx, 2, nz,...  12.3 us
    pallas_call x1, Pallas kernels, run_backward(): pl.pallas_call(backward_body, out_shape=jax.ShapeDtypeStruct((nx, nz, ny,...  6.73 us
    ppermute x2, starting transfers between devices, from_both(): lax.ppermute(other, axis, [(i, i + 1 if i % 2 else i - 1) for i in range(...  5.25 us
    ppermute x2, starting transfers between devices, from_both(): lax.ppermute(jnp.where(odd, first, last), axis, [(i, i ^ 1) for i in rang...  4.7 us
    slice x2, local copies, waits for them, and re-layouts, per_device(): first = jnp.concatenate([low[:, :, 0], cot[:, :, 0]], axis=0)  2.39 us
  transfers between devices with their start and end apart: 18, of which 13 were waited for; matrix products, arithmetic and copies ran while one was open for 5% of the time, Pallas kernels for 6%

profile of v3, /device:TPU:1, one launch (start us, length us, event | category | flops | bytes accessed | tf_op | source)
XLA Modules:
  0.0 107.1 jit_solution(279312099934881249)
XLA Ops:
  0.6 1.3 %fusion.33 = (bf16[32,6,1,128]{3,2,1,0:T(2,128)(2,1)S(1)}, bf16[32,6,1,128]{3,2,1,0:T(2,128)(2,1)S(1)}) fusion(bf16[32,6,32,128]{3,2,1,0:T(8,128)(2,1)} %bitcast.90), kind=kLoop, calls=%fused_computation.125 | loop fusion | bytes 196608 | tf_op jit(solution)/shard_map/slice | solution.py:340
  1.9 1.1 %fusion.34 = (bf16[16,6,1,128]{3,2,1,0:T(2,128)(2,1)S(1)}, bf16[16,6,1,128]{3,2,1,0:T(2,128)(2,1)S(1)}) fusion(bf16[16,6,16,128]{3,2,1,0:T(8,128)(2,1)} %bitcast.93), kind=kLoop, calls=%fused_computation.126 | loop fusion | bytes 98304 | tf_op jit(solution)/shard_map/slice | solution.py:340
  3.1 4.6 %collective-permute-start.1 = (bf16[48,6,128]{2,0,1:T(8,128)(2,1)S(1)}, bf16[48,6,128]{2,0,1:T(8,128)(2,1)S(1)}, u32[]{:S(2)}, u32[]{:S(2)}) collective-permute-start(bf16[48,6,128]{2,0,1:T(8,128)(2,1)S(1)} %get-tuple-element.48), channel_id=1, source_target_pairs={{1,2},{2,1},{3,4},{4,3},{5,6},{6,5},{7,8},{8,7},{9,10},{10,9},{11,... | collective-permute-start | bytes 221192 | tf_op jit(solution)/shard_map/ppermute | solution.py:275
  7.8 0.8 slice_bitcast_fusion.2
  8.7 0.8 slice_bitcast_fusion.6
  11.0 4.6 %collective-permute-start.2 = (bf16[6,52,128]{2,1,0:T(8,128)(2,1)S(1)}, bf16[6,52,128]{2,1,0:T(8,128)(2,1)S(1)}, u32[]{:S(2)}, u32[]{:S(2)}) collective-permute-start(bf16[6,52,128]{2,1,0:T(8,128)(2,1)S(1)} %get-tuple-element.45), channel_id=1, source_target_pairs={{0,16},{16,0},{32,48},{48,32},{64,80},{80,64},{96,112},{112,96},{1... | collective-permute-start | bytes 239624 | tf_op jit(solution)/shard_map/ppermute | solution.py:273
  16.9 1.1 %collective-permute-done.2 = bf16[6,52,128]{2,1,0:T(8,128)(2,1)S(1)} collective-permute-done((bf16[6,52,128]{2,1,0:T(8,128)(2,1)S(1)}, bf16[6,52,128]{2,1,0:T(8,128)(2,1)S(1)}, u32[]{:S(2)}, u32[]{:S(2)}) %collective-permute-start.2) | collective-permute-done | bytes 79904 | tf_op jit(solution)/shard_map/ppermute | solution.py:273
  18.7 12.3 %forward.1 = (bf16[16,2,6,32,128]{4,3,2,1,0:T(8,128)(2,1)}, bf16[2,17,2,6,16,128]{5,4,3,2,1,0:T(8,128)(2,1)}, f32[2048,128]{1,0:T(8,128)}, bf16[2064,128]{1,0:T(8,128)(2,1)}, f32[8,128]{1,0:T(8,128)}) custom-call(s32[1]{0:T(128)} %bitcast.upper, bf16[16,6,16,128]{3,2,1,0:T(8,128)(2,1)} %bitcast.95, bf16[48,6,128]{2,1,0:T(8,128)(2,1)} %copy.303.ylo, ...), custom_call_target="tpu_custom_call" | custom-call | flops 12884901888 | bytes 8388608 | tf_op jit(solution)/shard_map/forward/pallas_call | solution.py:150
  31.1 1.1 %collective-permute-start.4 = (bf16[2064,128]{1,0:T(8,128)(2,1)}, bf16[2064,128]{1,0:T(8,128)(2,1)S(1)}, u32[]{:S(2)}, u32[]{:S(2)}) collective-permute-start(bf16[2064,128]{1,0:T(8,128)(2,1)} %get-tuple-element.12), channel_id=1, source_target_pairs={{0,1},{1,0},{2,3},{3,2},{4,5},{5,4},{6,7},{7,6},{8,9},{9,8},{10,11... | collective-permute-start | bytes 1585160 | tf_op jit(solution)/shard_map/ppermute | solution.py:284
  32.2 1.7 %collective-permute-done.4 = bf16[2064,128]{1,0:T(8,128)(2,1)S(1)} collective-permute-done((bf16[2064,128]{1,0:T(8,128)(2,1)}, bf16[2064,128]{1,0:T(8,128)(2,1)S(1)}, u32[]{:S(2)}, u32[]{:S(2)}) %collective-permute-start.4) | collective-permute-done | bytes 528416 | tf_op jit(solution)/shard_map/ppermute | solution.py:284
  34.9 2.3 %collective-permute-start.5 = (bf16[1040,128]{1,0:T(8,128)(2,1)S(1)}, bf16[1040,128]{1,0:T(8,128)(2,1)S(1)}, u32[]{:S(2)}, u32[]{:S(2)}) collective-permute-start(bf16[1040,128]{1,0:T(8,128)(2,1)S(1)} %pad_maximum_fusion.1), channel_id=1, source_target_pairs={{0,4},{1,5},{2,6},{3,7},{4,0},{5,1},{6,2},{7,3},{8,12},{9,13},{10,... | collective-permute-start | bytes 798728 | tf_op jit(solution)/shard_map/ppermute | solution.py:284
  37.3 0.9 fusion.36
  38.1 5.5 %collective-permute-done.5 = bf16[1040,128]{1,0:T(8,128)(2,1)S(1)} collective-permute-done((bf16[1040,128]{1,0:T(8,128)(2,1)S(1)}, bf16[1040,128]{1,0:T(8,128)(2,1)S(1)}, u32[]{:S(2)}, u32[]{:S(2)}) %collective-permute-start.5) | collective-permute-done | bytes 266272 | tf_op jit(solution)/shard_map/ppermute | solution.py:284
  43.9 1.1 %collective-permute-start.6 = (bf16[528,128]{1,0:T(8,128)(2,1)S(1)}, bf16[528,128]{1,0:T(8,128)(2,1)S(1)}, u32[]{:S(2)}, u32[]{:S(2)}) collective-permute-start(bf16[528,128]{1,0:T(8,128)(2,1)S(1)} %pad_maximum_fusion.3), channel_id=1, source_target_pairs={{0,2},{1,3},{2,0},{3,1},{4,6},{5,7},{6,4},{7,5},{8,10},{9,11},{10,... | collective-permute-start | bytes 405512 | tf_op jit(solution)/shard_map/ppermute | solution.py:284
  45.0 1.0 fusion.35
  46.0 2.2 %collective-permute-done.6 = bf16[528,128]{1,0:T(8,128)(2,1)S(1)} collective-permute-done((bf16[528,128]{1,0:T(8,128)(2,1)S(1)}, bf16[528,128]{1,0:T(8,128)(2,1)S(1)}, u32[]{:S(2)}, u32[]{:S(2)}) %collective-permute-start.6) | collective-permute-done | bytes 135200 | tf_op jit(solution)/shard_map/ppermute | solution.py:284
  48.3 2.5 %collective-permute-start.7 = (bf16[272,128]{1,0:T(8,128)(2,1)S(1)}, bf16[272,128]{1,0:T(8,128)(2,1)S(1)}, u32[]{:S(2)}, u32[]{:S(2)}) collective-permute-start(bf16[272,128]{1,0:T(8,128)(2,1)S(1)} %pad_maximum_fusion.7), channel_id=1, source_target_pairs={{0,8},{1,9},{2,10},{3,11},{4,12},{5,13},{6,14},{7,15},{8,0},{9,1},... | collective-permute-start | bytes 208904 | tf_op jit(solution)/shard_map/ppermute | solution.py:284
  50.8 2.3 %collective-permute-done.7 = bf16[272,128]{1,0:T(8,128)(2,1)S(1)} collective-permute-done((bf16[272,128]{1,0:T(8,128)(2,1)S(1)}, bf16[272,128]{1,0:T(8,128)(2,1)S(1)}, u32[]{:S(2)}, u32[]{:S(2)}) %collective-permute-start.7) | collective-permute-done | bytes 69664 | tf_op jit(solution)/shard_map/ppermute | solution.py:284
  53.2 6.4 %collective-permute-start.10 = (bf16[272,128]{1,0:T(8,128)(2,1)S(1)}, bf16[272,128]{1,0:T(8,128)(2,1)S(1)}, u32[]{:S(2)}, u32[]{:S(2)}) collective-permute-start(bf16[272,128]{1,0:T(8,128)(2,1)S(1)} %pad_maximum_fusion.8), channel_id=1, source_target_pairs={{0,144},{16,128},{32,176},{48,160},{64,208},{80,192},{96,240},{112... | collective-permute-start | bytes 208904 | tf_op jit(solution)/shard_map/ppermute | solution.py:284
  60.1 1.1 %collective-permute-start.8 = (bf16[272,128]{1,0:T(8,128)(2,1)S(1)}, bf16[272,128]{1,0:T(8,128)(2,1)S(1)}, u32[]{:S(2)}, u32[]{:S(2)}) collective-permute-start(bf16[272,128]{1,0:T(8,128)(2,1)S(1)} %pad_maximum_fusion.8), channel_id=1, source_target_pairs={{0,16},{16,0},{32,48},{48,32},{64,80},{80,64},{96,112},{112,96},{1... | collective-permute-start | bytes 208904 | tf_op jit(solution)/shard_map/ppermute | solution.py:284
  61.3 3.7 %collective-permute-done.9 = bf16[272,128]{1,0:T(8,128)(2,1)S(1)} collective-permute-done((bf16[272,128]{1,0:T(8,128)(2,1)S(1)}, bf16[272,128]{1,0:T(8,128)(2,1)S(1)}, u32[]{:S(2)}, u32[]{:S(2)}) %collective-permute-start.9) | collective-permute-done | bytes 69664 | tf_op jit(solution)/shard_map/ppermute | solution.py:284
  65.2 2.0 %collective-permute-start.13 = (bf16[272,128]{1,0:T(8,128)(2,1)S(1)}, bf16[272,128]{1,0:T(8,128)(2,1)S(1)}, u32[]{:S(2)}, u32[]{:S(2)}) collective-permute-start(bf16[272,128]{1,0:T(8,128)(2,1)S(1)} %pad_maximum_fusion.9), channel_id=1, source_target_pairs={{0,112},{16,96},{32,80},{48,64},{64,48},{80,32},{96,16},{112,0},{1... | collective-permute-start | bytes 208904 | tf_op jit(solution)/shard_map/ppermute | solution.py:284
  67.2 3.6 %collective-permute-start.12 = (bf16[272,128]{1,0:T(8,128)(2,1)S(1)}, bf16[272,128]{1,0:T(8,128)(2,1)S(1)}, u32[]{:S(2)}, u32[]{:S(2)}) collective-permute-start(bf16[272,128]{1,0:T(8,128)(2,1)S(1)} %pad_maximum_fusion.9), channel_id=1, source_target_pairs={{0,80},{16,64},{32,112},{48,96},{64,16},{80,0},{96,48},{112,32},{1... | collective-permute-start | bytes 208904 | tf_op jit(solution)/shard_map/ppermute | solution.py:284
  70.8 2.5 %collective-permute-done.12 = bf16[272,128]{1,0:T(8,128)(2,1)S(1)} collective-permute-done((bf16[272,128]{1,0:T(8,128)(2,1)S(1)}, bf16[272,128]{1,0:T(8,128)(2,1)S(1)}, u32[]{:S(2)}, u32[]{:S(2)}) %collective-permute-start.12) | collective-permute-done | bytes 69664 | tf_op jit(solution)/shard_map/ppermute | solution.py:284
  73.4 1.5 %collective-permute-done.11 = bf16[272,128]{1,0:T(8,128)(2,1)S(1)} collective-permute-done((bf16[272,128]{1,0:T(8,128)(2,1)S(1)}, bf16[272,128]{1,0:T(8,128)(2,1)S(1)}, u32[]{:S(2)}, u32[]{:S(2)}) %collective-permute-start.11) | collective-permute-done | bytes 69664 | tf_op jit(solution)/shard_map/ppermute | solution.py:284
  74.9 2.1 %collective-permute-start.14 = (bf16[256,128]{1,0:T(8,128)(2,1)S(1)}, bf16[256,128]{1,0:T(8,128)(2,1)S(1)}, u32[]{:S(2)}, u32[]{:S(2)}) collective-permute-start(bf16[256,128]{1,0:T(8,128)(2,1)S(1)} %fusion.9), channel_id=1, source_target_pairs={{0,8},{1,9},{2,10},{3,11},{4,12},{5,13},{6,14},{7,15},{8,0},{9,1},... | collective-permute-start | bytes 196616 | tf_op jit(solution)/shard_map/ppermute | solution.py:284
  77.0 2.6 %collective-permute-done.14 = bf16[256,128]{1,0:T(8,128)(2,1)S(1)} collective-permute-done((bf16[256,128]{1,0:T(8,128)(2,1)S(1)}, bf16[256,128]{1,0:T(8,128)(2,1)S(1)}, u32[]{:S(2)}, u32[]{:S(2)}) %collective-permute-start.14) | collective-permute-done | bytes 65568 | tf_op jit(solution)/shard_map/ppermute | solution.py:284
  80.0 3.6 %collective-permute-done.15 = bf16[512,128]{1,0:T(8,128)(2,1)S(1)} collective-permute-done((bf16[512,128]{1,0:T(8,128)(2,1)S(1)}, bf16[512,128]{1,0:T(8,128)(2,1)S(1)}, u32[]{:S(2)}, u32[]{:S(2)}) %collective-permute-start.15) | collective-permute-done | bytes 131104 | tf_op jit(solution)/shard_map/ppermute | solution.py:284
  84.3 4.6 %collective-permute-done.16 = bf16[1024,128]{1,0:T(8,128)(2,1)S(1)} collective-permute-done((bf16[1024,128]{1,0:T(8,128)(2,1)S(1)}, bf16[1024,128]{1,0:T(8,128)(2,1)S(1)}, u32[]{:S(2)}, u32[]{:S(2)}) %collective-permute-start.16) | collective-permute-done | bytes 262176 | tf_op jit(solution)/shard_map/ppermute | solution.py:284
  89.1 8.9 %collective-permute-start.17 = (bf16[2048,128]{1,0:T(8,128)(2,1)S(1)}, bf16[2048,128]{1,0:T(8,128)(2,1)S(1)}, u32[]{:S(2)}, u32[]{:S(2)}) collective-permute-start(bf16[2048,128]{1,0:T(8,128)(2,1)S(1)} %pad_maximum_fusion), channel_id=1, source_target_pairs={{0,1},{1,0},{2,3},{3,2},{4,5},{5,4},{6,7},{7,6},{8,9},{9,8},{10,11... | collective-permute-start | bytes 1572872 | tf_op jit(solution)/shard_map/ppermute | solution.py:284
  98.0 6.7 %backward.1 = bf16[16,6,16,128]{3,2,1,0:T(8,128)(2,1)} custom-call(bf16[2,17,2,6,16,128]{5,4,3,2,1,0:T(8,128)(2,1)S(1)} %copy-done.2, f32[4,8,32,128]{3,2,1,0:T(8,128)S(1)} %fusion.2.cols, f32[2,2,6,24,128]{4,3,2,1,0:T(8,128)S(1)} %pad_convert_fusion.ccols, bf16[4,4,4,64,128]{4,3,2,1,0:T(8,128)(2,1)S(1)} %copy-done, f32[1,64]{1,0:T(1,128)S(1)} %bitcast.88), custom_call_target="tpu_custom_call" | custom-call | flops 4294967296 | bytes 4194304 | tf_op jit(solution)/shard_map/backward/pallas_call | solution.py:252
  105.6 1.5 %convert_multiply_fusion = f32[4096,128]{1,0:T(8,128)} fusion(bf16[2048,128]{1,0:T(8,128)(2,1)S(1)} %get-tuple-element.33, bf16[2048,128]{1,0:T(8,128)(2,1)S(1)} %get-tuple-element.32), kind=kLoop, calls=%fused_computation | loop fusion | flops 2621440 | bytes 3145728 | tf_op jit(solution)/shard_map/div | solution.py:368
  (105 shorter events, 8.0 us)
Async XLA Ops:
  3.1 6.6 %collective-permute-start.1 = (bf16[48,6,128]{2,0,1:T(8,128)(2,1)S(1)}, bf16[48,6,128]{2,0,1:T(8,128)(2,1)S(1)}, u32[]{:S(2)}, u32[]{:S(2)}) collective-permute-start(bf16[48,6,128]{2,0,1:T(8,128)(2,1)S(1)} %get-tuple-element.48), channel_id=1, source_target_pairs={{1,2},{2,1},{3,4},{4,3},{5,6},{6,5},{7,8},{8,7},{9,10},{10,9},{11,... | collective-permute-start | bytes 221192 | tf_op jit(solution)/shard_map/ppermute | solution.py:275
  7.7 2.0 %collective-permute-start = (bf16[48,6,128]{2,0,1:T(8,128)(2,1)S(1)}, bf16[48,6,128]{2,0,1:T(8,128)(2,1)S(1)}, u32[]{:S(2)}, u32[]{:S(2)}) collective-permute-start(bf16[48,6,128]{2,0,1:T(8,128)(2,1)S(1)} %get-tuple-element.49), channel_id=1, source_target_pairs={{0,1},{1,0},{2,3},{3,2},{4,5},{5,4},{6,7},{7,6},{8,9},{9,8},{10,11... | collective-permute-start | bytes 221192 | tf_op jit(solution)/shard_map/ppermute | solution.py:273
  10.3 6.6 %collective-permute-start.3 = (bf16[6,52,128]{2,1,0:T(8,128)(2,1)S(1)}, bf16[6,52,128]{2,1,0:T(8,128)(2,1)S(1)}, u32[]{:S(2)}, u32[]{:S(2)}) collective-permute-start(bf16[6,52,128]{2,1,0:T(8,128)(2,1)S(1)} %get-tuple-element.44), channel_id=1, source_target_pairs={{16,32},{32,16},{48,64},{64,48},{80,96},{96,80},{112,128},{128,112... | collective-permute-start | bytes 239624 | tf_op jit(solution)/shard_map/ppermute | solution.py:275
  11.0 7.1 %collective-permute-start.2 = (bf16[6,52,128]{2,1,0:T(8,128)(2,1)S(1)}, bf16[6,52,128]{2,1,0:T(8,128)(2,1)S(1)}, u32[]{:S(2)}, u32[]{:S(2)}) collective-permute-start(bf16[6,52,128]{2,1,0:T(8,128)(2,1)S(1)} %get-tuple-element.45), channel_id=1, source_target_pairs={{0,16},{16,0},{32,48},{48,32},{64,80},{80,64},{96,112},{112,96},{1... | collective-permute-start | bytes 239624 | tf_op jit(solution)/shard_map/ppermute | solution.py:273
  31.1 3.6 %copy-start.3 = (f32[2048,128]{1,0:T(8,128)S(1)}, f32[2048,128]{1,0:T(8,128)}, u32[]{:S(2)}) copy-start(f32[2048,128]{1,0:T(8,128)} %get-tuple-element.11) | copy-start | bytes 3145732
  31.1 2.9 %collective-permute-start.4 = (bf16[2064,128]{1,0:T(8,128)(2,1)}, bf16[2064,128]{1,0:T(8,128)(2,1)S(1)}, u32[]{:S(2)}, u32[]{:S(2)}) collective-permute-start(bf16[2064,128]{1,0:T(8,128)(2,1)} %get-tuple-element.12), channel_id=1, source_target_pairs={{0,1},{1,0},{2,3},{3,2},{4,5},{5,4},{6,7},{7,6},{8,9},{9,8},{10,11... | collective-permute-start | bytes 1585160 | tf_op jit(solution)/shard_map/ppermute | solution.py:284
  34.9 8.7 %collective-permute-start.5 = (bf16[1040,128]{1,0:T(8,128)(2,1)S(1)}, bf16[1040,128]{1,0:T(8,128)(2,1)S(1)}, u32[]{:S(2)}, u32[]{:S(2)}) collective-permute-start(bf16[1040,128]{1,0:T(8,128)(2,1)S(1)} %pad_maximum_fusion.1), channel_id=1, source_target_pairs={{0,4},{1,5},{2,6},{3,7},{4,0},{5,1},{6,2},{7,3},{8,12},{9,13},{10,... | collective-permute-start | bytes 798728 | tf_op jit(solution)/shard_map/ppermute | solution.py:284
  43.9 4.3 %collective-permute-start.6 = (bf16[528,128]{1,0:T(8,128)(2,1)S(1)}, bf16[528,128]{1,0:T(8,128)(2,1)S(1)}, u32[]{:S(2)}, u32[]{:S(2)}) collective-permute-start(bf16[528,128]{1,0:T(8,128)(2,1)S(1)} %pad_maximum_fusion.3), channel_id=1, source_target_pairs={{0,2},{1,3},{2,0},{3,1},{4,6},{5,7},{6,4},{7,5},{8,10},{9,11},{10,... | collective-permute-start | bytes 405512 | tf_op jit(solution)/shard_map/ppermute | solution.py:284
  48.3 4.8 %collective-permute-start.7 = (bf16[272,128]{1,0:T(8,128)(2,1)S(1)}, bf16[272,128]{1,0:T(8,128)(2,1)S(1)}, u32[]{:S(2)}, u32[]{:S(2)}) collective-permute-start(bf16[272,128]{1,0:T(8,128)(2,1)S(1)} %pad_maximum_fusion.7), channel_id=1, source_target_pairs={{0,8},{1,9},{2,10},{3,11},{4,12},{5,13},{6,14},{7,15},{8,0},{9,1},... | collective-permute-start | bytes 208904 | tf_op jit(solution)/shard_map/ppermute | solution.py:284
  53.2 8.1 %collective-permute-start.10 = (bf16[272,128]{1,0:T(8,128)(2,1)S(1)}, bf16[272,128]{1,0:T(8,128)(2,1)S(1)}, u32[]{:S(2)}, u32[]{:S(2)}) collective-permute-start(bf16[272,128]{1,0:T(8,128)(2,1)S(1)} %pad_maximum_fusion.8), channel_id=1, source_target_pairs={{0,144},{16,128},{32,176},{48,160},{64,208},{80,192},{96,240},{112... | collective-permute-start | bytes 208904 | tf_op jit(solution)/shard_map/ppermute | solution.py:284
  59.6 5.4 %collective-permute-start.9 = (bf16[272,128]{1,0:T(8,128)(2,1)S(1)}, bf16[272,128]{1,0:T(8,128)(2,1)S(1)}, u32[]{:S(2)}, u32[]{:S(2)}) collective-permute-start(bf16[272,128]{1,0:T(8,128)(2,1)S(1)} %pad_maximum_fusion.8), channel_id=1, source_target_pairs={{0,128},{16,144},{32,160},{48,176},{64,192},{80,208},{96,224},{112... | collective-permute-start | bytes 208904 | tf_op jit(solution)/shard_map/ppermute | solution.py:284
  60.1 4.9 %collective-permute-start.8 = (bf16[272,128]{1,0:T(8,128)(2,1)S(1)}, bf16[272,128]{1,0:T(8,128)(2,1)S(1)}, u32[]{:S(2)}, u32[]{:S(2)}) collective-permute-start(bf16[272,128]{1,0:T(8,128)(2,1)S(1)} %pad_maximum_fusion.8), channel_id=1, source_target_pairs={{0,16},{16,0},{32,48},{48,32},{64,80},{80,64},{96,112},{112,96},{1... | collective-permute-start | bytes 208904 | tf_op jit(solution)/shard_map/ppermute | solution.py:284
  65.2 5.6 %collective-permute-start.13 = (bf16[272,128]{1,0:T(8,128)(2,1)S(1)}, bf16[272,128]{1,0:T(8,128)(2,1)S(1)}, u32[]{:S(2)}, u32[]{:S(2)}) collective-permute-start(bf16[272,128]{1,0:T(8,128)(2,1)S(1)} %pad_maximum_fusion.9), channel_id=1, source_target_pairs={{0,112},{16,96},{32,80},{48,64},{64,48},{80,32},{96,16},{112,0},{1... | collective-permute-start | bytes 208904 | tf_op jit(solution)/shard_map/ppermute | solution.py:284
  67.2 6.2 %collective-permute-start.12 = (bf16[272,128]{1,0:T(8,128)(2,1)S(1)}, bf16[272,128]{1,0:T(8,128)(2,1)S(1)}, u32[]{:S(2)}, u32[]{:S(2)}) collective-permute-start(bf16[272,128]{1,0:T(8,128)(2,1)S(1)} %pad_maximum_fusion.9), channel_id=1, source_target_pairs={{0,80},{16,64},{32,112},{48,96},{64,16},{80,0},{96,48},{112,32},{1... | collective-permute-start | bytes 208904 | tf_op jit(solution)/shard_map/ppermute | solution.py:284
  70.8 4.1 %collective-permute-start.11 = (bf16[272,128]{1,0:T(8,128)(2,1)S(1)}, bf16[272,128]{1,0:T(8,128)(2,1)S(1)}, u32[]{:S(2)}, u32[]{:S(2)}) collective-permute-start(bf16[272,128]{1,0:T(8,128)(2,1)S(1)} %pad_maximum_fusion.9), channel_id=1, source_target_pairs={{0,32},{16,48},{32,0},{48,16},{64,96},{80,112},{96,64},{112,80},{1... | collective-permute-start | bytes 208904 | tf_op jit(solution)/shard_map/ppermute | solution.py:284
  74.9 4.7 %collective-permute-start.14 = (bf16[256,128]{1,0:T(8,128)(2,1)S(1)}, bf16[256,128]{1,0:T(8,128)(2,1)S(1)}, u32[]{:S(2)}, u32[]{:S(2)}) collective-permute-start(bf16[256,128]{1,0:T(8,128)(2,1)S(1)} %fusion.9), channel_id=1, source_target_pairs={{0,8},{1,9},{2,10},{3,11},{4,12},{5,13},{6,14},{7,15},{8,0},{9,1},... | collective-permute-start | bytes 196616 | tf_op jit(solution)/shard_map/ppermute | solution.py:284
  79.6 3.9 %collective-permute-start.15 = (bf16[512,128]{1,0:T(8,128)(2,1)S(1)}, bf16[512,128]{1,0:T(8,128)(2,1)S(1)}, u32[]{:S(2)}, u32[]{:S(2)}) collective-permute-start(bf16[512,128]{1,0:T(8,128)(2,1)S(1)} %pad_maximum_fusion.4), channel_id=1, source_target_pairs={{0,2},{1,3},{2,0},{3,1},{4,6},{5,7},{6,4},{7,5},{8,10},{9,11},{10,... | collective-permute-start | bytes 393224 | tf_op jit(solution)/shard_map/ppermute | solution.py:284
  83.6 14.4 %copy-start = (bf16[4,4,4,64,128]{4,3,2,1,0:T(8,128)(2,1)S(1)}, bf16[4,4,4,64,128]{4,3,2,1,0:T(8,128)(2,1)}, u32[]{:S(2)}) copy-start(bf16[4,4,4,64,128]{4,3,2,1,0:T(8,128)(2,1)} %kern.1) | copy-start | bytes 3145732
  83.6 14.4 %copy-start.1 = (f32[64]{0:T(128)S(1)}, f32[64]{0:T(128)}, u32[]{:S(2)}) copy-start(f32[64]{0:T(128)} %param.6) | copy-start | bytes 772
  83.6 14.4 %copy-start.2 = (bf16[2,17,2,6,16,128]{5,4,3,2,1,0:T(8,128)(2,1)S(1)}, bf16[2,17,2,6,16,128]{5,4,3,2,1,0:T(8,128)(2,1)}, u32[]{:S(2)}) copy-start(bf16[2,17,2,6,16,128]{5,4,3,2,1,0:T(8,128)(2,1)} %get-tuple-element.10.dpre) | copy-start | bytes 5013508
  83.7 5.3 %collective-permute-start.16 = (bf16[1024,128]{1,0:T(8,128)(2,1)S(1)}, bf16[1024,128]{1,0:T(8,128)(2,1)S(1)}, u32[]{:S(2)}, u32[]{:S(2)}) collective-permute-start(bf16[1024,128]{1,0:T(8,128)(2,1)S(1)} %pad_maximum_fusion.2), channel_id=1, source_target_pairs={{0,4},{1,5},{2,6},{3,7},{4,0},{5,1},{6,2},{7,3},{8,12},{9,13},{10,... | collective-permute-start | bytes 786440 | tf_op jit(solution)/shard_map/ppermute | solution.py:284
  89.1 16.3 %collective-permute-start.17 = (bf16[2048,128]{1,0:T(8,128)(2,1)S(1)}, bf16[2048,128]{1,0:T(8,128)(2,1)S(1)}, u32[]{:S(2)}, u32[]{:S(2)}) collective-permute-start(bf16[2048,128]{1,0:T(8,128)(2,1)S(1)} %pad_maximum_fusion), channel_id=1, source_target_pairs={{0,1},{1,0},{2,3},{3,2},{4,5},{5,4},{6,7},{7,6},{8,9},{9,8},{10,11... | collective-permute-start | bytes 1572872 | tf_op jit(solution)/shard_map/ppermute | solution.py:284

commit v4 on v3

--- a/solution.py
+++ b/solution.py
@@ -82,7 +82,9 @@
                     for dz in range(3):
                         col = ((ux * 2 + vy) * 3 + dz) * ch
                         im[py, pl.ds(base, rows), col:col + ch] = xs[SHIFT_Y[py][vy], z + dz, ux:ux + nx + 1].reshape(rows, ch)
-            pre = dot_nt(im[py, pl.ds(base, rows), :], wt[py])
+        both = [dot_nt(im[py, pl.ds(base, rows), :], wt[py]) for py in range(2)]
+        for py in range(2):
+            pre = both[py]
             dd[py, pl.ds(base, ny), 0:ch] = jnp.zeros((ny, ch), BF16)
             dd[py, pl.ds(base + nx * ny, ny), ch:2 * ch] = jnp.zeros((ny, ch), BF16)
             for q in range(2):
@@ -105,7 +107,7 @@
         out[:, :, z] = o32[...].astype(BF16)
         return acc
 
-    sums = jnp.sum(lax.fori_loop(0, nz, layer_step, jnp.zeros((8, ch), F32)), axis=0, keepdims=True)
+    sums = jnp.sum(lax.fori_loop(0, nz, layer_step, jnp.zeros((8, ch), F32), unroll=True), axis=0, keepdims=True)
     put_out = pltpu.make_async_copy(out, out_to, sems.at[3])
     put_out.start()
     put_dpre = pltpu.make_async_copy(dpre, dpre_to, sems.at[4])
@@ -217,7 +219,7 @@
                 ds[py * 2 + vy, 1 + z] = df[py, :, :, lead:lead + ny, :].astype(BF16)
         return carry
 
-    lax.fori_loop(0, nz, layer_load, 0)
+    lax.fori_loop(0, nz, layer_load, 0, unroll=2)
     for py in range(2):
         for vy in range(2):
             for q in range(4):
@@ -242,7 +244,7 @@
         grad[:, z] = acc.astype(BF16).reshape(nx, ny, ch)
         return carry
 
-    lax.fori_loop(0, nz, layer_step, 0)
+    lax.fori_loop(0, nz, layer_step, 0, unroll=True)
 
 
 def run_backward(dpre, cols, ccols, kern, bias_row):
@@ -276,8 +278,8 @@
     return jnp.where(odd, inner, outer), jnp.where(odd, outer, inner)
 
 
-HALVE = (("gy", 1), ("gy", 4), ("gy", 2), ("gy", 8))
-GROUPS = (("gx", (1, 8, 9)), ("gx", (2, 5, 7)))
+HALVE = (("gy", 1), ("gy", 4), ("gy", 2))
+GROUPS = (("gy", (8,)), ("gx", (1, 8, 9)), ("gx", (2, 5, 7)))
 
 
 def swap(values, axis, bits):

time: 108 us -> 106 us (0.981)
  waiting for transfers between devices: 31.8 us -> 37.1 us
  starting transfers between devices: 42.1 us -> 37.2 us
  Pallas kernels: 19.1 us -> 17 us
    ppermute x14 -> x13, waiting for transfers between devices: 30.3 us -> 35.6 us  [swap(): lax.ppermute(values, axis, [(i, i ^ bits) for i in range(lax.axis_size(ax...]
    ppermute x14 -> x13, starting transfers between devices: 32.2 us -> 27.3 us  [swap(): lax.ppermute(values, axis, [(i, i ^ bits) for i in range(lax.axis_size(ax...]
    pallas_call x1, Pallas kernels: 12.3 us -> 11.1 us  [run_forward(): pl.pallas_call(forward_body, out_shape=(jax.ShapeDtypeStruct((nx, 2, nz,...]
  transfers between devices with their start and end apart: 18 -> 17, of which waited for: 13 -> 12; matrix products, arithmetic and copies ran while one was open for 5% -> 6% of each run, Pallas kernels for 6% -> 6%
where the time goes in v4:
time: 106 us; the launch traced here: 105 us
  starting transfers between devices  37.2 us (35%)
  waiting for transfers between devices  37.1 us (35%)
  Pallas kernels  17 us (16%)
  local copies, waits for them, and re-layouts  7.9 us (7%)
  other arithmetic  5 us (5%)
  between operations  1.19 us (1%)
    ppermute x13, waiting for transfers between devices, swap(): lax.ppermute(values, axis, [(i, i ^ bits) for i in range(lax.axis_size(ax...  35.6 us
    ppermute x13, starting transfers between devices, swap(): lax.ppermute(values, axis, [(i, i ^ bits) for i in range(lax.axis_size(ax...  27.3 us
    pallas_call x1, Pallas kernels, run_forward(): pl.pallas_call(forward_body, out_shape=(jax.ShapeDtypeStruct((nx, 2, nz,...  11.1 us
    pallas_call x1, Pallas kernels, run_backward(): pl.pallas_call(backward_body, out_shape=jax.ShapeDtypeStruct((nx, nz, ny,...  5.84 us
    ppermute x2, starting transfers between devices, from_both(): lax.ppermute(other, axis, [(i, i + 1 if i % 2 else i - 1) for i in range(...  5.25 us
    ppermute x2, starting transfers between devices, from_both(): lax.ppermute(jnp.where(odd, first, last), axis, [(i, i ^ 1) for i in rang...  4.7 us
    slice x2, local copies, waits for them, and re-layouts, per_device(): first = jnp.concatenate([low[:, :, 0], cot[:, :, 0]], axis=0)  2.39 us
  transfers between devices with their start and end apart: 17, of which 12 were waited for; matrix products, arithmetic and copies ran while one was open for 6% of the time, Pallas kernels for 6%

profile of v4, /device:TPU:1, one launch (start us, length us, event | category | flops | bytes accessed | tf_op | source)
XLA Modules:
  0.0 105.3 jit_solution(3236226859106451106)
XLA Ops:
  0.6 1.3 %fusion.35 = (bf16[32,6,1,128]{3,2,1,0:T(2,128)(2,1)S(1)}, bf16[32,6,1,128]{3,2,1,0:T(2,128)(2,1)S(1)}) fusion(bf16[32,6,32,128]{3,2,1,0:T(8,128)(2,1)} %bitcast.90), kind=kLoop, calls=%fused_computation.123 | loop fusion | bytes 196608 | tf_op jit(solution)/shard_map/slice | solution.py:342
  1.9 1.1 %fusion.36 = (bf16[16,6,1,128]{3,2,1,0:T(2,128)(2,1)S(1)}, bf16[16,6,1,128]{3,2,1,0:T(2,128)(2,1)S(1)}) fusion(bf16[16,6,16,128]{3,2,1,0:T(8,128)(2,1)} %bitcast.93), kind=kLoop, calls=%fused_computation.124 | loop fusion | bytes 98304 | tf_op jit(solution)/shard_map/slice | solution.py:342
  3.1 4.6 %collective-permute-start.1 = (bf16[48,6,128]{2,0,1:T(8,128)(2,1)S(1)}, bf16[48,6,128]{2,0,1:T(8,128)(2,1)S(1)}, u32[]{:S(2)}, u32[]{:S(2)}) collective-permute-start(bf16[48,6,128]{2,0,1:T(8,128)(2,1)S(1)} %get-tuple-element.48), channel_id=1, source_target_pairs={{1,2},{2,1},{3,4},{4,3},{5,6},{6,5},{7,8},{8,7},{9,10},{10,9},{11,... | collective-permute-start | bytes 221192 | tf_op jit(solution)/shard_map/ppermute | solution.py:277
  7.8 0.8 slice_bitcast_fusion.2
  8.7 0.8 slice_bitcast_fusion.6
  11.0 4.6 %collective-permute-start.2 = (bf16[6,52,128]{2,1,0:T(8,128)(2,1)S(1)}, bf16[6,52,128]{2,1,0:T(8,128)(2,1)S(1)}, u32[]{:S(2)}, u32[]{:S(2)}) collective-permute-start(bf16[6,52,128]{2,1,0:T(8,128)(2,1)S(1)} %get-tuple-element.45), channel_id=1, source_target_pairs={{0,16},{16,0},{32,48},{48,32},{64,80},{80,64},{96,112},{112,96},{1... | collective-permute-start | bytes 239624 | tf_op jit(solution)/shard_map/ppermute | solution.py:275
  16.9 1.1 %collective-permute-done.2 = bf16[6,52,128]{2,1,0:T(8,128)(2,1)S(1)} collective-permute-done((bf16[6,52,128]{2,1,0:T(8,128)(2,1)S(1)}, bf16[6,52,128]{2,1,0:T(8,128)(2,1)S(1)}, u32[]{:S(2)}, u32[]{:S(2)}) %collective-permute-start.2) | collective-permute-done | bytes 79904 | tf_op jit(solution)/shard_map/ppermute | solution.py:275
  18.0 0.7 broadcast_select_fusion.6
  18.7 11.1 %forward.1 = (bf16[16,2,6,32,128]{4,3,2,1,0:T(8,128)(2,1)}, bf16[2,17,2,6,16,128]{5,4,3,2,1,0:T(8,128)(2,1)}, f32[2048,128]{1,0:T(8,128)}, bf16[2064,128]{1,0:T(8,128)(2,1)}, f32[8,128]{1,0:T(8,128)}) custom-call(s32[1]{0:T(128)} %bitcast.upper, bf16[16,6,16,128]{3,2,1,0:T(8,128)(2,1)} %bitcast.95, bf16[48,6,128]{2,1,0:T(8,128)(2,1)} %copy.303.ylo, ...), custom_call_target="tpu_custom_call" | custom-call | flops 12884901888 | bytes 8388608 | tf_op jit(solution)/shard_map/forward/pallas_call | solution.py:152
  29.9 1.1 %collective-permute-start.4 = (bf16[2064,128]{1,0:T(8,128)(2,1)}, bf16[2064,128]{1,0:T(8,128)(2,1)S(1)}, u32[]{:S(2)}, u32[]{:S(2)}) collective-permute-start(bf16[2064,128]{1,0:T(8,128)(2,1)} %get-tuple-element.12), channel_id=1, source_target_pairs={{0,1},{1,0},{2,3},{3,2},{4,5},{5,4},{6,7},{7,6},{8,9},{9,8},{10,11... | collective-permute-start | bytes 1585160 | tf_op jit(solution)/shard_map/ppermute | solution.py:286
  31.0 1.7 %collective-permute-done.4 = bf16[2064,128]{1,0:T(8,128)(2,1)S(1)} collective-permute-done((bf16[2064,128]{1,0:T(8,128)(2,1)}, bf16[2064,128]{1,0:T(8,128)(2,1)S(1)}, u32[]{:S(2)}, u32[]{:S(2)}) %collective-permute-start.4) | collective-permute-done | bytes 528416 | tf_op jit(solution)/shard_map/ppermute | solution.py:286
  33.7 2.3 %collective-permute-start.5 = (bf16[1040,128]{1,0:T(8,128)(2,1)S(1)}, bf16[1040,128]{1,0:T(8,128)(2,1)S(1)}, u32[]{:S(2)}, u32[]{:S(2)}) collective-permute-start(bf16[1040,128]{1,0:T(8,128)(2,1)S(1)} %pad_maximum_fusion.1), channel_id=1, source_target_pairs={{0,4},{1,5},{2,6},{3,7},{4,0},{5,1},{6,2},{7,3},{8,12},{9,13},{10,... | collective-permute-start | bytes 798728 | tf_op jit(solution)/shard_map/ppermute | solution.py:286
  36.0 6.4 %collective-permute-done.5 = bf16[1040,128]{1,0:T(8,128)(2,1)S(1)} collective-permute-done((bf16[1040,128]{1,0:T(8,128)(2,1)S(1)}, bf16[1040,128]{1,0:T(8,128)(2,1)S(1)}, u32[]{:S(2)}, u32[]{:S(2)}) %collective-permute-start.5) | collective-permute-done | bytes 266272 | tf_op jit(solution)/shard_map/ppermute | solution.py:286
  42.7 1.1 %collective-permute-start.6 = (bf16[528,128]{1,0:T(8,128)(2,1)S(1)}, bf16[528,128]{1,0:T(8,128)(2,1)S(1)}, u32[]{:S(2)}, u32[]{:S(2)}) collective-permute-start(bf16[528,128]{1,0:T(8,128)(2,1)S(1)} %pad_maximum_fusion.3), channel_id=1, source_target_pairs={{0,2},{1,3},{2,0},{3,1},{4,6},{5,7},{6,4},{7,5},{8,10},{9,11},{10,... | collective-permute-start | bytes 405512 | tf_op jit(solution)/shard_map/ppermute | solution.py:286
  43.8 0.9 fusion.38
  44.6 2.3 %collective-permute-done.6 = bf16[528,128]{1,0:T(8,128)(2,1)S(1)} collective-permute-done((bf16[528,128]{1,0:T(8,128)(2,1)S(1)}, bf16[528,128]{1,0:T(8,128)(2,1)S(1)}, u32[]{:S(2)}, u32[]{:S(2)}) %collective-permute-start.6) | collective-permute-done | bytes 135200 | tf_op jit(solution)/shard_map/ppermute | solution.py:286
  47.1 2.5 %collective-permute-start.7 = (bf16[528,128]{1,0:T(8,128)(2,1)S(1)}, bf16[528,128]{1,0:T(8,128)(2,1)S(1)}, u32[]{:S(2)}, u32[]{:S(2)}) collective-permute-start(bf16[528,128]{1,0:T(8,128)(2,1)S(1)} %pad_maximum_fusion.4), channel_id=1, source_target_pairs={{0,8},{1,9},{2,10},{3,11},{4,12},{5,13},{6,14},{7,15},{8,0},{9,1},... | collective-permute-start | bytes 405512 | tf_op jit(solution)/shard_map/ppermute | solution.py:286
  49.6 0.9 fusion.37
  50.5 2.1 %collective-permute-done.7 = bf16[528,128]{1,0:T(8,128)(2,1)S(1)} collective-permute-done((bf16[528,128]{1,0:T(8,128)(2,1)S(1)}, bf16[528,128]{1,0:T(8,128)(2,1)S(1)}, u32[]{:S(2)}, u32[]{:S(2)}) %collective-permute-start.7) | collective-permute-done | bytes 135200 | tf_op jit(solution)/shard_map/ppermute | solution.py:286
  52.7 6.6 %collective-permute-start.10 = (bf16[528,128]{1,0:T(8,128)(2,1)S(1)}, bf16[528,128]{1,0:T(8,128)(2,1)S(1)}, u32[]{:S(2)}, u32[]{:S(2)}) collective-permute-start(bf16[528,128]{1,0:T(8,128)(2,1)S(1)} %pad_maximum_fusion.5), channel_id=1, source_target_pairs={{0,144},{16,128},{32,176},{48,160},{64,208},{80,192},{96,240},{112... | collective-permute-start | bytes 405512 | tf_op jit(solution)/shard_map/ppermute | solution.py:286
  59.8 1.1 %collective-permute-start.8 = (bf16[528,128]{1,0:T(8,128)(2,1)S(1)}, bf16[528,128]{1,0:T(8,128)(2,1)S(1)}, u32[]{:S(2)}, u32[]{:S(2)}) collective-permute-start(bf16[528,128]{1,0:T(8,128)(2,1)S(1)} %pad_maximum_fusion.5), channel_id=1, source_target_pairs={{0,16},{16,0},{32,48},{48,32},{64,80},{80,64},{96,112},{112,96},{1... | collective-permute-start | bytes 405512 | tf_op jit(solution)/shard_map/ppermute | solution.py:286
  60.9 0.8 collective-permute-done.10
  61.7 4.4 %collective-permute-done.9 = bf16[528,128]{1,0:T(8,128)(2,1)S(1)} collective-permute-done((bf16[528,128]{1,0:T(8,128)(2,1)S(1)}, bf16[528,128]{1,0:T(8,128)(2,1)S(1)}, u32[]{:S(2)}, u32[]{:S(2)}) %collective-permute-start.9) | collective-permute-done | bytes 135200 | tf_op jit(solution)/shard_map/ppermute | solution.py:286
  66.3 2.0 %collective-permute-start.13 = (bf16[528,128]{1,0:T(8,128)(2,1)S(1)}, bf16[528,128]{1,0:T(8,128)(2,1)S(1)}, u32[]{:S(2)}, u32[]{:S(2)}) collective-permute-start(bf16[528,128]{1,0:T(8,128)(2,1)S(1)} %pad_maximum_fusion.6), channel_id=1, source_target_pairs={{0,112},{16,96},{32,80},{48,64},{64,48},{80,32},{96,16},{112,0},{1... | collective-permute-start | bytes 405512 | tf_op jit(solution)/shard_map/ppermute | solution.py:286
  68.3 3.6 %collective-permute-start.12 = (bf16[528,128]{1,0:T(8,128)(2,1)S(1)}, bf16[528,128]{1,0:T(8,128)(2,1)S(1)}, u32[]{:S(2)}, u32[]{:S(2)}) collective-permute-start(bf16[528,128]{1,0:T(8,128)(2,1)S(1)} %pad_maximum_fusion.6), channel_id=1, source_target_pairs={{0,80},{16,64},{32,112},{48,96},{64,16},{80,0},{96,48},{112,32},{1... | collective-permute-start | bytes 405512 | tf_op jit(solution)/shard_map/ppermute | solution.py:286
  72.0 7.5 %collective-permute-done.12 = bf16[528,128]{1,0:T(8,128)(2,1)S(1)} collective-permute-done((bf16[528,128]{1,0:T(8,128)(2,1)S(1)}, bf16[528,128]{1,0:T(8,128)(2,1)S(1)}, u32[]{:S(2)}, u32[]{:S(2)}) %collective-permute-start.12) | collective-permute-done | bytes 135200 | tf_op jit(solution)/shard_map/ppermute | solution.py:286
  79.5 1.8 %collective-permute-done.11 = bf16[528,128]{1,0:T(8,128)(2,1)S(1)} collective-permute-done((bf16[528,128]{1,0:T(8,128)(2,1)S(1)}, bf16[528,128]{1,0:T(8,128)(2,1)S(1)}, u32[]{:S(2)}, u32[]{:S(2)}) %collective-permute-start.11) | collective-permute-done | bytes 135200 | tf_op jit(solution)/shard_map/ppermute | solution.py:286
  81.8 3.6 %collective-permute-done.14 = bf16[512,128]{1,0:T(8,128)(2,1)S(1)} collective-permute-done((bf16[512,128]{1,0:T(8,128)(2,1)S(1)}, bf16[512,128]{1,0:T(8,128)(2,1)S(1)}, u32[]{:S(2)}, u32[]{:S(2)}) %collective-permute-start.14) | collective-permute-done | bytes 131104 | tf_op jit(solution)/shard_map/ppermute | solution.py:286
  85.6 5.1 %collective-permute-done.15 = bf16[1024,128]{1,0:T(8,128)(2,1)S(1)} collective-permute-done((bf16[1024,128]{1,0:T(8,128)(2,1)S(1)}, bf16[1024,128]{1,0:T(8,128)(2,1)S(1)}, u32[]{:S(2)}, u32[]{:S(2)}) %collective-permute-start.15) | collective-permute-done | bytes 262176 | tf_op jit(solution)/shard_map/ppermute | solution.py:286
  90.9 6.3 %collective-permute-start.16 = (bf16[2048,128]{1,0:T(8,128)(2,1)S(1)}, bf16[2048,128]{1,0:T(8,128)(2,1)S(1)}, u32[]{:S(2)}, u32[]{:S(2)}) collective-permute-start(bf16[2048,128]{1,0:T(8,128)(2,1)S(1)} %pad_maximum_fusion), channel_id=1, source_target_pairs={{0,1},{1,0},{2,3},{3,2},{4,5},{5,4},{6,7},{7,6},{8,9},{9,8},{10,11... | collective-permute-start | bytes 1572872 | tf_op jit(solution)/shard_map/ppermute | solution.py:286
  97.2 5.8 %backward.1 = bf16[16,6,16,128]{3,2,1,0:T(8,128)(2,1)} custom-call(bf16[2,17,2,6,16,128]{5,4,3,2,1,0:T(8,128)(2,1)S(1)} %copy-done.2, f32[4,8,32,128]{3,2,1,0:T(8,128)S(1)} %fusion.8.cols, f32[2,2,6,24,128]{4,3,2,1,0:T(8,128)S(1)} %pad_convert_fusion.ccols, bf16[4,4,4,64,128]{4,3,2,1,0:T(8,128)(2,1)S(1)} %copy-done, f32[1,64]{1,0:T(1,128)S(1)} %bitcast.88), custom_call_target="tpu_custom_call" | custom-call | flops 4294967296 | bytes 4194304 | tf_op jit(solution)/shard_map/backward/pallas_call | solution.py:254
  103.9 1.5 %convert_multiply_fusion = f32[4096,128]{1,0:T(8,128)} fusion(bf16[2048,128]{1,0:T(8,128)(2,1)S(1)} %get-tuple-element.33, bf16[2048,128]{1,0:T(8,128)(2,1)S(1)} %get-tuple-element.32), kind=kLoop, calls=%fused_computation | loop fusion | flops 2621440 | bytes 3145728 | tf_op jit(solution)/shard_map/div | solution.py:370
  (100 shorter events, 6.8 us)
Async XLA Ops:
  3.1 6.6 %collective-permute-start.1 = (bf16[48,6,128]{2,0,1:T(8,128)(2,1)S(1)}, bf16[48,6,128]{2,0,1:T(8,128)(2,1)S(1)}, u32[]{:S(2)}, u32[]{:S(2)}) collective-permute-start(bf16[48,6,128]{2,0,1:T(8,128)(2,1)S(1)} %get-tuple-element.48), channel_id=1, source_target_pairs={{1,2},{2,1},{3,4},{4,3},{5,6},{6,5},{7,8},{8,7},{9,10},{10,9},{11,... | collective-permute-start | bytes 221192 | tf_op jit(solution)/shard_map/ppermute | solution.py:277
  7.7 2.0 %collective-permute-start = (bf16[48,6,128]{2,0,1:T(8,128)(2,1)S(1)}, bf16[48,6,128]{2,0,1:T(8,128)(2,1)S(1)}, u32[]{:S(2)}, u32[]{:S(2)}) collective-permute-start(bf16[48,6,128]{2,0,1:T(8,128)(2,1)S(1)} %get-tuple-element.49), channel_id=1, source_target_pairs={{0,1},{1,0},{2,3},{3,2},{4,5},{5,4},{6,7},{7,6},{8,9},{9,8},{10,11... | collective-permute-start | bytes 221192 | tf_op jit(solution)/shard_map/ppermute | solution.py:275
  10.3 6.6 %collective-permute-start.3 = (bf16[6,52,128]{2,1,0:T(8,128)(2,1)S(1)}, bf16[6,52,128]{2,1,0:T(8,128)(2,1)S(1)}, u32[]{:S(2)}, u32[]{:S(2)}) collective-permute-start(bf16[6,52,128]{2,1,0:T(8,128)(2,1)S(1)} %get-tuple-element.44), channel_id=1, source_target_pairs={{16,32},{32,16},{48,64},{64,48},{80,96},{96,80},{112,128},{128,112... | collective-permute-start | bytes 239624 | tf_op jit(solution)/shard_map/ppermute | solution.py:277
  11.0 7.1 %collective-permute-start.2 = (bf16[6,52,128]{2,1,0:T(8,128)(2,1)S(1)}, bf16[6,52,128]{2,1,0:T(8,128)(2,1)S(1)}, u32[]{:S(2)}, u32[]{:S(2)}) collective-permute-start(bf16[6,52,128]{2,1,0:T(8,128)(2,1)S(1)} %get-tuple-element.45), channel_id=1, source_target_pairs={{0,16},{16,0},{32,48},{48,32},{64,80},{80,64},{96,112},{112,96},{1... | collective-permute-start | bytes 239624 | tf_op jit(solution)/shard_map/ppermute | solution.py:275
  29.8 3.6 %copy-start.3 = (f32[2048,128]{1,0:T(8,128)S(1)}, f32[2048,128]{1,0:T(8,128)}, u32[]{:S(2)}) copy-start(f32[2048,128]{1,0:T(8,128)} %get-tuple-element.11) | copy-start | bytes 3145732
  29.9 2.9 %collective-permute-start.4 = (bf16[2064,128]{1,0:T(8,128)(2,1)}, bf16[2064,128]{1,0:T(8,128)(2,1)S(1)}, u32[]{:S(2)}, u32[]{:S(2)}) collective-permute-start(bf16[2064,128]{1,0:T(8,128)(2,1)} %get-tuple-element.12), channel_id=1, source_target_pairs={{0,1},{1,0},{2,3},{3,2},{4,5},{5,4},{6,7},{7,6},{8,9},{9,8},{10,11... | collective-permute-start | bytes 1585160 | tf_op jit(solution)/shard_map/ppermute | solution.py:286
  33.7 8.7 %collective-permute-start.5 = (bf16[1040,128]{1,0:T(8,128)(2,1)S(1)}, bf16[1040,128]{1,0:T(8,128)(2,1)S(1)}, u32[]{:S(2)}, u32[]{:S(2)}) collective-permute-start(bf16[1040,128]{1,0:T(8,128)(2,1)S(1)} %pad_maximum_fusion.1), channel_id=1, source_target_pairs={{0,4},{1,5},{2,6},{3,7},{4,0},{5,1},{6,2},{7,3},{8,12},{9,13},{10,... | collective-permute-start | bytes 798728 | tf_op jit(solution)/shard_map/ppermute | solution.py:286
  42.7 4.3 %collective-permute-start.6 = (bf16[528,128]{1,0:T(8,128)(2,1)S(1)}, bf16[528,128]{1,0:T(8,128)(2,1)S(1)}, u32[]{:S(2)}, u32[]{:S(2)}) collective-permute-start(bf16[528,128]{1,0:T(8,128)(2,1)S(1)} %pad_maximum_fusion.3), channel_id=1, source_target_pairs={{0,2},{1,3},{2,0},{3,1},{4,6},{5,7},{6,4},{7,5},{8,10},{9,11},{10,... | collective-permute-start | bytes 405512 | tf_op jit(solution)/shard_map/ppermute | solution.py:286
  47.1 5.5 %collective-permute-start.7 = (bf16[528,128]{1,0:T(8,128)(2,1)S(1)}, bf16[528,128]{1,0:T(8,128)(2,1)S(1)}, u32[]{:S(2)}, u32[]{:S(2)}) collective-permute-start(bf16[528,128]{1,0:T(8,128)(2,1)S(1)} %pad_maximum_fusion.4), channel_id=1, source_target_pairs={{0,8},{1,9},{2,10},{3,11},{4,12},{5,13},{6,14},{7,15},{8,0},{9,1},... | collective-permute-start | bytes 405512 | tf_op jit(solution)/shard_map/ppermute | solution.py:286
  52.7 9.0 %collective-permute-start.10 = (bf16[528,128]{1,0:T(8,128)(2,1)S(1)}, bf16[528,128]{1,0:T(8,128)(2,1)S(1)}, u32[]{:S(2)}, u32[]{:S(2)}) collective-permute-start(bf16[528,128]{1,0:T(8,128)(2,1)S(1)} %pad_maximum_fusion.5), channel_id=1, source_target_pairs={{0,144},{16,128},{32,176},{48,160},{64,208},{80,192},{96,240},{112... | collective-permute-start | bytes 405512 | tf_op jit(solution)/shard_map/ppermute | solution.py:286
  59.3 6.8 %collective-permute-start.9 = (bf16[528,128]{1,0:T(8,128)(2,1)S(1)}, bf16[528,128]{1,0:T(8,128)(2,1)S(1)}, u32[]{:S(2)}, u32[]{:S(2)}) collective-permute-start(bf16[528,128]{1,0:T(8,128)(2,1)S(1)} %pad_maximum_fusion.5), channel_id=1, source_target_pairs={{0,128},{16,144},{32,160},{48,176},{64,192},{80,208},{96,224},{112... | collective-permute-start | bytes 405512 | tf_op jit(solution)/shard_map/ppermute | solution.py:286
  59.8 6.3 %collective-permute-start.8 = (bf16[528,128]{1,0:T(8,128)(2,1)S(1)}, bf16[528,128]{1,0:T(8,128)(2,1)S(1)}, u32[]{:S(2)}, u32[]{:S(2)}) collective-permute-start(bf16[528,128]{1,0:T(8,128)(2,1)S(1)} %pad_maximum_fusion.5), channel_id=1, source_target_pairs={{0,16},{16,0},{32,48},{48,32},{64,80},{80,64},{96,112},{112,96},{1... | collective-permute-start | bytes 405512 | tf_op jit(solution)/shard_map/ppermute | solution.py:286
  66.3 5.6 %collective-permute-start.13 = (bf16[528,128]{1,0:T(8,128)(2,1)S(1)}, bf16[528,128]{1,0:T(8,128)(2,1)S(1)}, u32[]{:S(2)}, u32[]{:S(2)}) collective-permute-start(bf16[528,128]{1,0:T(8,128)(2,1)S(1)} %pad_maximum_fusion.6), channel_id=1, source_target_pairs={{0,112},{16,96},{32,80},{48,64},{64,48},{80,32},{96,16},{112,0},{1... | collective-permute-start | bytes 405512 | tf_op jit(solution)/shard_map/ppermute | solution.py:286
  68.3 11.2 %collective-permute-start.12 = (bf16[528,128]{1,0:T(8,128)(2,1)S(1)}, bf16[528,128]{1,0:T(8,128)(2,1)S(1)}, u32[]{:S(2)}, u32[]{:S(2)}) collective-permute-start(bf16[528,128]{1,0:T(8,128)(2,1)S(1)} %pad_maximum_fusion.6), channel_id=1, source_target_pairs={{0,80},{16,64},{32,112},{48,96},{64,16},{80,0},{96,48},{112,32},{1... | collective-permute-start | bytes 405512 | tf_op jit(solution)/shard_map/ppermute | solution.py:286
  71.9 9.4 %collective-permute-start.11 = (bf16[528,128]{1,0:T(8,128)(2,1)S(1)}, bf16[528,128]{1,0:T(8,128)(2,1)S(1)}, u32[]{:S(2)}, u32[]{:S(2)}) collective-permute-start(bf16[528,128]{1,0:T(8,128)(2,1)S(1)} %pad_maximum_fusion.6), channel_id=1, source_target_pairs={{0,32},{16,48},{32,0},{48,16},{64,96},{80,112},{96,64},{112,80},{1... | collective-permute-start | bytes 405512 | tf_op jit(solution)/shard_map/ppermute | solution.py:286
  81.4 3.9 %collective-permute-start.14 = (bf16[512,128]{1,0:T(8,128)(2,1)S(1)}, bf16[512,128]{1,0:T(8,128)(2,1)S(1)}, u32[]{:S(2)}, u32[]{:S(2)}) collective-permute-start(bf16[512,128]{1,0:T(8,128)(2,1)S(1)} %fusion.3), channel_id=1, source_target_pairs={{0,2},{1,3},{2,0},{3,1},{4,6},{5,7},{6,4},{7,5},{8,10},{9,11},{10,... | collective-permute-start | bytes 393224 | tf_op jit(solution)/shard_map/ppermute | solution.py:286
  85.4 11.8 %copy-start = (bf16[4,4,4,64,128]{4,3,2,1,0:T(8,128)(2,1)S(1)}, bf16[4,4,4,64,128]{4,3,2,1,0:T(8,128)(2,1)}, u32[]{:S(2)}) copy-start(bf16[4,4,4,64,128]{4,3,2,1,0:T(8,128)(2,1)} %kern.1) | copy-start | bytes 3145732
  85.4 11.8 %copy-start.1 = (f32[64]{0:T(128)S(1)}, f32[64]{0:T(128)}, u32[]{:S(2)}) copy-start(f32[64]{0:T(128)} %param.6) | copy-start | bytes 772
  85.4 11.8 %copy-start.2 = (bf16[2,17,2,6,16,128]{5,4,3,2,1,0:T(8,128)(2,1)S(1)}, bf16[2,17,2,6,16,128]{5,4,3,2,1,0:T(8,128)(2,1)}, u32[]{:S(2)}) copy-start(bf16[2,17,2,6,16,128]{5,4,3,2,1,0:T(8,128)(2,1)} %get-tuple-element.10.dpre) | copy-start | bytes 5013508
  85.4 5.3 %collective-permute-start.15 = (bf16[1024,128]{1,0:T(8,128)(2,1)S(1)}, bf16[1024,128]{1,0:T(8,128)(2,1)S(1)}, u32[]{:S(2)}, u32[]{:S(2)}) collective-permute-start(bf16[1024,128]{1,0:T(8,128)(2,1)S(1)} %pad_maximum_fusion.2), channel_id=1, source_target_pairs={{0,4},{1,5},{2,6},{3,7},{4,0},{5,1},{6,2},{7,3},{8,12},{9,13},{10,... | collective-permute-start | bytes 786440 | tf_op jit(solution)/shard_map/ppermute | solution.py:286
  90.9 12.8 %collective-permute-start.16 = (bf16[2048,128]{1,0:T(8,128)(2,1)S(1)}, bf16[2048,128]{1,0:T(8,128)(2,1)S(1)}, u32[]{:S(2)}, u32[]{:S(2)}) collective-permute-start(bf16[2048,128]{1,0:T(8,128)(2,1)S(1)} %pad_maximum_fusion), channel_id=1, source_target_pairs={{0,1},{1,0},{2,3},{3,2},{4,5},{5,4},{6,7},{7,6},{8,9},{9,8},{10,11... | collective-permute-start | bytes 1572872 | tf_op jit(solution)/shard_map/ppermute | solution.py:286
